TPU v7x, 256 devices: a whole 4x4x8 slice. The times are simulated.
256 devices in a mesh: seq: 64 (over y, z, core), tensor: 4 (over x).
Axes of the slice: x: 4, y: 4, z: 8, core: 2. Of those that a mesh axis runs over, the one named last changes fastest.
Arguments:
- tokens: bfloat16 [32768, 3840], P('seq', 'tensor'), may hold values from -6 to 6
- w_query: bfloat16 [3840, 2048], P(None, 'tensor'), may hold values from -0.09375 to 0.09375
- w_key: bfloat16 [3840, 1024], P(None, 'tensor'), may hold values from -0.09375 to 0.09375
- w_value: bfloat16 [3840, 1024], P(None, 'tensor'), may hold values from -0.09375 to 0.09375
- query_gain: float32 [256], replicated, may hold values from 0.1 to 1.9
- key_gain: float32 [256], replicated, may hold values from 0.1 to 1.9
- adapter_down: bfloat16 [64, 64, 3840], P('seq', None, 'tensor'), may hold values from -0.09375 to 0.09375
- adapter_up: bfloat16 [64, 64, 2048], P('seq', None, 'tensor'), may hold values from -0.75 to 0.75
- adapter_ids: int32 [32768, 1], P('seq'), may hold values from 0 to 63; in each aligned block of 512 rows (0 to 511, 512 to 1023, ...) at most 16 rows name the same one
- doc_ids: int32 [32768], P('seq'), may hold values from 0 to 63, never falling along the last dimension, each value on 1 to 4096 neighbouring positions
- cotangent: bfloat16 [32768, 2048], P('seq', 'tensor'), may hold values from -6 to 6
Outputs:
- attended: bfloat16 [32768, 2048], P('seq', 'tensor')
- grad_up: float32 [64, 64, 2048], P('seq', None, 'tensor')
Inputs may be any that keep to these rules, and one draw needn't show every extreme that they name: `adapter_ids`: within the 512 tokens of one device no adapter is named by more than 16 tokens; in every draw some adapter is named by exactly 16 tokens of some device. `doc_ids`: document numbers never fall along the slab; each document has 1 to 4096 tokens and one has exactly 4096.
All inputs are finite; a program needn't handle non-finite values.
Results may differ from a plain program's by a relative error of at most 0.0088.
Values may be sent and summed in bfloat16 or wider, within the bound.
A program may use at most 128 MiB of HBM per device.

v0:
```python
import math

import jax
import jax.numpy as jnp
from jax import lax
from jax.sharding import PartitionSpec as P

HD = 256
R = 64
WINDOW = 1024
ADAPTERS = 64
CAP = 16


def passed_along(value, axis, steps):
    count = lax.axis_size(axis)
    first, last = (max(0, -steps), min(count, count - steps))
    return lax.ppermute(value, axis, [(source, source + steps) for source in range(first, last)])


def normalize(pre_field, gain_vec):
    mean_sq = jnp.mean(pre_field * pre_field, axis=-1, keepdims=True)
    return pre_field * lax.rsqrt(mean_sq + 1e-06) * gain_vec


def rotate(pre_field, positions):
    half_dim = pre_field.shape[-1] // 2
    frequency = jnp.exp(
        jnp.arange(half_dim, dtype=jnp.float32) * (-2.0 * math.log(10000.0) / pre_field.shape[-1])
    )
    angles = positions.astype(jnp.float32)[:, None] * frequency[None, :]
    cosine = jnp.cos(angles)[:, None, :]
    sine_part = jnp.sin(angles)[:, None, :]
    lower_half = pre_field[..., :half_dim]
    second = pre_field[..., half_dim:]
    return jnp.concatenate(
        [lower_half * cosine - second * sine_part, second * cosine + lower_half * sine_part],
        axis=-1,
    )


def shape_query(pre_field, gain_vec, positions):
    return rotate(normalize(pre_field, gain_vec), positions)


def attend(queries, key_rows, values, upstream, allowed):
    score_scale = 1.0 / math.sqrt(queries.shape[-1])
    scores = (
        jnp.einsum("tngd,knd->ngtk", queries, key_rows, preferred_element_type=jnp.float32)
        * score_scale
    )
    weights = jnp.where(allowed[None, None], jnp.exp(scores), 0.0)
    probs = weights / jnp.sum(weights, axis=-1, keepdims=True)
    probs_low = probs.astype(jnp.bfloat16)
    attended = jnp.einsum("ngtk,knd->tngd", probs_low, values, preferred_element_type=jnp.float32)
    dprobs = jnp.einsum("tngd,knd->ngtk", upstream, values, preferred_element_type=jnp.float32)
    delta = jnp.sum(probs * dprobs, axis=-1, keepdims=True)
    dscores = (probs * (dprobs - delta) * score_scale).astype(jnp.bfloat16)
    dqueries = jnp.einsum("ngtk,knd->tngd", dscores, key_rows, preferred_element_type=jnp.float32)
    return (attended.astype(jnp.bfloat16), dqueries)


def local(
    tokens,
    w_query,
    w_key,
    w_value,
    query_gain,
    key_gain,
    adapter_down,
    adapter_up,
    adapter_ids,
    doc_ids,
    cotangent,
):
    tok_count = tokens.shape[0]
    feat_width = tokens.shape[1]
    q_width = w_query.shape[1]
    kv_width = w_key.shape[1]
    local_heads = q_width // HD
    kv_heads = kv_width // HD
    head_group = local_heads // kv_heads
    positions = lax.axis_index("seq") * tok_count + jnp.arange(tok_count, dtype=jnp.int32)
    shard_cols = lax.all_gather(tokens, "tensor", axis=1, tiled=True)
    query_lin = jnp.dot(shard_cols, w_query, preferred_element_type=jnp.float32)
    key_lin = jnp.dot(shard_cols, w_key, preferred_element_type=jnp.float32)
    value_lin = jnp.dot(shard_cols, w_value, preferred_element_type=jnp.float32)
    token_adapter = adapter_ids[:, 0]
    chosen = token_adapter[:, None] == jnp.arange(ADAPTERS, dtype=jnp.int32)[None, :]
    before = jnp.cumsum(chosen.astype(jnp.int32), axis=0) - 1
    slot_rank = jnp.sum(jnp.where(chosen, before, 0), axis=1)
    slot_index = token_adapter * CAP + slot_rank
    dispatch = (slot_index[None, :] == jnp.arange(ADAPTERS * CAP, dtype=jnp.int32)[:, None]).astype(
        jnp.bfloat16
    )
    outgoing = jnp.dot(dispatch, tokens, preferred_element_type=jnp.float32).astype(jnp.bfloat16)
    all_down, all_up = (
        lax.all_gather(adapter_down, "seq", axis=0, tiled=True),
        lax.all_gather(adapter_up, "seq", axis=0, tiled=True),
    )
    slot_rows = outgoing.reshape(ADAPTERS, CAP, feat_width)
    partial_low = jnp.einsum(
        "acd,ard->acr", slot_rows, all_down, preferred_element_type=jnp.float32
    )
    slot_low = lax.psum(partial_low, "tensor").astype(jnp.bfloat16)
    slot_lift = jnp.einsum(
        "acr,are->ace", slot_low, all_up, preferred_element_type=jnp.float32
    ).astype(jnp.bfloat16)
    lifted = jnp.einsum(
        "st,se->te",
        dispatch,
        slot_lift.reshape(ADAPTERS * CAP, q_width),
        preferred_element_type=jnp.float32,
    ).astype(jnp.bfloat16)
    lowrank = jnp.einsum(
        "st,sr->tr",
        dispatch,
        slot_low.reshape(ADAPTERS * CAP, R),
        preferred_element_type=jnp.float32,
    ).astype(jnp.bfloat16)
    query_pre = (query_lin + lifted.astype(jnp.float32)).reshape(tok_count, local_heads, HD)
    queries, query_back = jax.vjp(
        lambda pre_query: shape_query(pre_query, query_gain, positions), query_pre
    )
    queries = queries.astype(jnp.bfloat16).reshape(tok_count, kv_heads, head_group, HD)
    key_rows = shape_query(key_lin.reshape(tok_count, kv_heads, HD), key_gain, positions).astype(
        jnp.bfloat16
    )
    values = value_lin.astype(jnp.bfloat16).reshape(tok_count, kv_heads, HD)
    rim_count = WINDOW // tok_count
    key_list = []
    value_list = []
    doc_list = []
    place_list = []
    for distance in range(rim_count, 0, -1):
        far_keys, far_values, far_docs = passed_along((key_rows, values, doc_ids), "seq", distance)
        key_list.append(far_keys)
        value_list.append(far_values)
        doc_list.append(far_docs)
        place_list.append(positions - distance * tok_count)
    key_list.append(key_rows)
    value_list.append(values)
    doc_list.append(doc_ids)
    place_list.append(positions)
    window_keys = jnp.concatenate(key_list, axis=0)
    window_values = jnp.concatenate(value_list, axis=0)
    key_docs = jnp.concatenate(doc_list, axis=0)
    key_pos = jnp.concatenate(place_list, axis=0)
    key_gap = positions[:, None] - key_pos[None, :]
    allowed = (
        (doc_ids[:, None] == key_docs[None, :])
        & (key_gap >= 0)
        & (key_gap < WINDOW)
        & (key_pos[None, :] >= 0)
    )
    upstream = cotangent.reshape(tok_count, kv_heads, head_group, HD)
    block_out, dqueries = attend(queries, window_keys, window_values, upstream, allowed)
    attended = block_out.reshape(tok_count, q_width)
    (dquery_pre,) = query_back(dqueries.reshape(tok_count, local_heads, HD))
    dquery_pre = dquery_pre.reshape(tok_count, q_width).astype(jnp.bfloat16)
    out_low = jnp.dot(dispatch, lowrank, preferred_element_type=jnp.float32).astype(jnp.bfloat16)
    out_grad = jnp.dot(dispatch, dquery_pre, preferred_element_type=jnp.float32).astype(
        jnp.bfloat16
    )
    slot_low_rows = out_low.reshape(ADAPTERS, CAP, R)
    slot_grad_rows = out_grad.reshape(ADAPTERS, CAP, q_width)
    grad_up = lax.psum_scatter(
        jnp.einsum(
            "acr,ace->are", slot_low_rows, slot_grad_rows, preferred_element_type=jnp.float32
        ),
        "seq",
        scatter_dimension=0,
        tiled=True,
    )
    return (attended, grad_up)


def solution(mesh):
    in_specs = (
        P("seq", "tensor"),
        P(None, "tensor"),
        P(None, "tensor"),
        P(None, "tensor"),
        P(),
        P(),
        P("seq", None, "tensor"),
        P("seq", None, "tensor"),
        P("seq", None),
        P("seq"),
        P("seq", "tensor"),
    )
    out_specs = (P("seq", "tensor"), P("seq", None, "tensor"))
    return jax.shard_map(local, mesh=mesh, in_specs=in_specs, out_specs=out_specs, check_vma=False)
```

profile of v0, /device:TPU:1, one launch (start us, length us, event | category | flops | bytes accessed | tf_op | source)
XLA Modules:
  0.0 405.0 jit_solution(11032409171625994337)
XLA Ops:
  9.4 4.9 %collective-permute-start.3 = (s32[512]{0:T(512)}, s32[512]{0:T(512)S(1)}, u32[]{:S(2)}, u32[]{:S(2)}) collective-permute-start(s32[512]{0:T(512)} %param.20), channel_id=1, source_target_pairs={{0,4},{4,8},{8,12},{12,16},{16,20},{20,24},{24,28},{28,32},{32,36}... | collective-permute-start | bytes 6152 | tf_op jit(solution)/shard_map/ppermute | solution.py:18
  14.4 3.5 collective-permute-start.2
  22.6 3.7 fusion.24
  26.4 4.0 copy.40
  30.4 2.5 fusion.16
  32.9 29.1 %all-gather.4.cloned.1.call-done = bf16[512,3840]{0,1:T(8,128)(2,1)} async-done(((bf16[512,960]{0,1:T(8,128)(2,1)}), bf16[512,3840]{0,1:T(8,128)(2,1)}) %all-gather.4.cloned.1.call-update) | async-done | bytes 3932176 | tf_op jit(solution)/shard_map/all_gather | solution.py:84
  62.0 3.5 multiply_reduce_fusion.2
  67.5 3.9 collective-permute-start.5
  71.5 3.9 collective-permute-start.4
  75.4 1.9 fusion.34
  77.3 1.9 collective-permute-start.1
  79.2 3.5 collective-permute-start
  82.7 66.4 %all-gather.6.cloned.1.call-done = bf16[64,64,960]{2,1,0:T(8,128)(2,1)} async-done(((bf16[1,64,960]{2,1,0:T(8,128)(2,1)}), bf16[64,64,960]{2,1,0:T(8,128)(2,1)}) %all-gather.6.cloned.1.call-update) | async-done | bytes 7864336 | tf_op jit(solution)/shard_map/all_gather | solution.py:98
  149.1 6.3 %fusion.73 = f32[64,16,64]{2,1,0:T(8,128)S(1)} fusion(bf16[64,16,960]{2,1,0:T(8,128)(2,1)} %bitcast.128, bf16[64,64,960]{2,1,0:T(8,128)(2,1)} %all-gather.6.cloned.1.call-done), kind=kOutput, calls=%fused_computation.106 | convolution fusion | flops 125829120 | bytes 10092544 | tf_op jit(solution)/shard_map/acd,ard->acr/dot_general | solution.py:102
  155.4 19.6 %all-reduce.3 = bf16[64,16,64]{2,1,0:T(8,128)(2,1)S(1)} all-reduce(f32[64,16,64]{2,1,0:T(8,128)S(1)} %fusion.73), channel_id=1, replica_groups=mesh['seq'=64,'tensor'=4] {'tensor'}, use_global_device_ids=true, to_apply=%region_4.5 | all-reduce | flops 65536 | bytes 393216 | tf_op jit(solution)/shard_map/psum | solution.py:105
  175.0 52.9 %all-gather.8.cloned.1.call-done = bf16[64,64,512]{2,1,0:T(8,128)(2,1)} async-done(((bf16[1,64,512]{2,1,0:T(8,128)(2,1)}), bf16[64,64,512]{2,1,0:T(8,128)(2,1)}) %all-gather.8.cloned.1.call-update) | async-done | bytes 4194320 | tf_op jit(solution)/shard_map/all_gather | solution.py:99
  227.9 3.0 convolution_convert_fusion
  232.5 2.3 multiply_reduce_fusion.1
  236.6 3.1 fusion.5
  239.7 4.4 %fusion = (f32[2,512]{1,0:T(2,128)S(1)}, f32[1536,512,2]{1,0,2:T(8,128)S(1)}) fusion(f32[2,512]{1,0:T(2,128)S(1)} %get-tuple-element.20, f32[1536,512,2]{1,0,2:T(8,128)S(1)} %get-tuple-element.21, pred[512,1536]{0,1:T(8,128)(4,1)S(1)} %copy-done.2, bf16[64,2,8,256]{3,2,1,0:T(8,128)(2,1)S(1)} %bitcast.139, bf16[512,1,256]{2,0,1:T(8,128)(2,1)} %fusion.34, ...), kind=kOutput, calls=%fused_computation.3 | convolution fusion | flops 815528960 | bytes 14688256 | tf_op jit(solution)/shard_map/tngd,knd->ngtk/dot_general | solution.py:56
  244.1 3.8 fusion.26
  249.7 4.5 %fusion.74 = f32[64,64,512]{2,1,0:T(8,128)} fusion(bf16[64,16,64]{2,1,0:T(8,128)(2,1)S(1)} %bitcast.130, bf16[64,16,512]{2,1,0:T(8,128)(2,1)S(1)} %bitcast.129), kind=kOutput, calls=%fused_computation.107 | convolution fusion | flops 67108864 | bytes 9568256 | tf_op jit(solution)/shard_map/acr,ace->are/dot_general | solution.py:168
  254.2 5.2 %fusion.31 = bf16[256,2,512]{2,0,1:T(8,128)(2,1)S(1)} fusion(f32[2,512]{1,0:T(2,128)S(1)} %get-tuple-element.20, f32[1536,512,2]{1,0,2:T(8,128)} %copy-done.11, pred[512,1536]{0,1:T(8,128)(4,1)S(1)} %copy-done.2, bf16[512,1,256]{2,0,1:T(8,128)(2,1)} %fusion.34, bf16[512,1,256]{2,0,1:T(8,128)(2,1)} %collective-permute-done.1, ...), kind=kOutput, calls=%fused_computation.35 | convolution fusion | flops 814219264 | bytes 8392704 | tf_op jit(solution)/shard_map/ngtk,knd->tngd/dot_general | solution.py:55
  260.4 138.1 %reduce-scatter.2.cloned.1.call-done = f32[1,64,512]{2,1,0:T(8,128)} async-done(((f32[64,64,512]{2,1,0:T(8,128)}), f32[1,64,512]{2,1,0:T(8,128)}) %reduce-scatter.2.cloned.1.call-update) | async-done | bytes 131088 | tf_op jit(solution)/shard_map/reduce_scatter | solution.py:167
  (71 shorter events, 15.0 us)
Async XLA Ops:
  7.2 54.8 %copy-start = (bf16[3840,256]{1,0:T(8,128)(2,1)S(1)}, bf16[3840,256]{1,0:T(8,128)(2,1)}, u32[]{:S(2)}) copy-start(bf16[3840,256]{1,0:T(8,128)(2,1)} %param.13) | copy-start | bytes 5898244
  7.2 54.8 %all-gather.4.cloned.1.call-start = ((), (), s32[]{:S(2)}) async-start(), calls=%async_computation.1 | async-start | bytes 4915200 | tf_op jit(solution)/shard_map/all_gather | solution.py:84
  7.9 141.2 %all-gather.6.cloned.1.call-start = ((), (), s32[]{:S(2)}) async-start(), calls=%async_computation.2 | async-start | bytes 8519680 | tf_op jit(solution)/shard_map/all_gather | solution.py:98
  8.7 219.2 %all-gather.8.cloned.1.call-start = ((), (), s32[]{:S(2)}) async-start(), calls=%async_computation.3 | async-start | bytes 4259840 | tf_op jit(solution)/shard_map/all_gather | solution.py:99
  9.4 389.1 %reduce-scatter.2.cloned.1.call-start = ((), (), s32[]{:S(2)}) async-start(), calls=%async_computation.4 | async-start | bytes 8519680 | tf_op jit(solution)/shard_map/reduce_scatter | solution.py:167
  9.4 20.9 %collective-permute-start.3 = (s32[512]{0:T(512)}, s32[512]{0:T(512)S(1)}, u32[]{:S(2)}, u32[]{:S(2)}) collective-permute-start(s32[512]{0:T(512)} %param.20), channel_id=1, source_target_pairs={{0,4},{4,8},{8,12},{12,16},{16,20},{20,24},{24,28},{28,32},{32,36}... | collective-permute-start | bytes 6152 | tf_op jit(solution)/shard_map/ppermute | solution.py:18
  14.4 16.0 %collective-permute-start.2 = (s32[512]{0:T(512)}, s32[512]{0:T(512)S(1)}, u32[]{:S(2)}, u32[]{:S(2)}) collective-permute-start(s32[512]{0:T(512)} %param.20), channel_id=1, source_target_pairs={{0,8},{4,12},{8,16},{12,20},{16,24},{20,28},{24,32},{28,36},{32,40... | collective-permute-start | bytes 6152 | tf_op jit(solution)/shard_map/ppermute | solution.py:18
  26.4 4.0 copy-start.4
  32.9 32.6 %copy-start.5 = (f32[256]{0:T(256)S(1)}, f32[256]{0:T(256)}, u32[]{:S(2)}) copy-start(f32[256]{0:T(256)} %param.16) | copy-start | bytes 3076
  62.0 13.3 %copy-start.7 = (bf16[512,3840]{0,1:T(8,128)(2,1)S(1)}, bf16[512,3840]{0,1:T(8,128)(2,1)}, u32[]{:S(2)}) copy-start(bf16[512,3840]{0,1:T(8,128)(2,1)} %all-gather.4.cloned.1.call-done) | copy-start | bytes 11796484
  62.0 13.3 %copy-start.9 = (bf16[3840,256]{1,0:T(8,128)(2,1)S(1)}, bf16[3840,256]{1,0:T(8,128)(2,1)}, u32[]{:S(2)}) copy-start(bf16[3840,256]{1,0:T(8,128)(2,1)} %param.14) | copy-start | bytes 5898244
  67.5 169.0 %collective-permute-start.5 = (bf16[512,1,256]{0,2,1:T(8,128)(2,1)}, bf16[512,1,256]{0,2,1:T(8,128)(2,1)}, u32[]{:S(2)}, u32[]{:S(2)}) collective-permute-start(bf16[512,1,256]{0,2,1:T(8,128)(2,1)} %pad_maximum_fusion), channel_id=1, source_target_pairs={{0,4},{4,8},{8,12},{12,16},{16,20},{20,24},{24,28},{28,32},{32,36}... | collective-permute-start | bytes 786440 | tf_op jit(solution)/shard_map/ppermute | solution.py:18
  71.5 165.1 %collective-permute-start.4 = (bf16[512,1,256]{0,2,1:T(8,128)(2,1)}, bf16[512,1,256]{0,2,1:T(8,128)(2,1)}, u32[]{:S(2)}, u32[]{:S(2)}) collective-permute-start(bf16[512,1,256]{0,2,1:T(8,128)(2,1)} %pad_maximum_fusion), channel_id=1, source_target_pairs={{0,8},{4,12},{8,16},{12,20},{16,24},{20,28},{24,32},{28,36},{32,40... | collective-permute-start | bytes 786440 | tf_op jit(solution)/shard_map/ppermute | solution.py:18
  77.3 162.4 %collective-permute-start.1 = (bf16[512,1,256]{2,0,1:T(8,128)(2,1)}, bf16[512,1,256]{2,0,1:T(8,128)(2,1)}, u32[]{:S(2)}, u32[]{:S(2)}) collective-permute-start(bf16[512,1,256]{2,0,1:T(8,128)(2,1)} %fusion.34), channel_id=1, source_target_pairs={{0,4},{4,8},{8,12},{12,16},{16,20},{20,24},{24,28},{28,32},{32,36}... | collective-permute-start | bytes 786440 | tf_op jit(solution)/shard_map/ppermute | solution.py:18
  79.2 160.5 %collective-permute-start = (bf16[512,1,256]{2,0,1:T(8,128)(2,1)}, bf16[512,1,256]{2,0,1:T(8,128)(2,1)}, u32[]{:S(2)}, u32[]{:S(2)}) collective-permute-start(bf16[512,1,256]{2,0,1:T(8,128)(2,1)} %fusion.34), channel_id=1, source_target_pairs={{0,8},{4,12},{8,16},{12,20},{16,24},{20,28},{24,32},{28,36},{32,40... | collective-permute-start | bytes 786440 | tf_op jit(solution)/shard_map/ppermute | solution.py:18
  227.9 3.8 copy-start.6
  227.9 4.6 %copy-start.8 = (bf16[512,3840]{0,1:T(8,128)(2,1)S(1)}, bf16[512,3840]{0,1:T(8,128)(2,1)}, u32[]{:S(2)}) copy-start(bf16[512,3840]{0,1:T(8,128)(2,1)} %all-gather.4.cloned.1.call-done) | copy-start | bytes 11796484
  234.7 1.4 copy-start.3
  235.1 1.5 copy-start.2
  236.6 3.1 copy-start.10
  239.7 4.5 %copy-start.11 = (f32[1536,512,2]{1,0,2:T(8,128)}, f32[1536,512,2]{1,0,2:T(8,128)S(1)}, u32[]{:S(2)}) copy-start(f32[1536,512,2]{1,0,2:T(8,128)S(1)} %get-tuple-element.21) | copy-start | bytes 18874372
  254.2 144.3 %copy-start.1 = (bf16[3840,256]{1,0:T(8,128)(2,1)S(1)}, bf16[3840,256]{1,0:T(8,128)(2,1)}, u32[]{:S(2)}) copy-start(bf16[3840,256]{1,0:T(8,128)(2,1)} %param.13) | copy-start | bytes 5898244
Sparse Core Ops, SparseCore 0:
  9.8 52.1 all-gather.3
  64.8 84.2 all-gather.5
  151.9 75.9 all-gather.7
  254.3 144.1 reduce-scatter.1
where the time goes:
time: 410 us; the launch traced here: 405 us
  waiting for transfers between devices  289 us (70%)
  matrix products  44.1 us (11%)
  starting transfers between devices  21.8 us (5%)
  blocking collectives  19.6 us (5%)
  between operations  14.1 us (3%)
  other arithmetic  10.1 us (2%)
  local copies, waits for them, and re-layouts  6.73 us (2%)
    reduce_scatter x1, waiting for transfers between devices, local(): lax.psum_scatter(jnp.einsum('acr,ace->are', slot_low_rows, slot_grad_rows...  138 us
    all_gather x1, waiting for transfers between devices, local(): lax.all_gather(adapter_down, 'seq', axis=0, tiled=True)  66.4 us
    all_gather x1, waiting for transfers between devices, local(): lax.all_gather(adapter_up, 'seq', axis=0, tiled=True)  52.9 us
    all_gather x1, waiting for transfers between devices, local(): shard_cols = lax.all_gather(tokens, 'tensor', axis=1, tiled=True)  29.1 us
    ppermute x6, starting transfers between devices, passed_along(): lax.ppermute(value, axis, [(source, source + steps) for source in range(f...  21.7 us
    psum x1, blocking collectives, local(): slot_low = lax.psum(partial_low, 'tensor').astype(jnp.bfloat16)  19.6 us
  transfers between devices with their start and end apart: 10, of which 4 were waited for; matrix products, arithmetic and copies ran while one was open for 11% of the time, Pallas kernels for 0%

commit v1 on v0

--- a/solution.py
+++ b/solution.py
@@ -94,28 +94,25 @@
         jnp.bfloat16
     )
     outgoing = jnp.dot(dispatch, tokens, preferred_element_type=jnp.float32).astype(jnp.bfloat16)
-    all_down, all_up = (
-        lax.all_gather(adapter_down, "seq", axis=0, tiled=True),
-        lax.all_gather(adapter_up, "seq", axis=0, tiled=True),
+    seq_count = lax.axis_size("seq")
+    own_adapters = adapter_down.shape[0]
+    arrived = lax.all_to_all(outgoing, "seq", 0, 0, tiled=True).reshape(
+        seq_count, own_adapters, CAP, feat_width
     )
-    slot_rows = outgoing.reshape(ADAPTERS, CAP, feat_width)
     partial_low = jnp.einsum(
-        "acd,ard->acr", slot_rows, all_down, preferred_element_type=jnp.float32
+        "sacd,ard->sacr", arrived, adapter_down, preferred_element_type=jnp.float32
     )
     slot_low = lax.psum(partial_low, "tensor").astype(jnp.bfloat16)
     slot_lift = jnp.einsum(
-        "acr,are->ace", slot_low, all_up, preferred_element_type=jnp.float32
+        "sacr,are->sace", slot_low, adapter_up, preferred_element_type=jnp.float32
     ).astype(jnp.bfloat16)
+    back_lift = lax.all_to_all(
+        slot_lift.reshape(seq_count * own_adapters * CAP, q_width), "seq", 0, 0, tiled=True
+    )
     lifted = jnp.einsum(
         "st,se->te",
         dispatch,
-        slot_lift.reshape(ADAPTERS * CAP, q_width),
-        preferred_element_type=jnp.float32,
-    ).astype(jnp.bfloat16)
-    lowrank = jnp.einsum(
-        "st,sr->tr",
-        dispatch,
-        slot_low.reshape(ADAPTERS * CAP, R),
+        back_lift,
         preferred_element_type=jnp.float32,
     ).astype(jnp.bfloat16)
     query_pre = (query_lin + lifted.astype(jnp.float32)).reshape(tok_count, local_heads, HD)
@@ -158,19 +155,14 @@
     attended = block_out.reshape(tok_count, q_width)
     (dquery_pre,) = query_back(dqueries.reshape(tok_count, local_heads, HD))
     dquery_pre = dquery_pre.reshape(tok_count, q_width).astype(jnp.bfloat16)
-    out_low = jnp.dot(dispatch, lowrank, preferred_element_type=jnp.float32).astype(jnp.bfloat16)
     out_grad = jnp.dot(dispatch, dquery_pre, preferred_element_type=jnp.float32).astype(
         jnp.bfloat16
     )
-    slot_low_rows = out_low.reshape(ADAPTERS, CAP, R)
-    slot_grad_rows = out_grad.reshape(ADAPTERS, CAP, q_width)
-    grad_up = lax.psum_scatter(
-        jnp.einsum(
-            "acr,ace->are", slot_low_rows, slot_grad_rows, preferred_element_type=jnp.float32
-        ),
-        "seq",
-        scatter_dimension=0,
-        tiled=True,
+    grad_rows = lax.all_to_all(out_grad, "seq", 0, 0, tiled=True).reshape(
+        seq_count, own_adapters, CAP, q_width
+    )
+    grad_up = jnp.einsum(
+        "sacr,sace->are", slot_low, grad_rows, preferred_element_type=jnp.float32
     )
     return (attended, grad_up)
 

time: 410 us -> 220 us (0.54); the launches traced: 405 us -> 219 us
  waiting for transfers between devices: 289 us -> 67.7 us
  starting transfers between devices: 21.8 us -> 54.5 us
  other arithmetic: 10.1 us -> 14.5 us
    reduce_scatter x1 -> x0, waiting for transfers between devices: 138 us -> none  [local(): lax.psum_scatter(jnp.einsum('acr,ace->are', slot_low_rows, slot_grad_rows...]
    all_gather x2 -> x0, waiting for transfers between devices: 119 us -> none  [the longest x1 66.4 us: local(): lax.all_gather(adapter_down, 'seq', axis=0, tiled=True)]
    all_to_all x0 -> x3, starting transfers between devices: none -> 34.6 us  [the longest x1 13.5 us: local(): lax.all_to_all(outgoing, 'seq', 0, 0, tiled=True)]
    all_to_all x0 -> x3, waiting for transfers between devices: none -> 33.9 us  [the longest x1 20.4 us: local(): lax.all_to_all(out_grad, 'seq', 0, 0, tiled=True)]
    ppermute x6, waiting for transfers between devices: 0.02 us -> 33 us  [passed_along(): lax.ppermute(value, axis, [(source, source + steps) for source in range(f...]
    all_gather x1, waiting for transfers between devices: 29.1 us -> 0.01 us  [local(): shard_cols = lax.all_gather(tokens, 'tensor', axis=1, tiled=True)]
    dot_general x5 -> x4, matrix products: 15.5 us -> 5.41 us  [the longest x1 2.29 us: local(): jnp.einsum('sacd,ard->sacr', arrived, adapter_down, preferred_element_typ...]
    dot_general x1, matrix products: 2.25 us -> 6.53 us  [local(): query_lin = jnp.dot(shard_cols, w_query, preferred_element_type=jnp.float32)]
  transfers between devices with their start and end apart: 10 -> 10, of which waited for: 4 -> 6; matrix products, arithmetic and copies ran while one was open for 11% -> 23% of each run, Pallas kernels for 0% -> 0%
where the time goes in v1:
time: 220 us; the launch traced here: 219 us
  waiting for transfers between devices  67.7 us (31%)
  starting transfers between devices  54.5 us (25%)
  matrix products  40.7 us (19%)
  blocking collectives  18.4 us (8%)
  other arithmetic  14.5 us (7%)
  between operations  14.5 us (7%)
  local copies, waits for them, and re-layouts  9.09 us (4%)
    ppermute x6, waiting for transfers between devices, passed_along(): lax.ppermute(value, axis, [(source, source + steps) for source in range(f...  33 us
    all_to_all x1, waiting for transfers between devices, local(): lax.all_to_all(out_grad, 'seq', 0, 0, tiled=True)  20.4 us
    ppermute x6, starting transfers between devices, passed_along(): lax.ppermute(value, axis, [(source, source + steps) for source in range(f...  19.8 us
    psum x1, blocking collectives, local(): slot_low = lax.psum(partial_low, 'tensor').astype(jnp.bfloat16)  18.4 us
    all_to_all x1, starting transfers between devices, local(): lax.all_to_all(outgoing, 'seq', 0, 0, tiled=True)  13.5 us
    all_to_all x1, starting transfers between devices, local(): lax.all_to_all(out_grad, 'seq', 0, 0, tiled=True)  10.8 us
    all_to_all x1, starting transfers between devices, local(): lax.all_to_all(slot_lift.reshape(seq_count * own_adapters * CAP, q_width)...  10.4 us
    all_to_all x1, waiting for transfers between devices, local(): lax.all_to_all(outgoing, 'seq', 0, 0, tiled=True)  9.25 us
  transfers between devices with their start and end apart: 10, of which 6 were waited for; matrix products, arithmetic and copies ran while one was open for 23% of the time, Pallas kernels for 0%

profile of v1, /device:TPU:1, one launch (start us, length us, event | category | flops | bytes accessed | tf_op | source)
XLA Modules:
  0.0 219.2 jit_solution(11503913755307704186)
XLA Ops:
  11.6 3.7 %fusion.22 = bf16[1024,960]{0,1:T(8,128)(2,1)} fusion(bf16[512,960]{0,1:T(8,128)(2,1)} %param.11, s32[512]{0:T(512)S(1)} %multiply_add_fusion.3), kind=kOutput, calls=%fused_computation.25 | convolution fusion | flops 1008140288 | bytes 2951168 | tf_op jit(solution)/shard_map/dot_general | solution.py:96
  15.3 3.9 %copy.42 = bf16[1024,960]{1,0:T(8,128)(2,1)} copy(bf16[1024,960]{0,1:T(8,128)(2,1)} %fusion.22) | data formatting | bytes 3932160 | tf_op jit(solution)/shard_map/convert_element_type | solution.py:96
  19.2 13.5 %all-to-all-start = ((bf16[64,16,960]{2,1,0:T(8,128)(2,1)}), bf16[64,16,960]{2,1,0:T(8,128)(2,1)}, u32[]{:S(2)}, u32[]{:S(2)}) async-start(bf16[64,16,960]{2,1,0:T(8,128)(2,1)} %bitcast.143), calls=%async_computation | async-start | bytes 4194304 | tf_op jit(solution)/shard_map/all_to_all | solution.py:99
  32.7 3.3 %collective-permute-start.2 = (s32[512]{0:T(512)S(1)}, s32[512]{0:T(512)S(1)}, u32[]{:S(2)}, u32[]{:S(2)}) collective-permute-start(s32[512]{0:T(512)S(1)} %copy-done.13), channel_id=1, source_target_pairs={{0,8},{4,12},{8,16},{12,20},{16,24},{20,28},{24,32},{28,36},{32,40... | collective-permute-start | bytes 6152 | tf_op jit(solution)/shard_map/ppermute | solution.py:18
  36.0 3.7 %collective-permute-start.3 = (s32[512]{0:T(512)S(1)}, s32[512]{0:T(512)S(1)}, u32[]{:S(2)}, u32[]{:S(2)}) collective-permute-start(s32[512]{0:T(512)S(1)} %copy-done.13), channel_id=1, source_target_pairs={{0,4},{4,8},{8,12},{12,16},{16,20},{20,24},{24,28},{28,32},{32,36}... | collective-permute-start | bytes 6152 | tf_op jit(solution)/shard_map/ppermute | solution.py:18
  42.1 32.5 %collective-permute-done.2 = s32[512]{0:T(512)S(1)} collective-permute-done((s32[512]{0:T(512)S(1)}, s32[512]{0:T(512)S(1)}, u32[]{:S(2)}, u32[]{:S(2)}) %collective-permute-start.2) | collective-permute-done | bytes 2080 | tf_op jit(solution)/shard_map/ppermute | solution.py:18
  74.7 9.3 %all-to-all-done = bf16[64,16,960]{2,1,0:T(8,128)(2,1)} async-done(((bf16[64,16,960]{2,1,0:T(8,128)(2,1)}), bf16[64,16,960]{2,1,0:T(8,128)(2,1)}, u32[]{:S(2)}, u32[]{:S(2)}) %all-to-all-start) | async-done | bytes 1966112 | tf_op jit(solution)/shard_map/all_to_all | solution.py:99
  84.0 2.3 %convolution_bitcast_fusion = f32[64,1,16,64]{3,2,0,1:T(8,128)S(1)} fusion(bf16[64,16,960]{2,1,0:T(8,128)(2,1)} %all-to-all-done, bf16[1,64,960]{2,1,0:T(8,128)(2,1)S(1)} %copy-done.7), kind=kOutput, calls=%fused_computation.34 | convolution fusion | flops 125829120 | bytes 2351104 | tf_op jit(solution)/shard_map/sacd,ard->sacr/dot_general | solution.py:102
  86.3 18.4 %all-reduce.3 = bf16[64,1,16,64]{3,2,0,1:T(8,128)(2,1)S(1)} all-reduce(f32[64,1,16,64]{3,2,0,1:T(8,128)S(1)} %convolution_bitcast_fusion), channel_id=1, replica_groups=mesh['seq'=64,'tensor'=4] {'tensor'}, use_global_device_ids=true, to_apply=%region_4.5 | all-reduce | flops 65536 | bytes 393216 | tf_op jit(solution)/shard_map/psum | solution.py:105
  106.1 10.4 %all-to-all-start.1 = ((bf16[64,16,512]{2,1,0:T(8,128)(2,1)}), bf16[64,16,512]{2,1,0:T(8,128)(2,1)S(1)}, u32[]{:S(2)}, u32[]{:S(2)}) async-start(bf16[64,16,512]{2,1,0:T(8,128)(2,1)} %convolution_convert_fusion), calls=%async_computation.1 | async-start | bytes 2097152 | tf_op jit(solution)/shard_map/all_to_all | solution.py:109
  116.5 3.6 %fusion.16 = pred[512,1536]{0,1:T(8,128)(4,1)} fusion(s32[1536]{0:T(1024)S(1)} %pad_add_fusion.1, s32[512]{0:T(512)} %copy-done.9, s32[512]{0:T(512)} %param.20, s32[1536]{0:T(1024)S(1)} %pad_add_fusion, pred[1536]{0:T(1024)(128)(4,1)} %broadcast_compare_fusion), kind=kLoop, calls=%fused_computation.20 | loop fusion | flops 5505024 | bytes 804352 | tf_op jit(solution)/shard_map/and | solution.py:148
  120.1 4.8 %fusion.32 = bf16[512,1,256]{2,0,1:T(8,128)(2,1)} fusion(bf16[512,3840]{0,1:T(8,128)(2,1)} %all-gather.2.cloned.1.call-done, bf16[3840,256]{1,0:T(8,128)(2,1)} %param.14), kind=kOutput, calls=%fused_computation.36 | convolution fusion | flops 1006764032 | bytes 6160384 | tf_op jit(solution)/shard_map/dot_general | solution.py:87
  125.0 3.7 %collective-permute-start.1 = (bf16[512,1,256]{2,0,1:T(8,128)(2,1)}, bf16[512,1,256]{2,0,1:T(8,128)(2,1)}, u32[]{:S(2)}, u32[]{:S(2)}) collective-permute-start(bf16[512,1,256]{2,0,1:T(8,128)(2,1)} %fusion.32), channel_id=1, source_target_pairs={{0,4},{4,8},{8,12},{12,16},{16,20},{20,24},{24,28},{28,32},{32,36}... | collective-permute-start | bytes 786440 | tf_op jit(solution)/shard_map/ppermute | solution.py:18
  128.6 3.8 %collective-permute-start = (bf16[512,1,256]{2,0,1:T(8,128)(2,1)}, bf16[512,1,256]{2,0,1:T(8,128)(2,1)}, u32[]{:S(2)}, u32[]{:S(2)}) collective-permute-start(bf16[512,1,256]{2,0,1:T(8,128)(2,1)} %fusion.32), channel_id=1, source_target_pairs={{0,8},{4,12},{8,16},{12,20},{16,24},{20,28},{24,32},{28,36},{32,40... | collective-permute-start | bytes 786440 | tf_op jit(solution)/shard_map/ppermute | solution.py:18
  137.8 3.5 %collective-permute-start.4 = (bf16[512,1,256]{0,2,1:T(8,128)(2,1)}, bf16[512,1,256]{0,2,1:T(8,128)(2,1)}, u32[]{:S(2)}, u32[]{:S(2)}) collective-permute-start(bf16[512,1,256]{0,2,1:T(8,128)(2,1)} %pad_maximum_fusion), channel_id=1, source_target_pairs={{0,8},{4,12},{8,16},{12,20},{16,24},{20,28},{24,32},{28,36},{32,40... | collective-permute-start | bytes 786440 | tf_op jit(solution)/shard_map/ppermute | solution.py:18
  141.3 4.3 %all-to-all-done.1 = bf16[64,16,512]{2,1,0:T(8,128)(2,1)S(1)} async-done(((bf16[64,16,512]{2,1,0:T(8,128)(2,1)}), bf16[64,16,512]{2,1,0:T(8,128)(2,1)S(1)}, u32[]{:S(2)}, u32[]{:S(2)}) %all-to-all-start.1) | async-done | bytes 1048608 | tf_op jit(solution)/shard_map/all_to_all | solution.py:109
  146.3 6.5 %multiply_reduce_fusion.1 = (f32[512,2]{0,1:T(2,128)S(1)}, f32[512,512]{0,1:T(8,128)}) fusion(f32[512,512]{0,1:T(8,128)S(1)} %fusion.28, bf16[512,3840]{0,1:T(8,128)(2,1)} %all-gather.2.cloned.1.call-done, bf16[3840,512]{1,0:T(8,128)(2,1)} %param.12), kind=kOutput, calls=%fused_computation.42 | convolution fusion | flops 2014051328 | bytes 9965568 | tf_op jit(solution)/shard_map/dot_general | solution.py:85
  156.3 3.1 %fusion.5 = (f32[2,512]{1,0:T(2,128)S(1)}, f32[1536,512,2]{1,0,2:T(8,128)S(1)}) fusion(pred[512,1536]{0,1:T(8,128)(4,1)S(1)} %copy-done.2, bf16[512,2,128]{2,0,1:T(8,128)(2,1)S(1)} %get-tuple-element.11, bf16[512,2,128]{2,0,1:T(8,128)(2,1)S(1)} %get-tuple-element.10, bf16[512,1,128]{0,2,1:T(8,128)(2,1)S(1)} %copy-done.6, ...), kind=kOutput, calls=%fused_computation.8 | convolution fusion | flops 814218240 | bytes 8392704 | tf_op jit(solution)/shard_map/tngd,knd->ngtk/dot_general | solution.py:49
  159.5 4.2 %fusion = (f32[2,512]{1,0:T(2,128)S(1)}, f32[1536,512,2]{1,0,2:T(8,128)S(1)}) fusion(f32[2,512]{1,0:T(2,128)S(1)} %get-tuple-element.20, f32[1536,512,2]{1,0,2:T(8,128)S(1)} %get-tuple-element.21, pred[512,1536]{0,1:T(8,128)(4,1)S(1)} %copy-done.2, bf16[64,2,8,256]{3,2,1,0:T(8,128)(2,1)S(1)} %bitcast.152, bf16[512,1,256]{2,0,1:T(8,128)(2,1)} %fusion.32, ...), kind=kOutput, calls=%fused_computation.3 | convolution fusion | flops 815528960 | bytes 14688256 | tf_op jit(solution)/shard_map/tngd,knd->ngtk/dot_general | solution.py:56
  163.7 3.8 %fusion.24 = f32[512,2,256]{2,0,1:T(8,128)S(1)} fusion(f32[1536,512,2]{1,0,2:T(8,128)S(1)} %get-tuple-element.23, f32[2,512]{1,0:T(2,128)S(1)} %get-tuple-element.22, f32[2,512]{1,0:T(2,128)S(1)} %get-tuple-element.20, f32[1536,512,2]{1,0,2:T(8,128)S(1)} %get-tuple-element.21, pred[512,1536]{0,1:T(8,128)(4,1)S(1)} %copy-done.2, ...), kind=kOutput, calls=%fused_computation.29 | convolution fusion | flops 819462144 | bytes 15212544 | tf_op jit(solution)/shard_map/ngtk,knd->tngd/dot_general | solution.py:59
  172.1 10.8 %all-to-all-start.2 = ((bf16[64,16,512]{2,1,0:T(8,128)(2,1)}), bf16[64,16,512]{2,1,0:T(8,128)(2,1)S(1)}, u32[]{:S(2)}, u32[]{:S(2)}) async-start(bf16[64,16,512]{2,1,0:T(8,128)(2,1)} %bitcast.145), calls=%async_computation.2 | async-start | bytes 2097152 | tf_op jit(solution)/shard_map/all_to_all | solution.py:161
  182.9 6.0 %fusion.29 = bf16[256,2,512]{2,0,1:T(8,128)(2,1)} fusion(f32[2,512]{1,0:T(2,128)S(1)} %get-tuple-element.20, f32[1536,512,2]{1,0,2:T(8,128)} %copy-done.21, pred[512,1536]{0,1:T(8,128)(4,1)} %fusion.16, bf16[512,1,256]{2,0,1:T(8,128)(2,1)} %fusion.32, bf16[512,1,256]{2,0,1:T(8,128)(2,1)} %collective-permute-done.1, ...), kind=kOutput, calls=%fused_computation.33 | convolution fusion | flops 814219264 | bytes 8392704 | tf_op jit(solution)/shard_map/ngtk,knd->tngd/dot_general | solution.py:55
  188.9 2.0 copy.55
  191.0 20.4 %all-to-all-done.2 = bf16[64,16,512]{2,1,0:T(8,128)(2,1)S(1)} async-done(((bf16[64,16,512]{2,1,0:T(8,128)(2,1)}), bf16[64,16,512]{2,1,0:T(8,128)(2,1)S(1)}, u32[]{:S(2)}, u32[]{:S(2)}) %all-to-all-start.2) | async-done | bytes 1048608 | tf_op jit(solution)/shard_map/all_to_all | solution.py:161
  (86 shorter events, 23.2 us)
Async XLA Ops:
  7.2 125.3 %copy-start = (bf16[3840,256]{1,0:T(8,128)(2,1)S(1)}, bf16[3840,256]{1,0:T(8,128)(2,1)}, u32[]{:S(2)}) copy-start(bf16[3840,256]{1,0:T(8,128)(2,1)} %param.13) | copy-start | bytes 5898244
  7.2 112.9 %all-gather.2.cloned.1.call-start = ((), (), s32[]{:S(2)}) async-start(), calls=%async_computation.3 | async-start | bytes 4915200 | tf_op jit(solution)/shard_map/all_gather | solution.py:84
  15.3 17.4 %copy-start.13 = (s32[512]{0:T(512)S(1)}, s32[512]{0:T(512)}, u32[]{:S(2)}) copy-start(s32[512]{0:T(512)} %param.20) | copy-start | bytes 6148
  19.2 64.7 %copy-start.7 = (bf16[1,64,960]{2,1,0:T(8,128)(2,1)S(1)}, bf16[1,64,960]{2,1,0:T(8,128)(2,1)}, u32[]{:S(2)}) copy-start(bf16[1,64,960]{2,1,0:T(8,128)(2,1)} %param.17) | copy-start | bytes 368644
  19.2 85.5 %copy-start.8 = (bf16[1,64,512]{2,1,0:T(8,128)(2,1)S(1)}, bf16[1,64,512]{2,1,0:T(8,128)(2,1)}, u32[]{:S(2)}) copy-start(bf16[1,64,512]{2,1,0:T(8,128)(2,1)} %param.18) | copy-start | bytes 196612
  19.2 64.7 %all-to-all-start = ((bf16[64,16,960]{2,1,0:T(8,128)(2,1)}), bf16[64,16,960]{2,1,0:T(8,128)(2,1)}, u32[]{:S(2)}, u32[]{:S(2)}) async-start(bf16[64,16,960]{2,1,0:T(8,128)(2,1)} %bitcast.143), calls=%async_computation | async-start | bytes 4194304 | tf_op jit(solution)/shard_map/all_to_all | solution.py:99
  32.7 41.9 %collective-permute-start.2 = (s32[512]{0:T(512)S(1)}, s32[512]{0:T(512)S(1)}, u32[]{:S(2)}, u32[]{:S(2)}) collective-permute-start(s32[512]{0:T(512)S(1)} %copy-done.13), channel_id=1, source_target_pairs={{0,8},{4,12},{8,16},{12,20},{16,24},{20,28},{24,32},{28,36},{32,40... | collective-permute-start | bytes 6152 | tf_op jit(solution)/shard_map/ppermute | solution.py:18
  36.0 38.7 %collective-permute-start.3 = (s32[512]{0:T(512)S(1)}, s32[512]{0:T(512)S(1)}, u32[]{:S(2)}, u32[]{:S(2)}) collective-permute-start(s32[512]{0:T(512)S(1)} %copy-done.13), channel_id=1, source_target_pairs={{0,4},{4,8},{8,12},{12,16},{16,20},{20,24},{24,28},{28,32},{32,36}... | collective-permute-start | bytes 6152 | tf_op jit(solution)/shard_map/ppermute | solution.py:18
  39.7 44.3 %copy-start.16 = (f32[128]{0:T(128)}, f32[128]{0:T(128)S(1)}, u32[]{:S(2)}) copy-start(f32[128]{0:T(128)S(1)} %multiply_exponential_fusion) | copy-start | bytes 1540
  39.7 44.3 %copy-start.9 = (s32[512]{0:T(512)}, s32[512]{0:T(512)S(1)}, u32[]{:S(2)}) copy-start(s32[512]{0:T(512)S(1)} %iota_add_fusion) | copy-start | bytes 6148
  39.7 44.3 %copy-start.10 = (f32[512]{0:T(512)}, f32[512]{0:T(512)S(1)}, u32[]{:S(2)}) copy-start(f32[512]{0:T(512)S(1)} %fusion.62) | copy-start | bytes 6148
  106.1 39.4 %all-to-all-start.1 = ((bf16[64,16,512]{2,1,0:T(8,128)(2,1)}), bf16[64,16,512]{2,1,0:T(8,128)(2,1)S(1)}, u32[]{:S(2)}, u32[]{:S(2)}) async-start(bf16[64,16,512]{2,1,0:T(8,128)(2,1)} %convolution_convert_fusion), calls=%async_computation.1 | async-start | bytes 2097152 | tf_op jit(solution)/shard_map/all_to_all | solution.py:109
  120.1 12.3 %copy-start.19 = (bf16[512,3840]{0,1:T(8,128)(2,1)S(1)}, bf16[512,3840]{0,1:T(8,128)(2,1)}, u32[]{:S(2)}) copy-start(bf16[512,3840]{0,1:T(8,128)(2,1)} %all-gather.2.cloned.1.call-done) | copy-start | bytes 11796484
  124.9 8.8 %copy-start.18 = (f32[256]{0:T(256)S(1)}, f32[256]{0:T(256)}, u32[]{:S(2)}) copy-start(f32[256]{0:T(256)} %param.16) | copy-start | bytes 3076
  124.9 8.9 %copy-start.11 = (f32[512]{0:T(512)S(1)}, f32[512]{0:T(512)}, u32[]{:S(2)}) copy-start(f32[512]{0:T(512)} %copy-done.10) | copy-start | bytes 6148
  124.9 8.9 %copy-start.17 = (f32[128]{0:T(128)S(1)}, f32[128]{0:T(128)}, u32[]{:S(2)}) copy-start(f32[128]{0:T(128)} %copy-done.16) | copy-start | bytes 1540
  124.9 20.6 %copy-start.15 = (s32[512]{0:T(512)S(1)}, s32[512]{0:T(512)}, u32[]{:S(2)}) copy-start(s32[512]{0:T(512)} %copy-done.14) | copy-start | bytes 6148
  125.0 34.5 %collective-permute-start.1 = (bf16[512,1,256]{2,0,1:T(8,128)(2,1)}, bf16[512,1,256]{2,0,1:T(8,128)(2,1)}, u32[]{:S(2)}, u32[]{:S(2)}) collective-permute-start(bf16[512,1,256]{2,0,1:T(8,128)(2,1)} %fusion.32), channel_id=1, source_target_pairs={{0,4},{4,8},{8,12},{12,16},{16,20},{20,24},{24,28},{28,32},{32,36}... | collective-permute-start | bytes 786440 | tf_op jit(solution)/shard_map/ppermute | solution.py:18
  128.6 30.8 %collective-permute-start = (bf16[512,1,256]{2,0,1:T(8,128)(2,1)}, bf16[512,1,256]{2,0,1:T(8,128)(2,1)}, u32[]{:S(2)}, u32[]{:S(2)}) collective-permute-start(bf16[512,1,256]{2,0,1:T(8,128)(2,1)} %fusion.32), channel_id=1, source_target_pairs={{0,8},{4,12},{8,16},{12,20},{16,24},{20,28},{24,32},{28,36},{32,40... | collective-permute-start | bytes 786440 | tf_op jit(solution)/shard_map/ppermute | solution.py:18
  135.8 20.0 %collective-permute-start.5 = (bf16[512,1,256]{0,2,1:T(8,128)(2,1)}, bf16[512,1,256]{0,2,1:T(8,128)(2,1)}, u32[]{:S(2)}, u32[]{:S(2)}) collective-permute-start(bf16[512,1,256]{0,2,1:T(8,128)(2,1)} %pad_maximum_fusion), channel_id=1, source_target_pairs={{0,4},{4,8},{8,12},{12,16},{16,20},{20,24},{24,28},{28,32},{32,36}... | collective-permute-start | bytes 786440 | tf_op jit(solution)/shard_map/ppermute | solution.py:18
  137.8 18.5 %collective-permute-start.4 = (bf16[512,1,256]{0,2,1:T(8,128)(2,1)}, bf16[512,1,256]{0,2,1:T(8,128)(2,1)}, u32[]{:S(2)}, u32[]{:S(2)}) collective-permute-start(bf16[512,1,256]{0,2,1:T(8,128)(2,1)} %pad_maximum_fusion), channel_id=1, source_target_pairs={{0,8},{4,12},{8,16},{12,20},{16,24},{20,28},{24,32},{28,36},{32,40... | collective-permute-start | bytes 786440 | tf_op jit(solution)/shard_map/ppermute | solution.py:18
  146.3 8.2 %copy-start.12 = (f32[256]{0:T(256)S(1)}, f32[256]{0:T(256)}, u32[]{:S(2)}) copy-start(f32[256]{0:T(256)} %param.15) | copy-start | bytes 3076
  159.4 4.2 %copy-start.21 = (f32[1536,512,2]{1,0,2:T(8,128)}, f32[1536,512,2]{1,0,2:T(8,128)S(1)}, u32[]{:S(2)}) copy-start(f32[1536,512,2]{1,0,2:T(8,128)S(1)} %get-tuple-element.21) | copy-start | bytes 18874372
  172.1 39.3 %all-to-all-start.2 = ((bf16[64,16,512]{2,1,0:T(8,128)(2,1)}), bf16[64,16,512]{2,1,0:T(8,128)(2,1)S(1)}, u32[]{:S(2)}, u32[]{:S(2)}) async-start(bf16[64,16,512]{2,1,0:T(8,128)(2,1)} %bitcast.145), calls=%async_computation.2 | async-start | bytes 2097152 | tf_op jit(solution)/shard_map/all_to_all | solution.py:161
  (8 other events, 21.8 us)
Sparse Core Ops, SparseCore 0:
  9.8 52.1 all-gather.1

commit v2 on v1

--- a/solution.py
+++ b/solution.py
@@ -95,19 +95,26 @@
     )
     outgoing = jnp.dot(dispatch, tokens, preferred_element_type=jnp.float32).astype(jnp.bfloat16)
     seq_count = lax.axis_size("seq")
-    own_adapters = adapter_down.shape[0]
-    arrived = lax.all_to_all(outgoing, "seq", 0, 0, tiled=True).reshape(
-        seq_count, own_adapters, CAP, feat_width
+    tensor_count = lax.axis_size("tensor")
+    part = CAP // tensor_count
+    both = ("seq", "tensor")
+    down_full = lax.all_gather(adapter_down, "tensor", axis=2, tiled=True)[0].reshape(
+        R, tensor_count, feat_width
     )
-    partial_low = jnp.einsum(
-        "sacd,ard->sacr", arrived, adapter_down, preferred_element_type=jnp.float32
+    up_full = lax.all_gather(adapter_up, "tensor", axis=2, tiled=True)[0].reshape(
+        R, tensor_count, q_width
     )
-    slot_low = lax.psum(partial_low, "tensor").astype(jnp.bfloat16)
+    arrived = lax.all_to_all(outgoing, both, 0, 0, tiled=True).reshape(
+        seq_count, tensor_count, part, feat_width
+    )
+    slot_low = jnp.einsum(
+        "stkf,rtf->skr", arrived, down_full, preferred_element_type=jnp.float32
+    ).astype(jnp.bfloat16)
     slot_lift = jnp.einsum(
-        "sacr,are->sace", slot_low, adapter_up, preferred_element_type=jnp.float32
+        "skr,rte->stke", slot_low, up_full, preferred_element_type=jnp.float32
     ).astype(jnp.bfloat16)
     back_lift = lax.all_to_all(
-        slot_lift.reshape(seq_count * own_adapters * CAP, q_width), "seq", 0, 0, tiled=True
+        slot_lift.reshape(seq_count * tensor_count * part, q_width), both, 0, 0, tiled=True
     )
     lifted = jnp.einsum(
         "st,se->te",
@@ -158,12 +165,13 @@
     out_grad = jnp.dot(dispatch, dquery_pre, preferred_element_type=jnp.float32).astype(
         jnp.bfloat16
     )
+    low_rows = lax.all_gather(slot_low, "tensor", axis=0)
     grad_rows = lax.all_to_all(out_grad, "seq", 0, 0, tiled=True).reshape(
-        seq_count, own_adapters, CAP, q_width
+        seq_count, tensor_count, part, q_width
     )
     grad_up = jnp.einsum(
-        "sacr,sace->are", slot_low, grad_rows, preferred_element_type=jnp.float32
-    )
+        "tskr,stke->re", low_rows, grad_rows, preferred_element_type=jnp.float32
+    )[None]
     return (attended, grad_up)
 
 

time: 220 us -> 237 us (1.077)
  blocking collectives: 18.4 us -> 70.5 us
  waiting for transfers between devices: 67.7 us -> 17.7 us
  local copies, waits for them, and re-layouts: 9.09 us -> 20.5 us
  starting transfers between devices: 54.5 us -> 57.5 us
  other arithmetic: 14.5 us -> 11.9 us
    all_gather x0 -> x3, blocking collectives: none -> 70.5 us  [the longest x1 50.9 us: local(): lax.all_gather(adapter_down, 'tensor', axis=2, tiled=True)[0]]
    ppermute x6, waiting for transfers between devices: 33 us -> 0.02 us  [passed_along(): lax.ppermute(value, axis, [(source, source + steps) for source in range(f...]
    psum x1 -> x0, blocking collectives: 18.4 us -> none  [local(): slot_low = lax.psum(partial_low, 'tensor').astype(jnp.bfloat16)]
    all_to_all x1, waiting for transfers between devices: 20.4 us -> 10.2 us  [local(): lax.all_to_all(out_grad, 'seq', 0, 0, tiled=True)]
    all_to_all x2, starting transfers between devices: 23.8 us -> 31 us  [the longest x1 16.7 us: local(): lax.all_to_all(outgoing, both, 0, 0, tiled=True)]
    all_to_all x2, waiting for transfers between devices: 13.5 us -> 6.77 us  [the longest x1 6.77 us: local(): lax.all_to_all(slot_lift.reshape(seq_count * tensor_count * part, q_width...]
    all_to_all x0 -> x3, local copies, waits for them, and re-layouts: none -> 5.83 us  [the longest x1 4.14 us: local(): lax.all_to_all(outgoing, both, 0, 0, tiled=True)]
    all_to_all x1, starting transfers between devices: 10.8 us -> 5.59 us  [local(): lax.all_to_all(out_grad, 'seq', 0, 0, tiled=True)]
  transfers between devices with their start and end apart: 10 -> 10, of which waited for: 6 -> 2; matrix products, arithmetic and copies ran while one was open for 23% -> 24% of each run, Pallas kernels for 0% -> 0%
where the time goes in v2:
time: 237 us; the launch traced here: 236 us
  blocking collectives  70.5 us (30%)
  starting transfers between devices  57.5 us (24%)
  matrix products  43 us (18%)
  local copies, waits for them, and re-layouts  20.5 us (9%)
  waiting for transfers between devices  17.7 us (7%)
  between operations  14.6 us (6%)
  other arithmetic  11.9 us (5%)
    all_gather x1, blocking collectives, local(): lax.all_gather(adapter_down, 'tensor', axis=2, tiled=True)[0]  50.9 us
    ppermute x6, starting transfers between devices, passed_along(): lax.ppermute(value, axis, [(source, source + steps) for source in range(f...  20.9 us
    all_to_all x1, starting transfers between devices, local(): lax.all_to_all(outgoing, both, 0, 0, tiled=True)  16.7 us
    all_to_all x1, starting transfers between devices, local(): lax.all_to_all(slot_lift.reshape(seq_count * tensor_count * part, q_width...  14.3 us
    all_gather x1, blocking collectives, local(): low_rows = lax.all_gather(slot_low, 'tensor', axis=0)  10.3 us
    all_to_all x1, waiting for transfers between devices, local(): lax.all_to_all(out_grad, 'seq', 0, 0, tiled=True)  10.2 us
    all_gather x1, blocking collectives, local(): lax.all_gather(adapter_up, 'tensor', axis=2, tiled=True)[0]  9.37 us
    unnamed x49, local copies, waits for them, and re-layouts  6.82 us
  transfers between devices with their start and end apart: 10, of which 2 were waited for; matrix products, arithmetic and copies ran while one was open for 24% of the time, Pallas kernels for 0%

profile of v2, /device:TPU:1, one launch (start us, length us, event | category | flops | bytes accessed | tf_op | source)
XLA Modules:
  0.0 235.6 jit_solution(1265424127064517056)
XLA Ops:
  12.2 3.7 %fusion.24 = bf16[1024,960]{0,1:T(8,128)(2,1)} fusion(bf16[512,960]{0,1:T(8,128)(2,1)} %param.11, s32[512]{0:T(512)S(1)} %multiply_add_fusion.3), kind=kOutput, calls=%fused_computation.27 | convolution fusion | flops 1008140288 | bytes 2951168 | tf_op jit(solution)/shard_map/dot_general | solution.py:96
  15.9 3.9 %copy.45 = bf16[1024,960]{1,0:T(8,128)(2,1)} copy(bf16[1024,960]{0,1:T(8,128)(2,1)} %fusion.24) | data formatting | bytes 3932160 | tf_op jit(solution)/shard_map/convert_element_type | solution.py:96
  19.8 4.1 %all_to_all.20 = bf16[256,4,960]{2,1,0:T(4,128)(2,1)} reshape(bf16[1024,960]{1,0:T(8,128)(2,1)} %copy.45) | data formatting | bytes 3932160 | tf_op jit(solution)/shard_map/all_to_all | solution.py:107
  24.0 16.7 %all-to-all-start = ((bf16[256,4,960]{2,1,0:T(4,128)(2,1)}), bf16[256,4,960]{2,1,0:T(4,128)(2,1)}, u32[]{:S(2)}, u32[]{:S(2)}) async-start(bf16[256,4,960]{2,1,0:T(4,128)(2,1)} %all_to_all.20), calls=%async_computation | async-start | bytes 4194304 | tf_op jit(solution)/shard_map/all_to_all | solution.py:107
  40.7 3.4 %collective-permute-start.2 = (s32[512]{0:T(512)S(1)}, s32[512]{0:T(512)S(1)}, u32[]{:S(2)}, u32[]{:S(2)}) collective-permute-start(s32[512]{0:T(512)S(1)} %copy-done.14), channel_id=1, source_target_pairs={{0,8},{4,12},{8,16},{12,20},{16,24},{20,28},{24,32},{28,36},{32,40... | collective-permute-start | bytes 6152 | tf_op jit(solution)/shard_map/ppermute | solution.py:18
  44.1 3.9 %collective-permute-start.3 = (s32[512]{0:T(512)S(1)}, s32[512]{0:T(512)S(1)}, u32[]{:S(2)}, u32[]{:S(2)}) collective-permute-start(s32[512]{0:T(512)S(1)} %copy-done.14), channel_id=1, source_target_pairs={{0,4},{4,8},{8,12},{12,16},{16,20},{20,24},{24,28},{28,32},{32,36}... | collective-permute-start | bytes 6152 | tf_op jit(solution)/shard_map/ppermute | solution.py:18
  49.4 50.9 %all_gather.16 = bf16[1,64,3840]{1,0,2:T(2,128)(2,1)} all-gather(bf16[1,64,960]{1,0,2:T(2,128)(2,1)S(1)} %copy.46), channel_id=1, replica_groups=mesh['seq'=64,'tensor'=4] {'tensor'}, dimensions={2}, use_global_device_ids=true | all-gather | bytes 614400 | tf_op jit(solution)/shard_map/all_gather | solution.py:101
  101.3 9.4 %all_gather.17 = bf16[1,64,2048]{2,1,0:T(8,128)(2,1)S(1)} all-gather(bf16[1,64,512]{2,1,0:T(8,128)(2,1)S(1)} %copy-done.9), channel_id=1, replica_groups=mesh['seq'=64,'tensor'=4] {'tensor'}, dimensions={2}, use_global_device_ids=true | all-gather | bytes 327680 | tf_op jit(solution)/shard_map/all_gather | solution.py:104
  113.5 4.3 %fusion.39 = bf16[64,4,64]{2,0,1:T(8,128)(2,1)S(1)} fusion(bf16[64,4,960,1]{0,2,1,3:T(8,128)(2,1)} %bitcast.153, bf16[64,4,4,960]{3,2,1,0:T(4,128)(2,1)} %bitcast.9), kind=kOutput, calls=%fused_computation.41 | convolution fusion | flops 125845504 | bytes 2490368 | tf_op jit(solution)/shard_map/stkf,rtf->skr/dot_general | solution.py:110
  120.1 14.3 %all-to-all-start.1 = ((bf16[256,4,512]{2,1,0:T(4,128)(2,1)}), bf16[256,4,512]{2,1,0:T(4,128)(2,1)S(1)}, u32[]{:S(2)}, u32[]{:S(2)}) async-start(bf16[256,4,512]{2,1,0:T(4,128)(2,1)} %bitcast.148), calls=%async_computation.1 | async-start | bytes 2097152 | tf_op jit(solution)/shard_map/all_to_all | solution.py:116
  134.5 3.7 %fusion.16 = pred[512,1536]{0,1:T(8,128)(4,1)} fusion(s32[1536]{0:T(1024)S(1)} %pad_add_fusion.1, s32[512]{0:T(512)} %copy-done.10, s32[512]{0:T(512)} %param.20, s32[1536]{0:T(1024)S(1)} %pad_add_fusion, pred[1536]{0:T(1024)(128)(4,1)} %broadcast_compare_fusion), kind=kLoop, calls=%fused_computation.20 | loop fusion | flops 5505024 | bytes 804352 | tf_op jit(solution)/shard_map/and | solution.py:155
  138.1 4.8 %fusion.35 = bf16[512,1,256]{2,0,1:T(8,128)(2,1)} fusion(bf16[512,3840]{0,1:T(8,128)(2,1)} %all-gather.3.cloned.1.call-done, bf16[3840,256]{1,0:T(8,128)(2,1)} %param.14), kind=kOutput, calls=%fused_computation.38 | convolution fusion | flops 1006764032 | bytes 6160384 | tf_op jit(solution)/shard_map/dot_general | solution.py:87
  143.0 3.8 %collective-permute-start.1 = (bf16[512,1,256]{2,0,1:T(8,128)(2,1)}, bf16[512,1,256]{2,0,1:T(8,128)(2,1)}, u32[]{:S(2)}, u32[]{:S(2)}) collective-permute-start(bf16[512,1,256]{2,0,1:T(8,128)(2,1)} %fusion.35), channel_id=1, source_target_pairs={{0,4},{4,8},{8,12},{12,16},{16,20},{20,24},{24,28},{28,32},{32,36}... | collective-permute-start | bytes 786440 | tf_op jit(solution)/shard_map/ppermute | solution.py:18
  146.8 4.1 %collective-permute-start = (bf16[512,1,256]{2,0,1:T(8,128)(2,1)}, bf16[512,1,256]{2,0,1:T(8,128)(2,1)}, u32[]{:S(2)}, u32[]{:S(2)}) collective-permute-start(bf16[512,1,256]{2,0,1:T(8,128)(2,1)} %fusion.35), channel_id=1, source_target_pairs={{0,8},{4,12},{8,16},{12,20},{16,24},{20,28},{24,32},{28,36},{32,40... | collective-permute-start | bytes 786440 | tf_op jit(solution)/shard_map/ppermute | solution.py:18
  156.1 3.8 %collective-permute-start.4 = (bf16[512,1,256]{0,2,1:T(8,128)(2,1)}, bf16[512,1,256]{0,2,1:T(8,128)(2,1)}, u32[]{:S(2)}, u32[]{:S(2)}) collective-permute-start(bf16[512,1,256]{0,2,1:T(8,128)(2,1)} %pad_maximum_fusion), channel_id=1, source_target_pairs={{0,8},{4,12},{8,16},{12,20},{16,24},{20,28},{24,32},{28,36},{32,40... | collective-permute-start | bytes 786440 | tf_op jit(solution)/shard_map/ppermute | solution.py:18
  159.9 6.8 %all-to-all-done.1 = bf16[256,4,512]{2,1,0:T(4,128)(2,1)S(1)} async-done(((bf16[256,4,512]{2,1,0:T(4,128)(2,1)}), bf16[256,4,512]{2,1,0:T(4,128)(2,1)S(1)}, u32[]{:S(2)}, u32[]{:S(2)}) %all-to-all-start.1) | async-done | bytes 1048608 | tf_op jit(solution)/shard_map/all_to_all | solution.py:116
  169.8 6.5 %multiply_reduce_fusion.1 = (f32[512,2]{0,1:T(2,128)S(1)}, f32[512,512]{0,1:T(8,128)}) fusion(f32[512,512]{0,1:T(8,128)S(1)} %fusion.31, bf16[512,3840]{0,1:T(8,128)(2,1)} %all-gather.3.cloned.1.call-done, bf16[3840,512]{1,0:T(8,128)(2,1)} %param.12), kind=kOutput, calls=%fused_computation.47 | convolution fusion | flops 2014051328 | bytes 9965568 | tf_op jit(solution)/shard_map/dot_general | solution.py:85
  179.1 3.1 %fusion.5 = (f32[2,512]{1,0:T(2,128)S(1)}, f32[1536,512,2]{1,0,2:T(8,128)S(1)}) fusion(pred[512,1536]{0,1:T(8,128)(4,1)S(1)} %copy-done.1, bf16[512,2,128]{2,0,1:T(8,128)(2,1)S(1)} %get-tuple-element.11, bf16[512,2,128]{2,0,1:T(8,128)(2,1)S(1)} %get-tuple-element.10, bf16[512,1,128]{0,2,1:T(8,128)(2,1)S(1)} %copy-done.5, ...), kind=kOutput, calls=%fused_computation.8 | convolution fusion | flops 814218240 | bytes 8392704 | tf_op jit(solution)/shard_map/tngd,knd->ngtk/dot_general | solution.py:49
  182.3 4.2 %fusion = (f32[2,512]{1,0:T(2,128)S(1)}, f32[1536,512,2]{1,0,2:T(8,128)S(1)}) fusion(f32[2,512]{1,0:T(2,128)S(1)} %get-tuple-element.20, f32[1536,512,2]{1,0,2:T(8,128)S(1)} %get-tuple-element.21, pred[512,1536]{0,1:T(8,128)(4,1)S(1)} %copy-done.1, bf16[64,2,8,256]{3,2,1,0:T(8,128)(2,1)S(1)} %bitcast.159, bf16[512,1,256]{2,0,1:T(8,128)(2,1)} %fusion.35, ...), kind=kOutput, calls=%fused_computation.3 | convolution fusion | flops 815528960 | bytes 14688256 | tf_op jit(solution)/shard_map/tngd,knd->ngtk/dot_general | solution.py:56
  186.5 3.8 %fusion.27 = f32[512,2,256]{2,0,1:T(8,128)S(1)} fusion(f32[1536,512,2]{1,0,2:T(8,128)S(1)} %get-tuple-element.23, f32[2,512]{1,0:T(2,128)S(1)} %get-tuple-element.22, f32[2,512]{1,0:T(2,128)S(1)} %get-tuple-element.20, f32[1536,512,2]{1,0,2:T(8,128)S(1)} %get-tuple-element.21, pred[512,1536]{0,1:T(8,128)(4,1)S(1)} %copy-done.1, ...), kind=kOutput, calls=%fused_computation.32 | convolution fusion | flops 819462144 | bytes 15212544 | tf_op jit(solution)/shard_map/ngtk,knd->tngd/dot_general | solution.py:59
  193.1 5.6 %all-to-all-start.2 = ((bf16[64,16,512]{2,1,0:T(8,128)(2,1)}), bf16[64,16,512]{2,1,0:T(8,128)(2,1)S(1)}, u32[]{:S(2)}, u32[]{:S(2)}) async-start(bf16[64,16,512]{2,1,0:T(8,128)(2,1)} %bitcast.150), calls=%async_computation.2 | async-start | bytes 2097152 | tf_op jit(solution)/shard_map/all_to_all | solution.py:169
  198.7 10.3 %all-gather = bf16[256,4,64]{2,0,1:T(8,128)(2,1)S(1)} all-gather(bf16[64,4,64]{2,0,1:T(8,128)(2,1)S(1)} %copy-done.7), channel_id=2, replica_groups=mesh['seq'=64,'tensor'=4] {'tensor'}, dimensions={0}, use_global_device_ids=true | all-gather | bytes 163840 | tf_op jit(solution)/shard_map/all_gather | solution.py:168
  208.9 6.0 %fusion.32 = bf16[256,2,512]{2,0,1:T(8,128)(2,1)} fusion(f32[2,512]{1,0:T(2,128)S(1)} %get-tuple-element.20, f32[1536,512,2]{1,0,2:T(8,128)} %copy-done.22, pred[512,1536]{0,1:T(8,128)(4,1)} %fusion.16, bf16[512,1,256]{2,0,1:T(8,128)(2,1)} %fusion.35, bf16[512,1,256]{2,0,1:T(8,128)(2,1)} %collective-permute-done.1, ...), kind=kOutput, calls=%fused_computation.36 | convolution fusion | flops 814219264 | bytes 8392704 | tf_op jit(solution)/shard_map/ngtk,knd->tngd/dot_general | solution.py:55
  217.0 10.2 %all-to-all-done.2 = bf16[64,16,512]{2,1,0:T(8,128)(2,1)S(1)} async-done(((bf16[64,16,512]{2,1,0:T(8,128)(2,1)}), bf16[64,16,512]{2,1,0:T(8,128)(2,1)S(1)}, u32[]{:S(2)}, u32[]{:S(2)}) %all-to-all-start.2) | async-done | bytes 1048608 | tf_op jit(solution)/shard_map/all_to_all | solution.py:169
  (97 shorter events, 29.7 us)
Async XLA Ops:
  7.2 143.7 %copy-start = (bf16[3840,256]{1,0:T(8,128)(2,1)S(1)}, bf16[3840,256]{1,0:T(8,128)(2,1)}, u32[]{:S(2)}) copy-start(bf16[3840,256]{1,0:T(8,128)(2,1)} %param.13) | copy-start | bytes 5898244
  7.2 130.9 %all-gather.3.cloned.1.call-start = ((), (), s32[]{:S(2)}) async-start(), calls=%async_computation.3 | async-start | bytes 4915200 | tf_op jit(solution)/shard_map/all_gather | solution.py:84
  19.8 20.8 %copy-start.14 = (s32[512]{0:T(512)S(1)}, s32[512]{0:T(512)}, u32[]{:S(2)}) copy-start(s32[512]{0:T(512)} %param.20) | copy-start | bytes 6148
  24.0 24.0 %copy-start.8 = (bf16[1,64,960]{2,1,0:T(8,128)(2,1)S(1)}, bf16[1,64,960]{2,1,0:T(8,128)(2,1)}, u32[]{:S(2)}) copy-start(bf16[1,64,960]{2,1,0:T(8,128)(2,1)} %param.17) | copy-start | bytes 368644
  24.0 77.3 %copy-start.9 = (bf16[1,64,512]{2,1,0:T(8,128)(2,1)S(1)}, bf16[1,64,512]{2,1,0:T(8,128)(2,1)}, u32[]{:S(2)}) copy-start(bf16[1,64,512]{2,1,0:T(8,128)(2,1)} %param.18) | copy-start | bytes 196612
  24.0 89.5 %all-to-all-start = ((bf16[256,4,960]{2,1,0:T(4,128)(2,1)}), bf16[256,4,960]{2,1,0:T(4,128)(2,1)}, u32[]{:S(2)}, u32[]{:S(2)}) async-start(bf16[256,4,960]{2,1,0:T(4,128)(2,1)} %all_to_all.20), calls=%async_computation | async-start | bytes 4194304 | tf_op jit(solution)/shard_map/all_to_all | solution.py:107
  40.7 72.8 %collective-permute-start.2 = (s32[512]{0:T(512)S(1)}, s32[512]{0:T(512)S(1)}, u32[]{:S(2)}, u32[]{:S(2)}) collective-permute-start(s32[512]{0:T(512)S(1)} %copy-done.14), channel_id=1, source_target_pairs={{0,8},{4,12},{8,16},{12,20},{16,24},{20,28},{24,32},{28,36},{32,40... | collective-permute-start | bytes 6152 | tf_op jit(solution)/shard_map/ppermute | solution.py:18
  44.1 69.4 %collective-permute-start.3 = (s32[512]{0:T(512)S(1)}, s32[512]{0:T(512)S(1)}, u32[]{:S(2)}, u32[]{:S(2)}) collective-permute-start(s32[512]{0:T(512)S(1)} %copy-done.14), channel_id=1, source_target_pairs={{0,4},{4,8},{8,12},{12,16},{16,20},{20,24},{24,28},{28,32},{32,36}... | collective-permute-start | bytes 6152 | tf_op jit(solution)/shard_map/ppermute | solution.py:18
  48.8 52.5 %copy-start.17 = (f32[128]{0:T(128)}, f32[128]{0:T(128)S(1)}, u32[]{:S(2)}) copy-start(f32[128]{0:T(128)S(1)} %multiply_exponential_fusion) | copy-start | bytes 1540
  48.8 52.5 %copy-start.10 = (s32[512]{0:T(512)}, s32[512]{0:T(512)S(1)}, u32[]{:S(2)}) copy-start(s32[512]{0:T(512)S(1)} %iota_add_fusion) | copy-start | bytes 6148
  48.8 52.5 %copy-start.11 = (f32[512]{0:T(512)}, f32[512]{0:T(512)S(1)}, u32[]{:S(2)}) copy-start(f32[512]{0:T(512)S(1)} %fusion.69) | copy-start | bytes 6148
  120.1 46.6 %all-to-all-start.1 = ((bf16[256,4,512]{2,1,0:T(4,128)(2,1)}), bf16[256,4,512]{2,1,0:T(4,128)(2,1)S(1)}, u32[]{:S(2)}, u32[]{:S(2)}) async-start(bf16[256,4,512]{2,1,0:T(4,128)(2,1)} %bitcast.148), calls=%async_computation.1 | async-start | bytes 2097152 | tf_op jit(solution)/shard_map/all_to_all | solution.py:116
  138.1 12.7 %copy-start.20 = (bf16[512,3840]{0,1:T(8,128)(2,1)S(1)}, bf16[512,3840]{0,1:T(8,128)(2,1)}, u32[]{:S(2)}) copy-start(bf16[512,3840]{0,1:T(8,128)(2,1)} %all-gather.3.cloned.1.call-done) | copy-start | bytes 11796484
  143.0 9.1 %copy-start.19 = (f32[256]{0:T(256)S(1)}, f32[256]{0:T(256)}, u32[]{:S(2)}) copy-start(f32[256]{0:T(256)} %param.16) | copy-start | bytes 3076
  143.0 9.3 %copy-start.12 = (f32[512]{0:T(512)S(1)}, f32[512]{0:T(512)}, u32[]{:S(2)}) copy-start(f32[512]{0:T(512)} %copy-done.11) | copy-start | bytes 6148
  143.0 9.3 %copy-start.18 = (f32[128]{0:T(128)S(1)}, f32[128]{0:T(128)}, u32[]{:S(2)}) copy-start(f32[128]{0:T(128)} %copy-done.17) | copy-start | bytes 1540
  143.0 39.3 %collective-permute-start.1 = (bf16[512,1,256]{2,0,1:T(8,128)(2,1)}, bf16[512,1,256]{2,0,1:T(8,128)(2,1)}, u32[]{:S(2)}, u32[]{:S(2)}) collective-permute-start(bf16[512,1,256]{2,0,1:T(8,128)(2,1)} %fusion.35), channel_id=1, source_target_pairs={{0,4},{4,8},{8,12},{12,16},{16,20},{20,24},{24,28},{28,32},{32,36}... | collective-permute-start | bytes 786440 | tf_op jit(solution)/shard_map/ppermute | solution.py:18
  146.8 35.5 %collective-permute-start = (bf16[512,1,256]{2,0,1:T(8,128)(2,1)}, bf16[512,1,256]{2,0,1:T(8,128)(2,1)}, u32[]{:S(2)}, u32[]{:S(2)}) collective-permute-start(bf16[512,1,256]{2,0,1:T(8,128)(2,1)} %fusion.35), channel_id=1, source_target_pairs={{0,8},{4,12},{8,16},{12,20},{16,24},{20,28},{24,32},{28,36},{32,40... | collective-permute-start | bytes 786440 | tf_op jit(solution)/shard_map/ppermute | solution.py:18
  152.1 15.7 %copy-start.16 = (s32[512]{0:T(512)S(1)}, s32[512]{0:T(512)}, u32[]{:S(2)}) copy-start(s32[512]{0:T(512)} %copy-done.15) | copy-start | bytes 6148
  154.2 24.2 %collective-permute-start.5 = (bf16[512,1,256]{0,2,1:T(8,128)(2,1)}, bf16[512,1,256]{0,2,1:T(8,128)(2,1)}, u32[]{:S(2)}, u32[]{:S(2)}) collective-permute-start(bf16[512,1,256]{0,2,1:T(8,128)(2,1)} %pad_maximum_fusion), channel_id=1, source_target_pairs={{0,4},{4,8},{8,12},{12,16},{16,20},{20,24},{24,28},{28,32},{32,36}... | collective-permute-start | bytes 786440 | tf_op jit(solution)/shard_map/ppermute | solution.py:18
  156.1 22.2 %collective-permute-start.4 = (bf16[512,1,256]{0,2,1:T(8,128)(2,1)}, bf16[512,1,256]{0,2,1:T(8,128)(2,1)}, u32[]{:S(2)}, u32[]{:S(2)}) collective-permute-start(bf16[512,1,256]{0,2,1:T(8,128)(2,1)} %pad_maximum_fusion), channel_id=1, source_target_pairs={{0,8},{4,12},{8,16},{12,20},{16,24},{20,28},{24,32},{28,36},{32,40... | collective-permute-start | bytes 786440 | tf_op jit(solution)/shard_map/ppermute | solution.py:18
  169.8 8.2 %copy-start.13 = (f32[256]{0:T(256)S(1)}, f32[256]{0:T(256)}, u32[]{:S(2)}) copy-start(f32[256]{0:T(256)} %param.15) | copy-start | bytes 3076
  191.3 7.3 %copy-start.7 = (bf16[64,4,64]{2,0,1:T(8,128)(2,1)S(1)}, bf16[64,4,64]{2,0,1:T(8,128)(2,1)}, u32[]{:S(2)}) copy-start(bf16[64,4,64]{2,0,1:T(8,128)(2,1)} %copy-done.6) | copy-start | bytes 98308
  193.1 34.1 %all-to-all-start.2 = ((bf16[64,16,512]{2,1,0:T(8,128)(2,1)}), bf16[64,16,512]{2,1,0:T(8,128)(2,1)S(1)}, u32[]{:S(2)}, u32[]{:S(2)}) async-start(bf16[64,16,512]{2,1,0:T(8,128)(2,1)} %bitcast.150), calls=%async_computation.2 | async-start | bytes 2097152 | tf_op jit(solution)/shard_map/all_to_all | solution.py:169
  (9 other events, 19.1 us)
Sparse Core Ops, SparseCore 0:
  9.8 89.1 all-gather.2

commit v3 on v1

--- a/solution.py
+++ b/solution.py
@@ -3,13 +3,14 @@
 import jax
 import jax.numpy as jnp
 from jax import lax
-from jax.sharding import PartitionSpec as P
+from jax.sharding import Mesh, PartitionSpec as P
 
 HD = 256
 R = 64
 WINDOW = 1024
 ADAPTERS = 64
 CAP = 16
+SEQ = ("sy", "szc")
 
 
 def passed_along(value, axis, steps):
@@ -80,7 +81,10 @@
     local_heads = q_width // HD
     kv_heads = kv_width // HD
     head_group = local_heads // kv_heads
-    positions = lax.axis_index("seq") * tok_count + jnp.arange(tok_count, dtype=jnp.int32)
+    zc_count = lax.axis_size("szc")
+    y_count = lax.axis_size("sy")
+    seq_index = lax.axis_index("sy") * zc_count + lax.axis_index("szc")
+    positions = seq_index * tok_count + jnp.arange(tok_count, dtype=jnp.int32)
     shard_cols = lax.all_gather(tokens, "tensor", axis=1, tiled=True)
     query_lin = jnp.dot(shard_cols, w_query, preferred_element_type=jnp.float32)
     key_lin = jnp.dot(shard_cols, w_key, preferred_element_type=jnp.float32)
@@ -89,25 +93,25 @@
     chosen = token_adapter[:, None] == jnp.arange(ADAPTERS, dtype=jnp.int32)[None, :]
     before = jnp.cumsum(chosen.astype(jnp.int32), axis=0) - 1
     slot_rank = jnp.sum(jnp.where(chosen, before, 0), axis=1)
-    slot_index = token_adapter * CAP + slot_rank
+    slot_index = ((token_adapter % zc_count) * y_count + token_adapter // zc_count) * CAP + slot_rank
     dispatch = (slot_index[None, :] == jnp.arange(ADAPTERS * CAP, dtype=jnp.int32)[:, None]).astype(
         jnp.bfloat16
     )
     outgoing = jnp.dot(dispatch, tokens, preferred_element_type=jnp.float32).astype(jnp.bfloat16)
-    seq_count = lax.axis_size("seq")
-    own_adapters = adapter_down.shape[0]
-    arrived = lax.all_to_all(outgoing, "seq", 0, 0, tiled=True).reshape(
-        seq_count, own_adapters, CAP, feat_width
+    column_down = lax.all_gather(adapter_down[0], "sy", axis=0)
+    column_up = lax.all_gather(adapter_up[0], "sy", axis=0)
+    arrived = lax.all_to_all(outgoing, "szc", 0, 0, tiled=True).reshape(
+        zc_count, y_count, CAP, feat_width
     )
     partial_low = jnp.einsum(
-        "sacd,ard->sacr", arrived, adapter_down, preferred_element_type=jnp.float32
+        "sycd,yrd->sycr", arrived, column_down, preferred_element_type=jnp.float32
     )
     slot_low = lax.psum(partial_low, "tensor").astype(jnp.bfloat16)
     slot_lift = jnp.einsum(
-        "sacr,are->sace", slot_low, adapter_up, preferred_element_type=jnp.float32
+        "sycr,yre->syce", slot_low, column_up, preferred_element_type=jnp.float32
     ).astype(jnp.bfloat16)
     back_lift = lax.all_to_all(
-        slot_lift.reshape(seq_count * own_adapters * CAP, q_width), "seq", 0, 0, tiled=True
+        slot_lift.reshape(zc_count * y_count * CAP, q_width), "szc", 0, 0, tiled=True
     )
     lifted = jnp.einsum(
         "st,se->te",
@@ -130,7 +134,7 @@
     doc_list = []
     place_list = []
     for distance in range(rim_count, 0, -1):
-        far_keys, far_values, far_docs = passed_along((key_rows, values, doc_ids), "seq", distance)
+        far_keys, far_values, far_docs = passed_along((key_rows, values, doc_ids), SEQ, distance)
         key_list.append(far_keys)
         value_list.append(far_values)
         doc_list.append(far_docs)
@@ -158,28 +162,34 @@
     out_grad = jnp.dot(dispatch, dquery_pre, preferred_element_type=jnp.float32).astype(
         jnp.bfloat16
     )
-    grad_rows = lax.all_to_all(out_grad, "seq", 0, 0, tiled=True).reshape(
-        seq_count, own_adapters, CAP, q_width
+    grad_rows = lax.all_to_all(out_grad, "szc", 0, 0, tiled=True).reshape(
+        zc_count, y_count, CAP, q_width
     )
-    grad_up = jnp.einsum(
-        "sacr,sace->are", slot_low, grad_rows, preferred_element_type=jnp.float32
+    column_grad = jnp.einsum(
+        "sycr,syce->yre", slot_low, grad_rows, preferred_element_type=jnp.float32
     )
+    grad_up = lax.psum_scatter(column_grad, "sy", scatter_dimension=0, tiled=True)
     return (attended, grad_up)
 
 
 def solution(mesh):
+    seq_size = mesh.shape["seq"]
+    zc_size = seq_size // 4
+    fine = Mesh(
+        mesh.devices.reshape(4, zc_size, mesh.shape["tensor"]), ("sy", "szc", "tensor")
+    )
     in_specs = (
-        P("seq", "tensor"),
+        P(SEQ, "tensor"),
         P(None, "tensor"),
         P(None, "tensor"),
         P(None, "tensor"),
         P(),
         P(),
-        P("seq", None, "tensor"),
-        P("seq", None, "tensor"),
-        P("seq", None),
-        P("seq"),
-        P("seq", "tensor"),
+        P(SEQ, None, "tensor"),
+        P(SEQ, None, "tensor"),
+        P(SEQ, None),
+        P(SEQ),
+        P(SEQ, "tensor"),
     )
-    out_specs = (P("seq", "tensor"), P("seq", None, "tensor"))
-    return jax.shard_map(local, mesh=mesh, in_specs=in_specs, out_specs=out_specs, check_vma=False)
+    out_specs = (P(SEQ, "tensor"), P(SEQ, None, "tensor"))
+    return jax.shard_map(local, mesh=fine, in_specs=in_specs, out_specs=out_specs, check_vma=False)

time: 220 us -> 246 us (1.12)
  blocking collectives: 18.4 us -> 78.4 us
  starting transfers between devices: 54.5 us -> 38.4 us
  waiting for transfers between devices: 67.7 us -> 53.6 us
  matrix products: 40.7 us -> 35.6 us
    all_to_all x0 -> x1, blocking collectives: none -> 36.7 us  [local(): lax.all_to_all(out_grad, 'szc', 0, 0, tiled=True)]
    all_gather x0 -> x2, blocking collectives: none -> 22.7 us  [the longest x1 11.6 us: local(): column_down = lax.all_gather(adapter_down[0], 'sy', axis=0)]
    ppermute x6, waiting for transfers between devices: 33 us -> 13.6 us  [passed_along(): lax.ppermute(value, axis, [(source, source + steps) for source in range(f...]
    all_to_all x3 -> x2, starting transfers between devices: 34.6 us -> 18.9 us  [the longest x1 10.1 us: local(): lax.all_to_all(outgoing, 'szc', 0, 0, tiled=True)]
    reduce_scatter x0 -> x1, waiting for transfers between devices: none -> 11.2 us  [local(): lax.psum_scatter(column_grad, 'sy', scatter_dimension=0, tiled=True)]
    all_to_all x3 -> x2, waiting for transfers between devices: 33.9 us -> 28.1 us  [the longest x1 25.7 us: local(): lax.all_to_all(outgoing, 'szc', 0, 0, tiled=True)]
    dot_general x1, matrix products: 6.53 us -> 3.22 us  [local(): query_lin = jnp.dot(shard_cols, w_query, preferred_element_type=jnp.float32)]
  transfers between devices with their start and end apart: 10 -> 10, of which waited for: 6 -> 5; matrix products, arithmetic and copies ran while one was open for 23% -> 12% of each run, Pallas kernels for 0% -> 0%
where the time goes in v3:
time: 246 us; the launch traced here: 244 us
  blocking collectives  78.4 us (32%)
  waiting for transfers between devices  53.6 us (22%)
  starting transfers between devices  38.4 us (16%)
  matrix products  35.6 us (14%)
  between operations  14.5 us (6%)
  other arithmetic  13.5 us (5%)
  local copies, waits for them, and re-layouts  9.74 us (4%)
    all_to_all x1, blocking collectives, local(): lax.all_to_all(out_grad, 'szc', 0, 0, tiled=True)  36.7 us
    all_to_all x1, waiting for transfers between devices, local(): lax.all_to_all(outgoing, 'szc', 0, 0, tiled=True)  25.7 us
    ppermute x6, starting transfers between devices, passed_along(): lax.ppermute(value, axis, [(source, source + steps) for source in range(f...  19.4 us
    psum x1, blocking collectives, local(): slot_low = lax.psum(partial_low, 'tensor').astype(jnp.bfloat16)  19.1 us
    ppermute x6, waiting for transfers between devices, passed_along(): lax.ppermute(value, axis, [(source, source + steps) for source in range(f...  13.6 us
    all_gather x1, blocking collectives, local(): column_down = lax.all_gather(adapter_down[0], 'sy', axis=0)  11.6 us
    reduce_scatter x1, waiting for transfers between devices, local(): lax.psum_scatter(column_grad, 'sy', scatter_dimension=0, tiled=True)  11.2 us
    all_gather x1, blocking collectives, local(): column_up = lax.all_gather(adapter_up[0], 'sy', axis=0)  11.1 us
  transfers between devices with their start and end apart: 10, of which 5 were waited for; matrix products, arithmetic and copies ran while one was open for 12% of the time, Pallas kernels for 0%

profile of v3, /device:TPU:1, one launch (start us, length us, event | category | flops | bytes accessed | tf_op | source)
XLA Modules:
  0.0 243.7 jit_solution(12141992711496944133)
XLA Ops:
  11.0 3.7 %fusion.24 = bf16[1024,960]{0,1:T(8,128)(2,1)} fusion(bf16[512,960]{0,1:T(8,128)(2,1)} %param.11, s32[512]{0:T(512)S(1)} %fusion.70), kind=kOutput, calls=%fused_computation.27 | convolution fusion | flops 1008140288 | bytes 2951168 | tf_op jit(solution)/shard_map/dot_general | solution.py:100
  14.7 3.9 %copy.58 = bf16[1024,960]{1,0:T(8,128)(2,1)} copy(bf16[1024,960]{0,1:T(8,128)(2,1)} %fusion.24) | data formatting | bytes 3932160 | tf_op jit(solution)/shard_map/convert_element_type | solution.py:100
  18.6 10.1 %all-to-all-start = ((bf16[16,64,960]{2,1,0:T(8,128)(2,1)}), bf16[16,64,960]{2,1,0:T(8,128)(2,1)}, u32[]{:S(2)}, u32[]{:S(2)}) async-start(bf16[16,64,960]{2,1,0:T(8,128)(2,1)} %bitcast.141), calls=%async_computation | async-start | bytes 4194304 | tf_op jit(solution)/shard_map/all_to_all | solution.py:103
  29.5 11.1 %all_gather.11 = bf16[4,64,512]{2,1,0:T(8,128)(2,1)S(1)} all-gather(bf16[1,64,512]{2,1,0:T(8,128)(2,1)S(1)} %copy-done.9), channel_id=1, replica_groups=mesh['sy'=4,'szc'=16,'tensor'=4] {'sy'}, dimensions={0}, use_global_device_ids=true | all-gather | bytes 327680 | tf_op jit(solution)/shard_map/all_gather | solution.py:102
  40.6 11.6 %all_gather.10 = bf16[4,64,960]{2,1,0:T(8,128)(2,1)S(1)} all-gather(bf16[1,64,960]{2,1,0:T(8,128)(2,1)S(1)} %copy-done.8), channel_id=1, replica_groups=mesh['sy'=4,'szc'=16,'tensor'=4] {'sy'}, dimensions={0}, use_global_device_ids=true | all-gather | bytes 614400 | tf_op jit(solution)/shard_map/all_gather | solution.py:101
  52.2 25.7 %all-to-all-done = bf16[16,64,960]{2,1,0:T(8,128)(2,1)} async-done(((bf16[16,64,960]{2,1,0:T(8,128)(2,1)}), bf16[16,64,960]{2,1,0:T(8,128)(2,1)}, u32[]{:S(2)}, u32[]{:S(2)}) %all-to-all-start) | async-done | bytes 1966112 | tf_op jit(solution)/shard_map/all_to_all | solution.py:103
  80.2 19.1 %all-reduce.3 = bf16[16,4,16,64]{3,2,0,1:T(8,128)(2,1)S(1)} all-reduce(f32[16,4,16,64]{3,2,0,1:T(8,128)S(1)} %fusion.35), channel_id=1, replica_groups=mesh['sy'=4,'szc'=16,'tensor'=4] {'tensor'}, use_global_device_ids=true, to_apply=%region_4.5 | all-reduce | flops 65536 | bytes 393216 | tf_op jit(solution)/shard_map/psum | solution.py:109
  100.8 8.8 %all-to-all-start.1 = ((bf16[16,64,512]{2,1,0:T(8,128)(2,1)}), bf16[16,64,512]{2,1,0:T(8,128)(2,1)S(1)}, u32[]{:S(2)}, u32[]{:S(2)}) async-start(bf16[16,64,512]{2,1,0:T(8,128)(2,1)} %bitcast.17), calls=%async_computation.1 | async-start | bytes 2097152 | tf_op jit(solution)/shard_map/all_to_all | solution.py:113
  109.6 3.3 %collective-permute-start.2 = (s32[512]{0:T(512)S(1)}, s32[512]{0:T(512)S(1)}, u32[]{:S(2)}, u32[]{:S(2)}) collective-permute-start(s32[512]{0:T(512)S(1)} %copy-done.11), channel_id=1, source_target_pairs={{0,8},{4,12},{8,16},{12,20},{16,24},{20,28},{24,32},{28,36},{32,40... | collective-permute-start | bytes 6152 | tf_op jit(solution)/shard_map/ppermute | solution.py:19
  112.9 3.7 %collective-permute-start.3 = (s32[512]{0:T(512)S(1)}, s32[512]{0:T(512)}, u32[]{:S(2)}, u32[]{:S(2)}) collective-permute-start(s32[512]{0:T(512)S(1)} %copy-done.11), channel_id=1, source_target_pairs={{0,4},{4,8},{8,12},{12,16},{16,20},{20,24},{24,28},{28,32},{32,36}... | collective-permute-start | bytes 6152 | tf_op jit(solution)/shard_map/ppermute | solution.py:19
  118.4 13.5 %collective-permute-done.2 = s32[512]{0:T(512)S(1)} collective-permute-done((s32[512]{0:T(512)S(1)}, s32[512]{0:T(512)S(1)}, u32[]{:S(2)}, u32[]{:S(2)}) %collective-permute-start.2) | collective-permute-done | bytes 2080 | tf_op jit(solution)/shard_map/ppermute | solution.py:19
  132.7 2.5 %fusion.16 = pred[512,1536]{0,1:T(8,128)(4,1)} fusion(s32[1536]{0:T(1024)S(1)} %pad_add_fusion.1, s32[512]{0:T(512)S(1)} %iota_add_fusion, s32[512]{0:T(512)S(1)} %copy-done.11, s32[1536]{0:T(1024)S(1)} %pad_add_fusion, pred[1536]{0:T(1024)(128)(4,1)S(1)} %broadcast_compare_fusion), kind=kLoop, calls=%fused_computation.20 | loop fusion | flops 5505024 | bytes 804352 | tf_op jit(solution)/shard_map/and | solution.py:152
  135.2 2.4 all-to-all-done.1
  139.3 4.8 %fusion.38 = bf16[512,1,256]{2,0,1:T(8,128)(2,1)} fusion(bf16[512,3840]{0,1:T(8,128)(2,1)} %all-gather.2.cloned.1.call-done, bf16[3840,256]{1,0:T(8,128)(2,1)} %param.14), kind=kOutput, calls=%fused_computation.40 | convolution fusion | flops 1006764032 | bytes 6160384 | tf_op jit(solution)/shard_map/dot_general | solution.py:91
  144.2 2.7 %collective-permute-start.1 = (bf16[512,1,256]{2,0,1:T(8,128)(2,1)}, bf16[512,1,256]{2,0,1:T(8,128)(2,1)}, u32[]{:S(2)}, u32[]{:S(2)}) collective-permute-start(bf16[512,1,256]{2,0,1:T(8,128)(2,1)} %fusion.38), channel_id=1, source_target_pairs={{0,4},{4,8},{8,12},{12,16},{16,20},{20,24},{24,28},{28,32},{32,36}... | collective-permute-start | bytes 786440 | tf_op jit(solution)/shard_map/ppermute | solution.py:19
  146.9 3.9 %collective-permute-start = (bf16[512,1,256]{2,0,1:T(8,128)(2,1)}, bf16[512,1,256]{2,0,1:T(8,128)(2,1)}, u32[]{:S(2)}, u32[]{:S(2)}) collective-permute-start(bf16[512,1,256]{2,0,1:T(8,128)(2,1)} %fusion.38), channel_id=1, source_target_pairs={{0,8},{4,12},{8,16},{12,20},{16,24},{20,28},{24,32},{28,36},{32,40... | collective-permute-start | bytes 786440 | tf_op jit(solution)/shard_map/ppermute | solution.py:19
  156.7 3.8 %collective-permute-start.4 = (bf16[512,1,256]{0,2,1:T(8,128)(2,1)}, bf16[512,1,256]{0,2,1:T(8,128)(2,1)}, u32[]{:S(2)}, u32[]{:S(2)}) collective-permute-start(bf16[512,1,256]{0,2,1:T(8,128)(2,1)} %pad_maximum_fusion), channel_id=1, source_target_pairs={{0,8},{4,12},{8,16},{12,20},{16,24},{20,28},{24,32},{28,36},{32,40... | collective-permute-start | bytes 786440 | tf_op jit(solution)/shard_map/ppermute | solution.py:19
  160.6 3.2 %multiply_reduce_fusion.1 = (f32[512,2]{0,1:T(2,128)S(1)}, f32[512,512]{0,1:T(8,128)}) fusion(f32[512,512]{0,1:T(8,128)S(1)} %copy-done.18, bf16[512,3840]{0,1:T(8,128)(2,1)S(1)} %copy-done.16, bf16[3840,512]{1,0:T(8,128)(2,1)S(1)} %copy-done.15), kind=kOutput, calls=%fused_computation.46 | convolution fusion | flops 2014051328 | bytes 9965568 | tf_op jit(solution)/shard_map/dot_general | solution.py:89
  166.8 3.1 %fusion.5 = (f32[2,512]{1,0:T(2,128)S(1)}, f32[1536,512,2]{1,0,2:T(8,128)S(1)}) fusion(pred[512,1536]{0,1:T(8,128)(4,1)S(1)} %copy-done.2, bf16[512,2,128]{2,0,1:T(8,128)(2,1)S(1)} %get-tuple-element.13, bf16[512,2,128]{2,0,1:T(8,128)(2,1)S(1)} %get-tuple-element.12, bf16[512,1,128]{0,2,1:T(8,128)(2,1)S(1)} %copy-done.7, ...), kind=kOutput, calls=%fused_computation.8 | convolution fusion | flops 814218240 | bytes 8392704 | tf_op jit(solution)/shard_map/tngd,knd->ngtk/dot_general | solution.py:50
  170.0 4.2 %fusion = (f32[2,512]{1,0:T(2,128)S(1)}, f32[1536,512,2]{1,0,2:T(8,128)S(1)}) fusion(f32[2,512]{1,0:T(2,128)S(1)} %get-tuple-element.22, f32[1536,512,2]{1,0,2:T(8,128)S(1)} %get-tuple-element.23, pred[512,1536]{0,1:T(8,128)(4,1)S(1)} %copy-done.2, bf16[64,2,8,256]{3,2,1,0:T(8,128)(2,1)S(1)} %bitcast.151, bf16[512,1,256]{2,0,1:T(8,128)(2,1)} %fusion.38, ...), kind=kOutput, calls=%fused_computation.3 | convolution fusion | flops 815528960 | bytes 14688256 | tf_op jit(solution)/shard_map/tngd,knd->ngtk/dot_general | solution.py:57
  174.2 3.8 %fusion.27 = f32[512,2,256]{2,0,1:T(8,128)S(1)} fusion(f32[1536,512,2]{1,0,2:T(8,128)S(1)} %get-tuple-element.25, f32[2,512]{1,0:T(2,128)S(1)} %get-tuple-element.24, f32[2,512]{1,0:T(2,128)S(1)} %get-tuple-element.22, f32[1536,512,2]{1,0,2:T(8,128)S(1)} %get-tuple-element.23, pred[512,1536]{0,1:T(8,128)(4,1)S(1)} %copy-done.2, ...), kind=kOutput, calls=%fused_computation.32 | convolution fusion | flops 819462144 | bytes 15212544 | tf_op jit(solution)/shard_map/ngtk,knd->tngd/dot_general | solution.py:60
  181.7 36.7 %all_to_all.30 = bf16[16,64,512]{2,1,0:T(8,128)(2,1)S(1)} all-to-all(bf16[16,64,512]{2,1,0:T(8,128)(2,1)S(1)} %bitcast.145), channel_id=1, replica_groups=mesh['sy'=4,'szc'=16,'tensor'=4] {'szc'}, dimensions={0} | all-to-all | bytes 2097152 | tf_op jit(solution)/shard_map/all_to_all | solution.py:165
  219.6 5.1 %fusion.32 = bf16[256,2,512]{2,0,1:T(8,128)(2,1)S(1)} fusion(f32[2,512]{1,0:T(2,128)S(1)} %get-tuple-element.22, f32[1536,512,2]{1,0,2:T(8,128)} %copy-done.19, pred[512,1536]{0,1:T(8,128)(4,1)S(1)} %copy-done.3, bf16[512,1,256]{2,0,1:T(8,128)(2,1)} %fusion.38, bf16[512,1,256]{2,0,1:T(8,128)(2,1)} %collective-permute-done.1, ...), kind=kOutput, calls=%fused_computation.36 | convolution fusion | flops 814219264 | bytes 8392704 | tf_op jit(solution)/shard_map/ngtk,knd->tngd/dot_general | solution.py:56
  225.7 11.2 %reduce-scatter.2.cloned.1.call-done = f32[1,64,512]{2,1,0:T(8,128)} async-done(((f32[4,64,512]{2,1,0:T(8,128)}), f32[1,64,512]{2,1,0:T(8,128)}) %reduce-scatter.2.cloned.1.call-update) | async-done | bytes 131088 | tf_op jit(solution)/shard_map/reduce_scatter | solution.py:171
  (87 shorter events, 27.3 us)
Async XLA Ops:
  7.2 143.6 %copy-start = (bf16[3840,256]{1,0:T(8,128)(2,1)S(1)}, bf16[3840,256]{1,0:T(8,128)(2,1)}, u32[]{:S(2)}) copy-start(bf16[3840,256]{1,0:T(8,128)(2,1)} %param.13) | copy-start | bytes 5898244
  18.6 10.8 %copy-start.9 = (bf16[1,64,512]{2,1,0:T(8,128)(2,1)S(1)}, bf16[1,64,512]{2,1,0:T(8,128)(2,1)}, u32[]{:S(2)}) copy-start(bf16[1,64,512]{2,1,0:T(8,128)(2,1)} %param.18) | copy-start | bytes 196612
  18.6 21.9 %copy-start.8 = (bf16[1,64,960]{2,1,0:T(8,128)(2,1)S(1)}, bf16[1,64,960]{2,1,0:T(8,128)(2,1)}, u32[]{:S(2)}) copy-start(bf16[1,64,960]{2,1,0:T(8,128)(2,1)} %param.17) | copy-start | bytes 368644
  18.6 59.3 %all-to-all-start = ((bf16[16,64,960]{2,1,0:T(8,128)(2,1)}), bf16[16,64,960]{2,1,0:T(8,128)(2,1)}, u32[]{:S(2)}, u32[]{:S(2)}) async-start(bf16[16,64,960]{2,1,0:T(8,128)(2,1)} %bitcast.141), calls=%async_computation | async-start | bytes 4194304 | tf_op jit(solution)/shard_map/all_to_all | solution.py:103
  28.8 110.6 %all-gather.2.cloned.1.call-start = ((), (), s32[]{:S(2)}) async-start(), calls=%async_computation.4 | async-start | bytes 4915200 | tf_op jit(solution)/shard_map/all_gather | solution.py:88
  80.2 29.4 %copy-start.11 = (s32[512]{0:T(512)S(1)}, s32[512]{0:T(512)}, u32[]{:S(2)}) copy-start(s32[512]{0:T(512)} %param.20) | copy-start | bytes 6148
  100.8 36.8 %all-to-all-start.1 = ((bf16[16,64,512]{2,1,0:T(8,128)(2,1)}), bf16[16,64,512]{2,1,0:T(8,128)(2,1)S(1)}, u32[]{:S(2)}, u32[]{:S(2)}) async-start(bf16[16,64,512]{2,1,0:T(8,128)(2,1)} %bitcast.17), calls=%async_computation.1 | async-start | bytes 2097152 | tf_op jit(solution)/shard_map/all_to_all | solution.py:113
  109.6 127.3 %reduce-scatter.2.cloned.1.call-start = ((), (), s32[]{:S(2)}) async-start(), calls=%async_computation.5 | async-start | bytes 655360 | tf_op jit(solution)/shard_map/reduce_scatter | solution.py:171
  109.6 22.3 %collective-permute-start.2 = (s32[512]{0:T(512)S(1)}, s32[512]{0:T(512)S(1)}, u32[]{:S(2)}, u32[]{:S(2)}) collective-permute-start(s32[512]{0:T(512)S(1)} %copy-done.11), channel_id=1, source_target_pairs={{0,8},{4,12},{8,16},{12,20},{16,24},{20,28},{24,32},{28,36},{32,40... | collective-permute-start | bytes 6152 | tf_op jit(solution)/shard_map/ppermute | solution.py:19
  112.9 19.1 %collective-permute-start.3 = (s32[512]{0:T(512)S(1)}, s32[512]{0:T(512)}, u32[]{:S(2)}, u32[]{:S(2)}) collective-permute-start(s32[512]{0:T(512)S(1)} %copy-done.11), channel_id=1, source_target_pairs={{0,4},{4,8},{8,12},{12,16},{16,20},{20,24},{24,28},{28,32},{32,36}... | collective-permute-start | bytes 6152 | tf_op jit(solution)/shard_map/ppermute | solution.py:19
  116.6 15.4 %copy-start.12 = (f32[128]{0:T(128)}, f32[128]{0:T(128)S(1)}, u32[]{:S(2)}) copy-start(f32[128]{0:T(128)S(1)} %multiply_exponential_fusion) | copy-start | bytes 1540
  139.3 11.4 %copy-start.16 = (bf16[512,3840]{0,1:T(8,128)(2,1)S(1)}, bf16[512,3840]{0,1:T(8,128)(2,1)}, u32[]{:S(2)}) copy-start(bf16[512,3840]{0,1:T(8,128)(2,1)} %all-gather.2.cloned.1.call-done) | copy-start | bytes 11796484
  144.1 7.9 %copy-start.14 = (f32[256]{0:T(256)S(1)}, f32[256]{0:T(256)}, u32[]{:S(2)}) copy-start(f32[256]{0:T(256)} %param.16) | copy-start | bytes 3076
  144.1 8.0 %copy-start.13 = (f32[128]{0:T(128)S(1)}, f32[128]{0:T(128)}, u32[]{:S(2)}) copy-start(f32[128]{0:T(128)} %copy-done.12) | copy-start | bytes 1540
  144.1 16.4 %copy-start.15 = (bf16[3840,512]{1,0:T(8,128)(2,1)S(1)}, bf16[3840,512]{1,0:T(8,128)(2,1)}, u32[]{:S(2)}) copy-start(bf16[3840,512]{1,0:T(8,128)(2,1)} %param.12) | copy-start | bytes 11796484
  144.2 16.4 %copy-start.18 = (f32[512,512]{0,1:T(8,128)S(1)}, f32[512,512]{0,1:T(8,128)}, u32[]{:S(2)}) copy-start(f32[512,512]{0,1:T(8,128)} %fusion.31) | copy-start | bytes 3145732
  144.2 25.8 %collective-permute-start.1 = (bf16[512,1,256]{2,0,1:T(8,128)(2,1)}, bf16[512,1,256]{2,0,1:T(8,128)(2,1)}, u32[]{:S(2)}, u32[]{:S(2)}) collective-permute-start(bf16[512,1,256]{2,0,1:T(8,128)(2,1)} %fusion.38), channel_id=1, source_target_pairs={{0,4},{4,8},{8,12},{12,16},{16,20},{20,24},{24,28},{28,32},{32,36}... | collective-permute-start | bytes 786440 | tf_op jit(solution)/shard_map/ppermute | solution.py:19
  146.9 23.1 %collective-permute-start = (bf16[512,1,256]{2,0,1:T(8,128)(2,1)}, bf16[512,1,256]{2,0,1:T(8,128)(2,1)}, u32[]{:S(2)}, u32[]{:S(2)}) collective-permute-start(bf16[512,1,256]{2,0,1:T(8,128)(2,1)} %fusion.38), channel_id=1, source_target_pairs={{0,8},{4,12},{8,16},{12,20},{16,24},{20,28},{24,32},{28,36},{32,40... | collective-permute-start | bytes 786440 | tf_op jit(solution)/shard_map/ppermute | solution.py:19
  154.7 10.7 %copy-start.10 = (f32[256]{0:T(256)S(1)}, f32[256]{0:T(256)}, u32[]{:S(2)}) copy-start(f32[256]{0:T(256)} %param.15) | copy-start | bytes 3076
  154.7 12.1 %collective-permute-start.5 = (bf16[512,1,256]{0,2,1:T(8,128)(2,1)}, bf16[512,1,256]{0,2,1:T(8,128)(2,1)}, u32[]{:S(2)}, u32[]{:S(2)}) collective-permute-start(bf16[512,1,256]{0,2,1:T(8,128)(2,1)} %pad_maximum_fusion), channel_id=1, source_target_pairs={{0,4},{4,8},{8,12},{12,16},{16,20},{20,24},{24,28},{28,32},{32,36}... | collective-permute-start | bytes 786440 | tf_op jit(solution)/shard_map/ppermute | solution.py:19
  156.7 10.0 %collective-permute-start.4 = (bf16[512,1,256]{0,2,1:T(8,128)(2,1)}, bf16[512,1,256]{0,2,1:T(8,128)(2,1)}, u32[]{:S(2)}, u32[]{:S(2)}) collective-permute-start(bf16[512,1,256]{0,2,1:T(8,128)(2,1)} %pad_maximum_fusion), channel_id=1, source_target_pairs={{0,8},{4,12},{8,16},{12,20},{16,24},{20,28},{24,32},{28,36},{32,40... | collective-permute-start | bytes 786440 | tf_op jit(solution)/shard_map/ppermute | solution.py:19
  170.0 4.2 %copy-start.19 = (f32[1536,512,2]{1,0,2:T(8,128)}, f32[1536,512,2]{1,0,2:T(8,128)S(1)}, u32[]{:S(2)}) copy-start(f32[1536,512,2]{1,0,2:T(8,128)S(1)} %get-tuple-element.23) | copy-start | bytes 18874372
  174.2 3.8 %copy-start.1 = (f32[512,128]{1,0:T(8,128)S(1)}, f32[512,128]{1,0:T(8,128)}, u32[]{:S(2)}) copy-start(f32[512,128]{1,0:T(8,128)} %get-tuple-element.17) | copy-start | bytes 786436
  180.9 38.6 %copy-start.3 = (pred[512,1536]{0,1:T(8,128)(4,1)S(1)}, pred[512,1536]{0,1:T(8,128)(4,1)}, u32[]{:S(2)}) copy-start(pred[512,1536]{0,1:T(8,128)(4,1)} %fusion.16) | copy-start | bytes 2359300
  (6 other events, 9.5 us)
Sparse Core Ops, SparseCore 0:
  31.4 49.4 all-gather.1
  219.7 17.1 reduce-scatter.1

commit v4 on v1

--- a/solution.py
+++ b/solution.py
@@ -103,16 +103,17 @@
         "sacd,ard->sacr", arrived, adapter_down, preferred_element_type=jnp.float32
     )
     slot_low = lax.psum(partial_low, "tensor").astype(jnp.bfloat16)
+    all_up = lax.all_gather(adapter_up, "seq", axis=0, tiled=True)
+    back_low = lax.all_to_all(
+        slot_low.reshape(seq_count * own_adapters * CAP, R), "seq", 0, 0, tiled=True
+    ).reshape(ADAPTERS, CAP, R)
     slot_lift = jnp.einsum(
-        "sacr,are->sace", slot_low, adapter_up, preferred_element_type=jnp.float32
+        "acr,are->ace", back_low, all_up, preferred_element_type=jnp.float32
     ).astype(jnp.bfloat16)
-    back_lift = lax.all_to_all(
-        slot_lift.reshape(seq_count * own_adapters * CAP, q_width), "seq", 0, 0, tiled=True
-    )
     lifted = jnp.einsum(
         "st,se->te",
         dispatch,
-        back_lift,
+        slot_lift.reshape(ADAPTERS * CAP, q_width),
         preferred_element_type=jnp.float32,
     ).astype(jnp.bfloat16)
     query_pre = (query_lin + lifted.astype(jnp.float32)).reshape(tok_count, local_heads, HD)

time: 220 us -> 220 us (level)
  starting transfers between devices: 54.5 us -> 49.3 us
  waiting for transfers between devices: 67.7 us -> 72.9 us
  local copies, waits for them, and re-layouts: 9.09 us -> 11.5 us
    all_to_all x1, waiting for transfers between devices: 4.25 us -> 8.53 us  [local(): lax.all_to_all(slot_low.reshape(seq_count * own_adapters * CAP, R), 'seq'...]
    dot_general x1, matrix products: 6.53 us -> 3.22 us  [local(): query_lin = jnp.dot(shard_cols, w_query, preferred_element_type=jnp.float32)]
    all_to_all x1, starting transfers between devices: 10.8 us -> 7.72 us  [local(): lax.all_to_all(out_grad, 'seq', 0, 0, tiled=True)]
    unnamed x45 -> x35, local copies, waits for them, and re-layouts: 2.15 us -> 4.56 us
  transfers between devices with their start and end apart: 10 -> 11, of which waited for: 6 -> 5; matrix products, arithmetic and copies ran while one was open for 23% -> 22% of each run, Pallas kernels for 0% -> 0%
where the time goes in v4:
time: 220 us; the launch traced here: 219 us
  waiting for transfers between devices  72.9 us (33%)
  starting transfers between devices  49.3 us (22%)
  matrix products  39 us (18%)
  blocking collectives  18.9 us (9%)
  between operations  14.5 us (7%)
  other arithmetic  12.7 us (6%)
  local copies, waits for them, and re-layouts  11.5 us (5%)
    ppermute x6, waiting for transfers between devices, passed_along(): lax.ppermute(value, axis, [(source, source + steps) for source in range(f...  33.2 us
    all_to_all x1, waiting for transfers between devices, local(): lax.all_to_all(out_grad, 'seq', 0, 0, tiled=True)  20.5 us
    psum x1, blocking collectives, local(): slot_low = lax.psum(partial_low, 'tensor').astype(jnp.bfloat16)  18.9 us
    ppermute x6, starting transfers between devices, passed_along(): lax.ppermute(value, axis, [(source, source + steps) for source in range(f...  18.2 us
    all_to_all x1, starting transfers between devices, local(): lax.all_to_all(outgoing, 'seq', 0, 0, tiled=True)  13.3 us
    all_to_all x1, starting transfers between devices, local(): lax.all_to_all(slot_low.reshape(seq_count * own_adapters * CAP, R), 'seq'...  9.9 us
    all_to_all x1, waiting for transfers between devices, local(): lax.all_to_all(outgoing, 'seq', 0, 0, tiled=True)  9.25 us
    all_to_all x1, waiting for transfers between devices, local(): lax.all_to_all(slot_low.reshape(seq_count * own_adapters * CAP, R), 'seq'...  8.53 us
  transfers between devices with their start and end apart: 11, of which 5 were waited for; matrix products, arithmetic and copies ran while one was open for 22% of the time, Pallas kernels for 0%

profile of v4, /device:TPU:1, one launch (start us, length us, event | category | flops | bytes accessed | tf_op | source)
XLA Modules:
  0.0 218.7 jit_solution(9688779733499012605)
XLA Ops:
  12.3 3.7 %fusion.22 = bf16[1024,960]{0,1:T(8,128)(2,1)} fusion(bf16[512,960]{0,1:T(8,128)(2,1)} %param.11, s32[512]{0:T(512)S(1)} %multiply_add_fusion.3), kind=kOutput, calls=%fused_computation.25 | convolution fusion | flops 1008140288 | bytes 2951168 | tf_op jit(solution)/shard_map/dot_general | solution.py:96
  16.0 3.9 %copy.42 = bf16[1024,960]{1,0:T(8,128)(2,1)} copy(bf16[1024,960]{0,1:T(8,128)(2,1)} %fusion.22) | data formatting | bytes 3932160 | tf_op jit(solution)/shard_map/convert_element_type | solution.py:96
  20.0 13.3 %all-to-all-start = ((bf16[64,16,960]{2,1,0:T(8,128)(2,1)}), bf16[64,16,960]{2,1,0:T(8,128)(2,1)}, u32[]{:S(2)}, u32[]{:S(2)}) async-start(bf16[64,16,960]{2,1,0:T(8,128)(2,1)} %bitcast.141), calls=%async_computation | async-start | bytes 4194304 | tf_op jit(solution)/shard_map/all_to_all | solution.py:99
  33.3 3.3 %collective-permute-start.2 = (s32[512]{0:T(512)S(1)}, s32[512]{0:T(512)S(1)}, u32[]{:S(2)}, u32[]{:S(2)}) collective-permute-start(s32[512]{0:T(512)S(1)} %copy-done.9), channel_id=1, source_target_pairs={{0,8},{4,12},{8,16},{12,20},{16,24},{20,28},{24,32},{28,36},{32,40... | collective-permute-start | bytes 6152 | tf_op jit(solution)/shard_map/ppermute | solution.py:18
  36.6 3.7 %collective-permute-start.3 = (s32[512]{0:T(512)S(1)}, s32[512]{0:T(512)S(1)}, u32[]{:S(2)}, u32[]{:S(2)}) collective-permute-start(s32[512]{0:T(512)S(1)} %copy-done.9), channel_id=1, source_target_pairs={{0,4},{4,8},{8,12},{12,16},{16,20},{20,24},{24,28},{28,32},{32,36}... | collective-permute-start | bytes 6152 | tf_op jit(solution)/shard_map/ppermute | solution.py:18
  42.1 33.1 %collective-permute-done.2 = s32[512]{0:T(512)S(1)} collective-permute-done((s32[512]{0:T(512)S(1)}, s32[512]{0:T(512)S(1)}, u32[]{:S(2)}, u32[]{:S(2)}) %collective-permute-start.2) | collective-permute-done | bytes 2080 | tf_op jit(solution)/shard_map/ppermute | solution.py:18
  75.3 9.3 %all-to-all-done = bf16[64,16,960]{2,1,0:T(8,128)(2,1)} async-done(((bf16[64,16,960]{2,1,0:T(8,128)(2,1)}), bf16[64,16,960]{2,1,0:T(8,128)(2,1)}, u32[]{:S(2)}, u32[]{:S(2)}) %all-to-all-start) | async-done | bytes 1966112 | tf_op jit(solution)/shard_map/all_to_all | solution.py:99
  84.6 2.3 %convolution_bitcast_fusion = f32[64,1,16,64]{3,2,0,1:T(8,128)S(1)} fusion(bf16[64,16,960]{2,1,0:T(8,128)(2,1)} %all-to-all-done, bf16[1,64,960]{2,1,0:T(8,128)(2,1)S(1)} %copy-done.7), kind=kOutput, calls=%fused_computation.34 | convolution fusion | flops 125829120 | bytes 2351104 | tf_op jit(solution)/shard_map/sacd,ard->sacr/dot_general | solution.py:102
  86.9 18.9 %all-reduce.3 = bf16[64,1,16,64]{3,2,0,1:T(8,128)(2,1)S(1)} all-reduce(f32[64,1,16,64]{3,2,0,1:T(8,128)S(1)} %convolution_bitcast_fusion), channel_id=1, replica_groups=mesh['seq'=64,'tensor'=4] {'tensor'}, use_global_device_ids=true, to_apply=%region_4.5 | all-reduce | flops 65536 | bytes 393216 | tf_op jit(solution)/shard_map/psum | solution.py:105
  106.6 9.9 %all-to-all-start.1 = ((bf16[64,2,512]{2,1,0:T(2,128)(2,1)}), bf16[64,2,512]{2,1,0:T(2,128)(2,1)S(1)}, u32[]{:S(2)}, u32[]{:S(2)}) async-start(bf16[64,2,512]{2,1,0:T(2,128)(2,1)} %reshape.401), calls=%async_computation.1 | async-start | bytes 262144 | tf_op jit(solution)/shard_map/all_to_all | solution.py:107
  116.5 2.5 %fusion.16 = pred[512,1536]{0,1:T(8,128)(4,1)} fusion(s32[1536]{0:T(1024)S(1)} %pad_add_fusion.1, s32[512]{0:T(512)S(1)} %iota_add_fusion, s32[512]{0:T(512)S(1)} %copy-done.9, s32[1536]{0:T(1024)S(1)} %pad_add_fusion, pred[1536]{0:T(1024)(128)(4,1)S(1)} %broadcast_compare_fusion), kind=kLoop, calls=%fused_computation.20 | loop fusion | flops 5505024 | bytes 804352 | tf_op jit(solution)/shard_map/and | solution.py:149
  119.0 8.5 %all-to-all-done.1 = bf16[64,2,512]{2,1,0:T(2,128)(2,1)S(1)} async-done(((bf16[64,2,512]{2,1,0:T(2,128)(2,1)}), bf16[64,2,512]{2,1,0:T(2,128)(2,1)S(1)}, u32[]{:S(2)}, u32[]{:S(2)}) %all-to-all-start.1) | async-done | bytes 131104 | tf_op jit(solution)/shard_map/all_to_all | solution.py:107
  127.8 4.9 %fusion.32 = bf16[512,1,256]{2,0,1:T(8,128)(2,1)} fusion(bf16[512,3840]{0,1:T(8,128)(2,1)} %all-gather.3.cloned.1.call-done, bf16[3840,256]{1,0:T(8,128)(2,1)} %param.14), kind=kOutput, calls=%fused_computation.36 | convolution fusion | flops 1006764032 | bytes 6160384 | tf_op jit(solution)/shard_map/dot_general | solution.py:87
  132.7 3.1 %collective-permute-start.1 = (bf16[512,1,256]{2,0,1:T(8,128)(2,1)}, bf16[512,1,256]{2,0,1:T(8,128)(2,1)}, u32[]{:S(2)}, u32[]{:S(2)}) collective-permute-start(bf16[512,1,256]{2,0,1:T(8,128)(2,1)} %fusion.32), channel_id=1, source_target_pairs={{0,4},{4,8},{8,12},{12,16},{16,20},{20,24},{24,28},{28,32},{32,36}... | collective-permute-start | bytes 786440 | tf_op jit(solution)/shard_map/ppermute | solution.py:18
  135.8 3.4 %collective-permute-start = (bf16[512,1,256]{2,0,1:T(8,128)(2,1)}, bf16[512,1,256]{2,0,1:T(8,128)(2,1)}, u32[]{:S(2)}, u32[]{:S(2)}) collective-permute-start(bf16[512,1,256]{2,0,1:T(8,128)(2,1)} %fusion.32), channel_id=1, source_target_pairs={{0,8},{4,12},{8,16},{12,20},{16,24},{20,28},{24,32},{28,36},{32,40... | collective-permute-start | bytes 786440 | tf_op jit(solution)/shard_map/ppermute | solution.py:18
  145.1 2.9 %collective-permute-start.4 = (bf16[512,1,256]{0,2,1:T(8,128)(2,1)}, bf16[512,1,256]{0,2,1:T(8,128)(2,1)}, u32[]{:S(2)}, u32[]{:S(2)}) collective-permute-start(bf16[512,1,256]{0,2,1:T(8,128)(2,1)} %pad_maximum_fusion), channel_id=1, source_target_pairs={{0,8},{4,12},{8,16},{12,20},{16,24},{20,28},{24,32},{28,36},{32,40... | collective-permute-start | bytes 786440 | tf_op jit(solution)/shard_map/ppermute | solution.py:18
  148.0 3.0 %convolution_convert_fusion = bf16[64,16,512]{2,1,0:T(8,128)(2,1)S(1)} fusion(bf16[64,16,64]{2,1,0:T(8,128)(2,1)S(1)} %reshape.402, bf16[64,64,512]{2,1,0:T(8,128)(2,1)} %all-gather.5.cloned.1.call-done), kind=kOutput, calls=%fused_computation.28 | convolution fusion | flops 67633152 | bytes 5373952 | tf_op jit(solution)/shard_map/acr,are->ace/dot_general | solution.py:110
  152.6 3.2 %multiply_reduce_fusion.1 = (f32[512,2]{0,1:T(2,128)S(1)}, f32[512,512]{0,1:T(8,128)}) fusion(f32[512,512]{0,1:T(8,128)S(1)} %fusion.28, bf16[512,3840]{0,1:T(8,128)(2,1)S(1)} %copy-done.13, bf16[3840,512]{1,0:T(8,128)(2,1)S(1)} %copy-done.11), kind=kOutput, calls=%fused_computation.42 | convolution fusion | flops 2014051328 | bytes 9965568 | tf_op jit(solution)/shard_map/dot_general | solution.py:85
  158.8 3.1 %fusion.5 = (f32[2,512]{1,0:T(2,128)S(1)}, f32[1536,512,2]{1,0,2:T(8,128)S(1)}) fusion(pred[512,1536]{0,1:T(8,128)(4,1)S(1)} %copy-done.2, bf16[512,2,128]{2,0,1:T(8,128)(2,1)S(1)} %get-tuple-element.11, bf16[512,2,128]{2,0,1:T(8,128)(2,1)S(1)} %get-tuple-element.10, bf16[512,1,128]{0,2,1:T(8,128)(2,1)S(1)} %copy-done.6, ...), kind=kOutput, calls=%fused_computation.8 | convolution fusion | flops 814218240 | bytes 8392704 | tf_op jit(solution)/shard_map/tngd,knd->ngtk/dot_general | solution.py:49
  162.0 4.2 %fusion = (f32[2,512]{1,0:T(2,128)S(1)}, f32[1536,512,2]{1,0,2:T(8,128)S(1)}) fusion(f32[2,512]{1,0:T(2,128)S(1)} %get-tuple-element.20, f32[1536,512,2]{1,0,2:T(8,128)S(1)} %get-tuple-element.21, pred[512,1536]{0,1:T(8,128)(4,1)S(1)} %copy-done.2, bf16[64,2,8,256]{3,2,1,0:T(8,128)(2,1)S(1)} %bitcast.151, bf16[512,1,256]{2,0,1:T(8,128)(2,1)} %fusion.32, ...), kind=kOutput, calls=%fused_computation.3 | convolution fusion | flops 815528960 | bytes 14688256 | tf_op jit(solution)/shard_map/tngd,knd->ngtk/dot_general | solution.py:56
  166.2 3.8 %fusion.24 = f32[512,2,256]{2,0,1:T(8,128)S(1)} fusion(f32[1536,512,2]{1,0,2:T(8,128)S(1)} %get-tuple-element.23, f32[2,512]{1,0:T(2,128)S(1)} %get-tuple-element.22, f32[2,512]{1,0:T(2,128)S(1)} %get-tuple-element.20, f32[1536,512,2]{1,0,2:T(8,128)S(1)} %get-tuple-element.21, pred[512,1536]{0,1:T(8,128)(4,1)S(1)} %copy-done.2, ...), kind=kOutput, calls=%fused_computation.29 | convolution fusion | flops 819462144 | bytes 15212544 | tf_op jit(solution)/shard_map/ngtk,knd->tngd/dot_general | solution.py:59
  174.7 7.7 %all-to-all-start.2 = ((bf16[64,16,512]{2,1,0:T(8,128)(2,1)}), bf16[64,16,512]{2,1,0:T(8,128)(2,1)S(1)}, u32[]{:S(2)}, u32[]{:S(2)}) async-start(bf16[64,16,512]{2,1,0:T(8,128)(2,1)} %bitcast.143), calls=%async_computation.2 | async-start | bytes 2097152 | tf_op jit(solution)/shard_map/all_to_all | solution.py:162
  182.4 6.0 %fusion.29 = bf16[256,2,512]{2,0,1:T(8,128)(2,1)} fusion(f32[2,512]{1,0:T(2,128)S(1)} %get-tuple-element.20, f32[1536,512,2]{1,0,2:T(8,128)} %copy-done.15, pred[512,1536]{0,1:T(8,128)(4,1)} %fusion.16, bf16[512,1,256]{2,0,1:T(8,128)(2,1)} %fusion.32, bf16[512,1,256]{2,0,1:T(8,128)(2,1)} %collective-permute-done.1, ...), kind=kOutput, calls=%fused_computation.33 | convolution fusion | flops 814219264 | bytes 8392704 | tf_op jit(solution)/shard_map/ngtk,knd->tngd/dot_general | solution.py:55
  190.5 20.5 %all-to-all-done.2 = bf16[64,16,512]{2,1,0:T(8,128)(2,1)S(1)} async-done(((bf16[64,16,512]{2,1,0:T(8,128)(2,1)}), bf16[64,16,512]{2,1,0:T(8,128)(2,1)S(1)}, u32[]{:S(2)}, u32[]{:S(2)}) %all-to-all-start.2) | async-done | bytes 1048608 | tf_op jit(solution)/shard_map/all_to_all | solution.py:162
  (79 shorter events, 26.0 us)
Async XLA Ops:
  7.2 132.1 %copy-start = (bf16[3840,256]{1,0:T(8,128)(2,1)S(1)}, bf16[3840,256]{1,0:T(8,128)(2,1)}, u32[]{:S(2)}) copy-start(bf16[3840,256]{1,0:T(8,128)(2,1)} %param.13) | copy-start | bytes 5898244
  7.2 120.6 %all-gather.3.cloned.1.call-start = ((), (), s32[]{:S(2)}) async-start(), calls=%async_computation.3 | async-start | bytes 4915200 | tf_op jit(solution)/shard_map/all_gather | solution.py:84
  7.9 140.1 %all-gather.5.cloned.1.call-start = ((), (), s32[]{:S(2)}) async-start(), calls=%async_computation.4 | async-start | bytes 4259840 | tf_op jit(solution)/shard_map/all_gather | solution.py:106
  16.0 17.3 %copy-start.9 = (s32[512]{0:T(512)S(1)}, s32[512]{0:T(512)}, u32[]{:S(2)}) copy-start(s32[512]{0:T(512)} %param.20) | copy-start | bytes 6148
  16.0 68.6 %copy-start.7 = (bf16[1,64,960]{2,1,0:T(8,128)(2,1)S(1)}, bf16[1,64,960]{2,1,0:T(8,128)(2,1)}, u32[]{:S(2)}) copy-start(bf16[1,64,960]{2,1,0:T(8,128)(2,1)} %param.17) | copy-start | bytes 368644
  20.0 64.6 %all-to-all-start = ((bf16[64,16,960]{2,1,0:T(8,128)(2,1)}), bf16[64,16,960]{2,1,0:T(8,128)(2,1)}, u32[]{:S(2)}, u32[]{:S(2)}) async-start(bf16[64,16,960]{2,1,0:T(8,128)(2,1)} %bitcast.141), calls=%async_computation | async-start | bytes 4194304 | tf_op jit(solution)/shard_map/all_to_all | solution.py:99
  33.3 41.9 %collective-permute-start.2 = (s32[512]{0:T(512)S(1)}, s32[512]{0:T(512)S(1)}, u32[]{:S(2)}, u32[]{:S(2)}) collective-permute-start(s32[512]{0:T(512)S(1)} %copy-done.9), channel_id=1, source_target_pairs={{0,8},{4,12},{8,16},{12,20},{16,24},{20,28},{24,32},{28,36},{32,40... | collective-permute-start | bytes 6152 | tf_op jit(solution)/shard_map/ppermute | solution.py:18
  36.6 38.7 %collective-permute-start.3 = (s32[512]{0:T(512)S(1)}, s32[512]{0:T(512)S(1)}, u32[]{:S(2)}, u32[]{:S(2)}) collective-permute-start(s32[512]{0:T(512)S(1)} %copy-done.9), channel_id=1, source_target_pairs={{0,4},{4,8},{8,12},{12,16},{16,20},{20,24},{24,28},{28,32},{32,36}... | collective-permute-start | bytes 6152 | tf_op jit(solution)/shard_map/ppermute | solution.py:18
  106.6 21.0 %all-to-all-start.1 = ((bf16[64,2,512]{2,1,0:T(2,128)(2,1)}), bf16[64,2,512]{2,1,0:T(2,128)(2,1)S(1)}, u32[]{:S(2)}, u32[]{:S(2)}) async-start(bf16[64,2,512]{2,1,0:T(2,128)(2,1)} %reshape.401), calls=%async_computation.1 | async-start | bytes 262144 | tf_op jit(solution)/shard_map/all_to_all | solution.py:107
  127.8 11.4 %copy-start.12 = (bf16[512,3840]{0,1:T(8,128)(2,1)S(1)}, bf16[512,3840]{0,1:T(8,128)(2,1)}, u32[]{:S(2)}) copy-start(bf16[512,3840]{0,1:T(8,128)(2,1)} %all-gather.3.cloned.1.call-done) | copy-start | bytes 11796484
  132.7 7.8 %copy-start.10 = (f32[256]{0:T(256)S(1)}, f32[256]{0:T(256)}, u32[]{:S(2)}) copy-start(f32[256]{0:T(256)} %param.16) | copy-start | bytes 3076
  132.7 29.3 %collective-permute-start.1 = (bf16[512,1,256]{2,0,1:T(8,128)(2,1)}, bf16[512,1,256]{2,0,1:T(8,128)(2,1)}, u32[]{:S(2)}, u32[]{:S(2)}) collective-permute-start(bf16[512,1,256]{2,0,1:T(8,128)(2,1)} %fusion.32), channel_id=1, source_target_pairs={{0,4},{4,8},{8,12},{12,16},{16,20},{20,24},{24,28},{28,32},{32,36}... | collective-permute-start | bytes 786440 | tf_op jit(solution)/shard_map/ppermute | solution.py:18
  135.8 26.2 %collective-permute-start = (bf16[512,1,256]{2,0,1:T(8,128)(2,1)}, bf16[512,1,256]{2,0,1:T(8,128)(2,1)}, u32[]{:S(2)}, u32[]{:S(2)}) collective-permute-start(bf16[512,1,256]{2,0,1:T(8,128)(2,1)} %fusion.32), channel_id=1, source_target_pairs={{0,8},{4,12},{8,16},{12,20},{16,24},{20,28},{24,32},{28,36},{32,40... | collective-permute-start | bytes 786440 | tf_op jit(solution)/shard_map/ppermute | solution.py:18
  143.2 15.6 %collective-permute-start.5 = (bf16[512,1,256]{0,2,1:T(8,128)(2,1)}, bf16[512,1,256]{0,2,1:T(8,128)(2,1)}, u32[]{:S(2)}, u32[]{:S(2)}) collective-permute-start(bf16[512,1,256]{0,2,1:T(8,128)(2,1)} %pad_maximum_fusion), channel_id=1, source_target_pairs={{0,4},{4,8},{8,12},{12,16},{16,20},{20,24},{24,28},{28,32},{32,36}... | collective-permute-start | bytes 786440 | tf_op jit(solution)/shard_map/ppermute | solution.py:18
  145.1 13.7 %collective-permute-start.4 = (bf16[512,1,256]{0,2,1:T(8,128)(2,1)}, bf16[512,1,256]{0,2,1:T(8,128)(2,1)}, u32[]{:S(2)}, u32[]{:S(2)}) collective-permute-start(bf16[512,1,256]{0,2,1:T(8,128)(2,1)} %pad_maximum_fusion), channel_id=1, source_target_pairs={{0,8},{4,12},{8,16},{12,20},{16,24},{20,28},{24,32},{28,36},{32,40... | collective-permute-start | bytes 786440 | tf_op jit(solution)/shard_map/ppermute | solution.py:18
  148.0 3.8 %copy-start.11 = (bf16[3840,512]{1,0:T(8,128)(2,1)S(1)}, bf16[3840,512]{1,0:T(8,128)(2,1)}, u32[]{:S(2)}) copy-start(bf16[3840,512]{1,0:T(8,128)(2,1)} %param.12) | copy-start | bytes 11796484
  148.0 4.6 %copy-start.13 = (bf16[512,3840]{0,1:T(8,128)(2,1)S(1)}, bf16[512,3840]{0,1:T(8,128)(2,1)}, u32[]{:S(2)}) copy-start(bf16[512,3840]{0,1:T(8,128)(2,1)} %all-gather.3.cloned.1.call-done) | copy-start | bytes 11796484
  152.6 4.8 %copy-start.8 = (f32[256]{0:T(256)S(1)}, f32[256]{0:T(256)}, u32[]{:S(2)}) copy-start(f32[256]{0:T(256)} %param.15) | copy-start | bytes 3076
  157.3 1.4 copy-start.2
  157.4 1.4 copy-start.4
  158.8 3.2 %copy-start.14 = (bf16[512,512]{1,0:T(8,128)(2,1)S(1)}, bf16[512,512]{1,0:T(8,128)(2,1)}, u32[]{:S(2)}) copy-start(bf16[512,512]{1,0:T(8,128)(2,1)} %param.21) | copy-start | bytes 1572868
  162.0 4.2 %copy-start.15 = (f32[1536,512,2]{1,0,2:T(8,128)}, f32[1536,512,2]{1,0,2:T(8,128)S(1)}, u32[]{:S(2)}) copy-start(f32[1536,512,2]{1,0,2:T(8,128)S(1)} %get-tuple-element.21) | copy-start | bytes 18874372
  166.2 3.8 %copy-start.1 = (f32[512,128]{1,0:T(8,128)S(1)}, f32[512,128]{1,0:T(8,128)}, u32[]{:S(2)}) copy-start(f32[512,128]{1,0:T(8,128)} %get-tuple-element.15) | copy-start | bytes 786436
  174.7 36.3 %all-to-all-start.2 = ((bf16[64,16,512]{2,1,0:T(8,128)(2,1)}), bf16[64,16,512]{2,1,0:T(8,128)(2,1)S(1)}, u32[]{:S(2)}, u32[]{:S(2)}) async-start(bf16[64,16,512]{2,1,0:T(8,128)(2,1)} %bitcast.143), calls=%async_computation.2 | async-start | bytes 2097152 | tf_op jit(solution)/shard_map/all_to_all | solution.py:162
  (3 other events, 3.4 us)
Sparse Core Ops, SparseCore 0:
  9.8 52.1 all-gather.2
  64.8 80.3 all-gather.4

commit v5 on v1

--- a/solution.py
+++ b/solution.py
@@ -99,27 +99,6 @@
     arrived = lax.all_to_all(outgoing, "seq", 0, 0, tiled=True).reshape(
         seq_count, own_adapters, CAP, feat_width
     )
-    partial_low = jnp.einsum(
-        "sacd,ard->sacr", arrived, adapter_down, preferred_element_type=jnp.float32
-    )
-    slot_low = lax.psum(partial_low, "tensor").astype(jnp.bfloat16)
-    slot_lift = jnp.einsum(
-        "sacr,are->sace", slot_low, adapter_up, preferred_element_type=jnp.float32
-    ).astype(jnp.bfloat16)
-    back_lift = lax.all_to_all(
-        slot_lift.reshape(seq_count * own_adapters * CAP, q_width), "seq", 0, 0, tiled=True
-    )
-    lifted = jnp.einsum(
-        "st,se->te",
-        dispatch,
-        back_lift,
-        preferred_element_type=jnp.float32,
-    ).astype(jnp.bfloat16)
-    query_pre = (query_lin + lifted.astype(jnp.float32)).reshape(tok_count, local_heads, HD)
-    queries, query_back = jax.vjp(
-        lambda pre_query: shape_query(pre_query, query_gain, positions), query_pre
-    )
-    queries = queries.astype(jnp.bfloat16).reshape(tok_count, kv_heads, head_group, HD)
     key_rows = shape_query(key_lin.reshape(tok_count, kv_heads, HD), key_gain, positions).astype(
         jnp.bfloat16
     )
@@ -150,6 +129,31 @@
         & (key_gap < WINDOW)
         & (key_pos[None, :] >= 0)
     )
+    arrived, query_lin, window_keys, window_values, allowed = lax.optimization_barrier(
+        (arrived, query_lin, window_keys, window_values, allowed)
+    )
+    partial_low = jnp.einsum(
+        "sacd,ard->sacr", arrived, adapter_down, preferred_element_type=jnp.float32
+    )
+    slot_low = lax.psum(partial_low, "tensor").astype(jnp.bfloat16)
+    all_up = lax.all_gather(adapter_up, "seq", axis=0, tiled=True)
+    back_low = lax.all_to_all(
+        slot_low.reshape(seq_count * own_adapters * CAP, R), "seq", 0, 0, tiled=True
+    ).reshape(ADAPTERS, CAP, R)
+    slot_lift = jnp.einsum(
+        "acr,are->ace", back_low, all_up, preferred_element_type=jnp.float32
+    ).astype(jnp.bfloat16)
+    lifted = jnp.einsum(
+        "st,se->te",
+        dispatch,
+        slot_lift.reshape(ADAPTERS * CAP, q_width),
+        preferred_element_type=jnp.float32,
+    ).astype(jnp.bfloat16)
+    query_pre = (query_lin + lifted.astype(jnp.float32)).reshape(tok_count, local_heads, HD)
+    queries, query_back = jax.vjp(
+        lambda pre_query: shape_query(pre_query, query_gain, positions), query_pre
+    )
+    queries = queries.astype(jnp.bfloat16).reshape(tok_count, kv_heads, head_group, HD)
     upstream = cotangent.reshape(tok_count, kv_heads, head_group, HD)
     block_out, dqueries = attend(queries, window_keys, window_values, upstream, allowed)
     attended = block_out.reshape(tok_count, q_width)

time: 220 us -> 215 us (0.977)
  matrix products: 40.7 us -> 34.2 us
  starting transfers between devices: 54.5 us -> 48.8 us
  local copies, waits for them, and re-layouts: 9.09 us -> 11.5 us
    all_gather x1, waiting for transfers between devices: 0.01 us -> 20.4 us  [local(): shard_cols = lax.all_gather(tokens, 'tensor', axis=1, tiled=True)]
    ppermute x6, waiting for transfers between devices: 33 us -> 17.5 us  [passed_along(): lax.ppermute(value, axis, [(source, source + steps) for source in range(f...]
    all_to_all x1, waiting for transfers between devices: 9.25 us -> 0.01 us  [local(): lax.all_to_all(outgoing, 'seq', 0, 0, tiled=True)]
    all_to_all x1, starting transfers between devices: 10.8 us -> 4.85 us  [local(): lax.all_to_all(out_grad, 'seq', 0, 0, tiled=True)]
    all_to_all x1, waiting for transfers between devices: 4.25 us -> 8.6 us  [local(): lax.all_to_all(slot_low.reshape(seq_count * own_adapters * CAP, R), 'seq'...]
    dot_general x1, matrix products: 6.53 us -> 3.18 us  [local(): query_lin = jnp.dot(shard_cols, w_query, preferred_element_type=jnp.float32)]
    all_to_all x1, starting transfers between devices: 13.5 us -> 10.2 us  [local(): lax.all_to_all(outgoing, 'seq', 0, 0, tiled=True)]
    reduce_sum x0 -> x1, other arithmetic: none -> 2.56 us  [normalize(): mean_sq = jnp.mean(pre_field * pre_field, axis=-1, keepdims=True)]
  transfers between devices with their start and end apart: 10 -> 11, of which waited for: 6 -> 7; matrix products, arithmetic and copies ran while one was open for 23% -> 18% of each run, Pallas kernels for 0% -> 0%
where the time goes in v5:
time: 215 us; the launch traced here: 214 us
  waiting for transfers between devices  68.3 us (32%)
  starting transfers between devices  48.8 us (23%)
  matrix products  34.2 us (16%)
  blocking collectives  20 us (9%)
  other arithmetic  16.5 us (8%)
  between operations  14.5 us (7%)
  local copies, waits for them, and re-layouts  11.5 us (5%)
    ppermute x6, starting transfers between devices, passed_along(): lax.ppermute(value, axis, [(source, source + steps) for source in range(f...  21.6 us
    all_to_all x1, waiting for transfers between devices, local(): lax.all_to_all(out_grad, 'seq', 0, 0, tiled=True)  20.4 us
    all_gather x1, waiting for transfers between devices, local(): shard_cols = lax.all_gather(tokens, 'tensor', axis=1, tiled=True)  20.4 us
    psum x1, blocking collectives, local(): slot_low = lax.psum(partial_low, 'tensor').astype(jnp.bfloat16)  20 us
    ppermute x6, waiting for transfers between devices, passed_along(): lax.ppermute(value, axis, [(source, source + steps) for source in range(f...  17.5 us
    all_to_all x1, starting transfers between devices, local(): lax.all_to_all(slot_low.reshape(seq_count * own_adapters * CAP, R), 'seq'...  12 us
    all_to_all x1, starting transfers between devices, local(): lax.all_to_all(outgoing, 'seq', 0, 0, tiled=True)  10.2 us
    all_to_all x1, waiting for transfers between devices, local(): lax.all_to_all(slot_low.reshape(seq_count * own_adapters * CAP, R), 'seq'...  8.6 us
  transfers between devices with their start and end apart: 11, of which 7 were waited for; matrix products, arithmetic and copies ran while one was open for 18% of the time, Pallas kernels for 0%

profile of v5, /device:TPU:1, one launch (start us, length us, event | category | flops | bytes accessed | tf_op | source)
XLA Modules:
  0.0 213.8 jit_solution(6500575352448793666)
XLA Ops:
  8.7 4.4 %collective-permute-start.4 = (s32[512]{0:T(512)}, s32[512]{0:T(512)S(1)}, u32[]{:S(2)}, u32[]{:S(2)}) collective-permute-start(s32[512]{0:T(512)} %param.20), channel_id=1, source_target_pairs={{0,8},{4,12},{8,16},{12,20},{16,24},{20,28},{24,32},{28,36},{32,40... | collective-permute-start | bytes 6152 | tf_op jit(solution)/shard_map/ppermute | solution.py:18
  13.0 4.4 %collective-permute-start.5 = (s32[512]{0:T(512)}, s32[512]{0:T(512)S(1)}, u32[]{:S(2)}, u32[]{:S(2)}) collective-permute-start(s32[512]{0:T(512)} %param.20), channel_id=1, source_target_pairs={{0,4},{4,8},{8,12},{12,16},{16,20},{20,24},{24,28},{28,32},{32,36}... | collective-permute-start | bytes 6152 | tf_op jit(solution)/shard_map/ppermute | solution.py:18
  21.1 3.7 %fusion.24 = bf16[1024,960]{0,1:T(8,128)(2,1)} fusion(bf16[512,960]{0,1:T(8,128)(2,1)} %param.11, s32[512]{0:T(512)S(1)} %multiply_add_fusion.3), kind=kOutput, calls=%fused_computation.27 | convolution fusion | flops 1008140288 | bytes 2951168 | tf_op jit(solution)/shard_map/dot_general | solution.py:96
  24.8 4.0 %copy.80 = bf16[1024,960]{1,0:T(8,128)(2,1)} copy(bf16[1024,960]{0,1:T(8,128)(2,1)} %fusion.24) | data formatting | bytes 3932160 | tf_op jit(solution)/shard_map/convert_element_type | solution.py:96
  28.8 10.2 %all-to-all-start = ((bf16[64,16,960]{2,1,0:T(8,128)(2,1)}), bf16[64,16,960]{2,1,0:T(8,128)(2,1)}, u32[]{:S(2)}, u32[]{:S(2)}) async-start(bf16[64,16,960]{2,1,0:T(8,128)(2,1)} %bitcast.160), calls=%async_computation | async-start | bytes 4194304 | tf_op jit(solution)/shard_map/all_to_all | solution.py:99
  41.6 20.4 %all-gather.3.cloned.1.call-done = bf16[512,3840]{0,1:T(8,128)(2,1)} async-done(((bf16[512,960]{0,1:T(8,128)(2,1)}), bf16[512,3840]{0,1:T(8,128)(2,1)}) %all-gather.3.cloned.1.call-update) | async-done | bytes 3932176 | tf_op jit(solution)/shard_map/all_gather | solution.py:84
  62.0 4.1 %fusion.38 = bf16[512,1,256]{2,0,1:T(8,128)(2,1)S(1)} fusion(bf16[512,3840]{0,1:T(8,128)(2,1)} %all-gather.3.cloned.1.call-done, bf16[3840,256]{1,0:T(8,128)(2,1)} %param.14), kind=kOutput, calls=%fused_computation.38 | convolution fusion | flops 1006764032 | bytes 6160384 | tf_op jit(solution)/shard_map/dot_general | solution.py:87
  66.1 4.2 %collective-permute-start.3 = (bf16[512,1,256]{2,0,1:T(8,128)(2,1)S(1)}, bf16[512,1,256]{2,0,1:T(8,128)(2,1)S(1)}, u32[]{:S(2)}, u32[]{:S(2)}) collective-permute-start(bf16[512,1,256]{2,0,1:T(8,128)(2,1)S(1)} %fusion.38), channel_id=1, source_target_pairs={{0,4},{4,8},{8,12},{12,16},{16,20},{20,24},{24,28},{28,32},{32,36}... | collective-permute-start | bytes 786440 | tf_op jit(solution)/shard_map/ppermute | solution.py:18
  70.3 3.2 %collective-permute-start.2 = (bf16[512,1,256]{2,0,1:T(8,128)(2,1)S(1)}, bf16[512,1,256]{2,0,1:T(8,128)(2,1)S(1)}, u32[]{:S(2)}, u32[]{:S(2)}) collective-permute-start(bf16[512,1,256]{2,0,1:T(8,128)(2,1)S(1)} %fusion.38), channel_id=1, source_target_pairs={{0,8},{4,12},{8,16},{12,20},{16,24},{20,28},{24,32},{28,36},{32,40... | collective-permute-start | bytes 786440 | tf_op jit(solution)/shard_map/ppermute | solution.py:18
  78.5 3.2 %collective-permute-start = (bf16[512,1,256]{0,2,1:T(8,128)(2,1)S(1)}, bf16[512,1,256]{0,2,1:T(8,128)(2,1)S(1)}, u32[]{:S(2)}, u32[]{:S(2)}) collective-permute-start(bf16[512,1,256]{0,2,1:T(8,128)(2,1)S(1)} %pad_maximum_fusion.1), channel_id=1, source_target_pairs={{0,8},{4,12},{8,16},{12,20},{16,24},{20,28},{24,32},{28,36},{32,40... | collective-permute-start | bytes 786440 | tf_op jit(solution)/shard_map/ppermute | solution.py:18
  81.7 3.2 %fusion.78 = f32[512,512]{1,0:T(8,128)} fusion(bf16[512,3840]{0,1:T(8,128)(2,1)S(1)} %copy-done.2, bf16[3840,512]{1,0:T(8,128)(2,1)S(1)} %copy-done.1), kind=kOutput, calls=%fused_computation.112 | convolution fusion | flops 2013265920 | bytes 8912896 | tf_op jit(solution)/shard_map/dot_general | solution.py:85
  84.9 5.4 %collective-permute-done.3 = bf16[512,1,256]{2,0,1:T(8,128)(2,1)S(1)} collective-permute-done((bf16[512,1,256]{2,0,1:T(8,128)(2,1)S(1)}, bf16[512,1,256]{2,0,1:T(8,128)(2,1)S(1)}, u32[]{:S(2)}, u32[]{:S(2)}) %collective-permute-start.3) | collective-permute-done | bytes 262176 | tf_op jit(solution)/shard_map/ppermute | solution.py:18
  90.3 6.3 %collective-permute-done.2 = bf16[512,1,256]{2,0,1:T(8,128)(2,1)S(1)} collective-permute-done((bf16[512,1,256]{2,0,1:T(8,128)(2,1)S(1)}, bf16[512,1,256]{2,0,1:T(8,128)(2,1)S(1)}, u32[]{:S(2)}, u32[]{:S(2)}) %collective-permute-start.2) | collective-permute-done | bytes 262176 | tf_op jit(solution)/shard_map/ppermute | solution.py:18
  97.6 2.9 %collective-permute-done.1 = bf16[512,1,256]{0,2,1:T(8,128)(2,1)S(1)} collective-permute-done((bf16[512,1,256]{0,2,1:T(8,128)(2,1)S(1)}, bf16[512,1,256]{0,2,1:T(8,128)(2,1)S(1)}, u32[]{:S(2)}, u32[]{:S(2)}) %collective-permute-start.1) | collective-permute-done | bytes 262176 | tf_op jit(solution)/shard_map/ppermute | solution.py:18
  100.4 2.9 %collective-permute-done = bf16[512,1,256]{0,2,1:T(8,128)(2,1)S(1)} collective-permute-done((bf16[512,1,256]{0,2,1:T(8,128)(2,1)S(1)}, bf16[512,1,256]{0,2,1:T(8,128)(2,1)S(1)}, u32[]{:S(2)}, u32[]{:S(2)}) %collective-permute-start) | collective-permute-done | bytes 262176 | tf_op jit(solution)/shard_map/ppermute | solution.py:18
  106.6 20.0 %all-reduce.3 = bf16[64,1,16,64]{3,2,0,1:T(8,128)(2,1)S(1)} all-reduce(f32[64,1,16,64]{3,2,0,1:T(8,128)S(1)} %fusion.35), channel_id=1, replica_groups=mesh['seq'=64,'tensor'=4] {'tensor'}, use_global_device_ids=true, to_apply=%region_4.5 | all-reduce | flops 65536 | bytes 393216 | tf_op jit(solution)/shard_map/psum | solution.py:138
  127.4 12.0 %all-to-all-start.1 = ((bf16[64,2,512]{2,1,0:T(2,128)(2,1)}), bf16[64,2,512]{2,1,0:T(2,128)(2,1)S(1)}, u32[]{:S(2)}, u32[]{:S(2)}) async-start(bf16[64,2,512]{2,1,0:T(2,128)(2,1)} %reshape.336), calls=%async_computation.1 | async-start | bytes 262144 | tf_op jit(solution)/shard_map/all_to_all | solution.py:140
  141.2 8.6 %all-to-all-done.1 = bf16[64,2,512]{2,1,0:T(2,128)(2,1)S(1)} async-done(((bf16[64,2,512]{2,1,0:T(2,128)(2,1)}), bf16[64,2,512]{2,1,0:T(2,128)(2,1)S(1)}, u32[]{:S(2)}, u32[]{:S(2)}) %all-to-all-start.1) | async-done | bytes 131104 | tf_op jit(solution)/shard_map/all_to_all | solution.py:140
  150.1 2.9 %convolution_convert_fusion = bf16[64,16,512]{2,1,0:T(8,128)(2,1)S(1)} fusion(bf16[64,16,64]{2,1,0:T(8,128)(2,1)S(1)} %reshape.337, bf16[64,64,512]{2,1,0:T(8,128)(2,1)} %all-gather.5.cloned.1.call-done), kind=kOutput, calls=%fused_computation.30 | convolution fusion | flops 67633152 | bytes 5373952 | tf_op jit(solution)/shard_map/acr,are->ace/dot_general | solution.py:143
  155.4 2.6 %multiply_reduce_fusion = f32[512,2]{1,0:T(8,128)} fusion(f32[512,2,256]{2,1,0:T(2,128)} %reshape.323), kind=kLoop, calls=%fused_computation.47 | loop fusion | flops 523264 | bytes 1052672 | tf_op jit(solution)/shard_map/jvp()/reduce_sum | solution.py:22
  165.3 2.7 %fusion.26 = f32[512,2,256]{2,0,1:T(8,128)S(1)} fusion(f32[1536,512,2]{1,0,2:T(8,128)S(1)} %get-tuple-element.35, f32[2,512]{1,0:T(2,128)S(1)} %get-tuple-element.34, f32[2,512]{1,0:T(2,128)S(1)} %get-tuple-element.32, f32[1536,512,2]{1,0,2:T(8,128)S(1)} %get-tuple-element.33, pred[512,1536]{0,1:T(8,128)(4,1)S(1)} %copy-done.5, ...), kind=kOutput, calls=%fused_computation.31 | convolution fusion | flops 816316416 | bytes 15212544 | tf_op jit(solution)/shard_map/ngtk,knd->tngd/dot_general | solution.py:59
  172.6 4.8 %all-to-all-start.2 = ((bf16[64,16,512]{2,1,0:T(8,128)(2,1)}), bf16[64,16,512]{2,1,0:T(8,128)(2,1)S(1)}, u32[]{:S(2)}, u32[]{:S(2)}) async-start(bf16[64,16,512]{2,1,0:T(8,128)(2,1)} %bitcast.162), calls=%async_computation.2 | async-start | bytes 2097152 | tf_op jit(solution)/shard_map/all_to_all | solution.py:165
  177.5 6.1 %fusion.32 = bf16[256,2,512]{2,0,1:T(8,128)(2,1)} fusion(f32[2,512]{1,0:T(2,128)S(1)} %get-tuple-element.32, f32[1536,512,2]{1,0,2:T(8,128)} %copy-done.13, pred[512,1536]{0,1:T(8,128)(4,1)} %fusion.16, bf16[1536,1,256]{2,0,1:T(8,128)(2,1)} %pad_maximum_fusion), kind=kOutput, calls=%fused_computation.35 | convolution fusion | flops 811859968 | bytes 8392704 | tf_op jit(solution)/shard_map/ngtk,knd->tngd/dot_general | solution.py:55
  185.6 20.4 %all-to-all-done.2 = bf16[64,16,512]{2,1,0:T(8,128)(2,1)S(1)} async-done(((bf16[64,16,512]{2,1,0:T(8,128)(2,1)}), bf16[64,16,512]{2,1,0:T(8,128)(2,1)S(1)}, u32[]{:S(2)}, u32[]{:S(2)}) %all-to-all-start.2) | async-done | bytes 1048608 | tf_op jit(solution)/shard_map/all_to_all | solution.py:165
  (79 shorter events, 36.8 us)
Async XLA Ops:
  7.2 66.4 %copy-start = (bf16[3840,256]{1,0:T(8,128)(2,1)S(1)}, bf16[3840,256]{1,0:T(8,128)(2,1)}, u32[]{:S(2)}) copy-start(bf16[3840,256]{1,0:T(8,128)(2,1)} %param.13) | copy-start | bytes 5898244
  7.2 54.8 %all-gather.3.cloned.1.call-start = ((), (), s32[]{:S(2)}) async-start(), calls=%async_computation.3 | async-start | bytes 4915200 | tf_op jit(solution)/shard_map/all_gather | solution.py:84
  7.9 142.2 %all-gather.5.cloned.1.call-start = ((), (), s32[]{:S(2)}) async-start(), calls=%async_computation.4 | async-start | bytes 4259840 | tf_op jit(solution)/shard_map/all_gather | solution.py:139
  8.7 30.4 %collective-permute-start.4 = (s32[512]{0:T(512)}, s32[512]{0:T(512)S(1)}, u32[]{:S(2)}, u32[]{:S(2)}) collective-permute-start(s32[512]{0:T(512)} %param.20), channel_id=1, source_target_pairs={{0,8},{4,12},{8,16},{12,20},{16,24},{20,28},{24,32},{28,36},{32,40... | collective-permute-start | bytes 6152 | tf_op jit(solution)/shard_map/ppermute | solution.py:18
  13.0 26.1 %collective-permute-start.5 = (s32[512]{0:T(512)}, s32[512]{0:T(512)S(1)}, u32[]{:S(2)}, u32[]{:S(2)}) collective-permute-start(s32[512]{0:T(512)} %param.20), channel_id=1, source_target_pairs={{0,4},{4,8},{8,12},{12,16},{16,20},{20,24},{24,28},{28,32},{32,36}... | collective-permute-start | bytes 6152 | tf_op jit(solution)/shard_map/ppermute | solution.py:18
  24.8 14.3 %copy-start.10 = (s32[512]{0:T(512)S(1)}, s32[512]{0:T(512)}, u32[]{:S(2)}) copy-start(s32[512]{0:T(512)} %param.20) | copy-start | bytes 6148
  28.8 75.5 %all-to-all-start = ((bf16[64,16,960]{2,1,0:T(8,128)(2,1)}), bf16[64,16,960]{2,1,0:T(8,128)(2,1)}, u32[]{:S(2)}, u32[]{:S(2)}) async-start(bf16[64,16,960]{2,1,0:T(8,128)(2,1)} %bitcast.160), calls=%async_computation | async-start | bytes 4194304 | tf_op jit(solution)/shard_map/all_to_all | solution.py:99
  62.0 11.5 %copy-start.2 = (bf16[512,3840]{0,1:T(8,128)(2,1)S(1)}, bf16[512,3840]{0,1:T(8,128)(2,1)}, u32[]{:S(2)}) copy-start(bf16[512,3840]{0,1:T(8,128)(2,1)} %all-gather.3.cloned.1.call-done) | copy-start | bytes 11796484
  66.1 8.7 %copy-start.11 = (f32[256]{0:T(256)S(1)}, f32[256]{0:T(256)}, u32[]{:S(2)}) copy-start(f32[256]{0:T(256)} %param.16) | copy-start | bytes 3076
  66.1 15.5 %copy-start.1 = (bf16[3840,512]{1,0:T(8,128)(2,1)S(1)}, bf16[3840,512]{1,0:T(8,128)(2,1)}, u32[]{:S(2)}) copy-start(bf16[3840,512]{1,0:T(8,128)(2,1)} %param.12) | copy-start | bytes 11796484
  66.1 24.1 %collective-permute-start.3 = (bf16[512,1,256]{2,0,1:T(8,128)(2,1)S(1)}, bf16[512,1,256]{2,0,1:T(8,128)(2,1)S(1)}, u32[]{:S(2)}, u32[]{:S(2)}) collective-permute-start(bf16[512,1,256]{2,0,1:T(8,128)(2,1)S(1)} %fusion.38), channel_id=1, source_target_pairs={{0,4},{4,8},{8,12},{12,16},{16,20},{20,24},{24,28},{28,32},{32,36}... | collective-permute-start | bytes 786440 | tf_op jit(solution)/shard_map/ppermute | solution.py:18
  70.3 26.3 %collective-permute-start.2 = (bf16[512,1,256]{2,0,1:T(8,128)(2,1)S(1)}, bf16[512,1,256]{2,0,1:T(8,128)(2,1)S(1)}, u32[]{:S(2)}, u32[]{:S(2)}) collective-permute-start(bf16[512,1,256]{2,0,1:T(8,128)(2,1)S(1)} %fusion.38), channel_id=1, source_target_pairs={{0,8},{4,12},{8,16},{12,20},{16,24},{20,28},{24,32},{28,36},{32,40... | collective-permute-start | bytes 786440 | tf_op jit(solution)/shard_map/ppermute | solution.py:18
  76.1 28.2 %copy-start.8 = (bf16[1,64,960]{2,1,0:T(8,128)(2,1)S(1)}, bf16[1,64,960]{2,1,0:T(8,128)(2,1)}, u32[]{:S(2)}) copy-start(bf16[1,64,960]{2,1,0:T(8,128)(2,1)} %param.17) | copy-start | bytes 368644
  76.1 24.3 %collective-permute-start.1 = (bf16[512,1,256]{0,2,1:T(8,128)(2,1)S(1)}, bf16[512,1,256]{0,2,1:T(8,128)(2,1)S(1)}, u32[]{:S(2)}, u32[]{:S(2)}) collective-permute-start(bf16[512,1,256]{0,2,1:T(8,128)(2,1)S(1)} %pad_maximum_fusion.1), channel_id=1, source_target_pairs={{0,4},{4,8},{8,12},{12,16},{16,20},{20,24},{24,28},{28,32},{32,36}... | collective-permute-start | bytes 786440 | tf_op jit(solution)/shard_map/ppermute | solution.py:18
  78.5 24.9 %collective-permute-start = (bf16[512,1,256]{0,2,1:T(8,128)(2,1)S(1)}, bf16[512,1,256]{0,2,1:T(8,128)(2,1)S(1)}, u32[]{:S(2)}, u32[]{:S(2)}) collective-permute-start(bf16[512,1,256]{0,2,1:T(8,128)(2,1)S(1)} %pad_maximum_fusion.1), channel_id=1, source_target_pairs={{0,8},{4,12},{8,16},{12,20},{16,24},{20,28},{24,32},{28,36},{32,40... | collective-permute-start | bytes 786440 | tf_op jit(solution)/shard_map/ppermute | solution.py:18
  127.4 22.4 %all-to-all-start.1 = ((bf16[64,2,512]{2,1,0:T(2,128)(2,1)}), bf16[64,2,512]{2,1,0:T(2,128)(2,1)S(1)}, u32[]{:S(2)}, u32[]{:S(2)}) async-start(bf16[64,2,512]{2,1,0:T(2,128)(2,1)} %reshape.336), calls=%async_computation.1 | async-start | bytes 262144 | tf_op jit(solution)/shard_map/all_to_all | solution.py:140
  150.1 3.0 %copy-start.4 = (f32[512,512]{1,0:T(8,128)S(1)}, f32[512,512]{1,0:T(8,128)}, u32[]{:S(2)}) copy-start(f32[512,512]{1,0:T(8,128)} %fusion.78) | copy-start | bytes 3145732
  153.0 6.1 %copy-start.9 = (f32[256]{0:T(256)S(1)}, f32[256]{0:T(256)}, u32[]{:S(2)}) copy-start(f32[256]{0:T(256)} %param.15) | copy-start | bytes 3076
  159.1 1.5 copy-start.7
  160.5 2.1 copy-start.6
  160.6 2.1 copy-start.12
  162.6 2.7 %copy-start.13 = (f32[1536,512,2]{1,0,2:T(8,128)}, f32[1536,512,2]{1,0,2:T(8,128)S(1)}, u32[]{:S(2)}) copy-start(f32[1536,512,2]{1,0,2:T(8,128)S(1)} %get-tuple-element.33) | copy-start | bytes 18874372
  165.3 2.7 %copy-start.3 = (f32[512,128]{1,0:T(8,128)S(1)}, f32[512,128]{1,0:T(8,128)}, u32[]{:S(2)}) copy-start(f32[512,128]{1,0:T(8,128)} %get-tuple-element.29) | copy-start | bytes 786436
  172.6 33.4 %all-to-all-start.2 = ((bf16[64,16,512]{2,1,0:T(8,128)(2,1)}), bf16[64,16,512]{2,1,0:T(8,128)(2,1)S(1)}, u32[]{:S(2)}, u32[]{:S(2)}) async-start(bf16[64,16,512]{2,1,0:T(8,128)(2,1)} %bitcast.162), calls=%async_computation.2 | async-start | bytes 2097152 | tf_op jit(solution)/shard_map/all_to_all | solution.py:165
  (1 other events, 1.5 us)
Sparse Core Ops, SparseCore 0:
  9.8 52.1 all-gather.2
  64.8 80.9 all-gather.4

commit v6 on v5

--- a/solution.py
+++ b/solution.py
@@ -108,10 +108,11 @@
     value_list = []
     doc_list = []
     place_list = []
+    kv_rows = jnp.stack([key_rows, values], axis=1)
     for distance in range(rim_count, 0, -1):
-        far_keys, far_values, far_docs = passed_along((key_rows, values, doc_ids), "seq", distance)
-        key_list.append(far_keys)
-        value_list.append(far_values)
+        far_kv, far_docs = passed_along((kv_rows, doc_ids), "seq", distance)
+        key_list.append(far_kv[:, 0])
+        value_list.append(far_kv[:, 1])
         doc_list.append(far_docs)
         place_list.append(positions - distance * tok_count)
     key_list.append(key_rows)

time: 215 us -> 214 us (level)
  waiting for transfers between devices: 68.3 us -> 75.5 us
  starting transfers between devices: 48.8 us -> 41.7 us
    ppermute x6 -> x4, waiting for transfers between devices: 17.5 us -> 24.7 us  [passed_along(): lax.ppermute(value, axis, [(source, source + steps) for source in range(f...]
    ppermute x6 -> x4, starting transfers between devices: 21.6 us -> 15.9 us  [passed_along(): lax.ppermute(value, axis, [(source, source + steps) for source in range(f...]
    dot_general x1, matrix products: 4.1 us -> 1.22 us  [local(): value_lin = jnp.dot(shard_cols, w_value, preferred_element_type=jnp.float32)]
    dot_general x1, matrix products: 1.24 us -> 3.5 us  [local(): key_lin = jnp.dot(shard_cols, w_key, preferred_element_type=jnp.float32)]
  transfers between devices with their start and end apart: 11 -> 9, of which waited for: 7 -> 5; matrix products, arithmetic and copies ran while one was open for 18% -> 18% of each run, Pallas kernels for 0% -> 0%
where the time goes in v6:
time: 214 us; the launch traced here: 213 us
  waiting for transfers between devices  75.5 us (35%)
  starting transfers between devices  41.7 us (19%)
  matrix products  33.6 us (16%)
  blocking collectives  20.2 us (9%)
  other arithmetic  15.9 us (7%)
  between operations  14.5 us (7%)
  local copies, waits for them, and re-layouts  11.5 us (5%)
    ppermute x4, waiting for transfers between devices, passed_along(): lax.ppermute(value, axis, [(source, source + steps) for source in range(f...  24.7 us
    all_gather x1, waiting for transfers between devices, local(): shard_cols = lax.all_gather(tokens, 'tensor', axis=1, tiled=True)  20.4 us
    all_to_all x1, waiting for transfers between devices, local(): lax.all_to_all(out_grad, 'seq', 0, 0, tiled=True)  20.4 us
    psum x1, blocking collectives, local(): slot_low = lax.psum(partial_low, 'tensor').astype(jnp.bfloat16)  20.2 us
    ppermute x4, starting transfers between devices, passed_along(): lax.ppermute(value, axis, [(source, source + steps) for source in range(f...  15.9 us
    all_to_all x1, starting transfers between devices, local(): lax.all_to_all(slot_low.reshape(seq_count * own_adapters * CAP, R), 'seq'...  10.7 us
    all_to_all x1, starting transfers between devices, local(): lax.all_to_all(outgoing, 'seq', 0, 0, tiled=True)  10.1 us
    all_to_all x1, waiting for transfers between devices, local(): lax.all_to_all(slot_low.reshape(seq_count * own_adapters * CAP, R), 'seq'...  8.58 us
  transfers between devices with their start and end apart: 9, of which 5 were waited for; matrix products, arithmetic and copies ran while one was open for 18% of the time, Pallas kernels for 0%

profile of v6, /device:TPU:1, one launch (start us, length us, event | category | flops | bytes accessed | tf_op | source)
XLA Modules:
  0.0 213.0 jit_solution(9116401820702605938)
XLA Ops:
  8.7 4.4 %collective-permute-start.2 = (s32[512]{0:T(512)}, s32[512]{0:T(512)S(1)}, u32[]{:S(2)}, u32[]{:S(2)}) collective-permute-start(s32[512]{0:T(512)} %param.20), channel_id=1, source_target_pairs={{0,8},{4,12},{8,16},{12,20},{16,24},{20,28},{24,32},{28,36},{32,40... | collective-permute-start | bytes 6152 | tf_op jit(solution)/shard_map/ppermute | solution.py:18
  13.0 4.4 %collective-permute-start.3 = (s32[512]{0:T(512)}, s32[512]{0:T(512)S(1)}, u32[]{:S(2)}, u32[]{:S(2)}) collective-permute-start(s32[512]{0:T(512)} %param.20), channel_id=1, source_target_pairs={{0,4},{4,8},{8,12},{12,16},{16,20},{20,24},{24,28},{28,32},{32,36}... | collective-permute-start | bytes 6152 | tf_op jit(solution)/shard_map/ppermute | solution.py:18
  21.1 3.7 %fusion.24 = bf16[1024,960]{0,1:T(8,128)(2,1)} fusion(bf16[512,960]{0,1:T(8,128)(2,1)} %param.11, s32[512]{0:T(512)S(1)} %multiply_add_fusion.3), kind=kOutput, calls=%fused_computation.27 | convolution fusion | flops 1008140288 | bytes 2951168 | tf_op jit(solution)/shard_map/dot_general | solution.py:96
  24.8 4.0 %copy.84 = bf16[1024,960]{1,0:T(8,128)(2,1)} copy(bf16[1024,960]{0,1:T(8,128)(2,1)} %fusion.24) | data formatting | bytes 3932160 | tf_op jit(solution)/shard_map/convert_element_type | solution.py:96
  28.8 10.1 %all-to-all-start = ((bf16[64,16,960]{2,1,0:T(8,128)(2,1)}), bf16[64,16,960]{2,1,0:T(8,128)(2,1)}, u32[]{:S(2)}, u32[]{:S(2)}) async-start(bf16[64,16,960]{2,1,0:T(8,128)(2,1)} %bitcast.170), calls=%async_computation | async-start | bytes 4194304 | tf_op jit(solution)/shard_map/all_to_all | solution.py:99
  39.1 2.5 %fusion.16 = pred[512,1536]{0,1:T(8,128)(4,1)} fusion(s32[1536]{0:T(1024)S(1)} %pad_add_fusion.1, s32[512]{0:T(512)S(1)} %iota_add_fusion, s32[512]{0:T(512)S(1)} %copy-done.10, s32[1536]{0:T(1024)S(1)} %pad_add_fusion, pred[1536]{0:T(1024)(128)(4,1)S(1)} %broadcast_compare_fusion), kind=kLoop, calls=%fused_computation.20 | loop fusion | flops 5505024 | bytes 804352 | tf_op jit(solution)/shard_map/and | solution.py:128
  41.6 20.4 %all-gather.3.cloned.1.call-done = bf16[512,3840]{0,1:T(8,128)(2,1)} async-done(((bf16[512,960]{0,1:T(8,128)(2,1)}), bf16[512,3840]{0,1:T(8,128)(2,1)}) %all-gather.3.cloned.1.call-update) | async-done | bytes 3932176 | tf_op jit(solution)/shard_map/all_gather | solution.py:84
  62.0 3.5 %multiply_reduce_fusion.1 = (f32[512]{0:T(512)S(1)}, f32[512,256]{0,1:T(8,128)S(1)}) fusion(bf16[512,3840]{0,1:T(8,128)(2,1)} %all-gather.3.cloned.1.call-done, bf16[3840,256]{1,0:T(8,128)(2,1)S(1)} %copy-done), kind=kOutput, calls=%fused_computation.69 | convolution fusion | flops 1006894592 | bytes 6424576 | tf_op jit(solution)/shard_map/dot_general | solution.py:86
  68.1 3.9 %collective-permute-start.1 = (bf16[512,2,1,256]{0,3,2,1:T(8,128)(2,1)S(1)}, bf16[512,2,1,256]{0,3,2,1:T(8,128)(2,1)S(1)}, u32[]{:S(2)}, u32[]{:S(2)}) collective-permute-start(bf16[512,2,1,256]{0,3,2,1:T(8,128)(2,1)S(1)} %pad_maximum_fusion.1), channel_id=1, source_target_pairs={{0,4},{4,8},{8,12},{12,16},{16,20},{20,24},{24,28},{28,32},{32,36}... | collective-permute-start | bytes 1572872 | tf_op jit(solution)/shard_map/ppermute | solution.py:18
  72.1 3.2 %collective-permute-start = (bf16[512,2,1,256]{0,3,2,1:T(8,128)(2,1)S(1)}, bf16[512,2,1,256]{0,3,2,1:T(8,128)(2,1)S(1)}, u32[]{:S(2)}, u32[]{:S(2)}) collective-permute-start(bf16[512,2,1,256]{0,3,2,1:T(8,128)(2,1)S(1)} %pad_maximum_fusion.1), channel_id=1, source_target_pairs={{0,8},{4,12},{8,16},{12,20},{16,24},{20,28},{24,32},{28,36},{32,40... | collective-permute-start | bytes 1572872 | tf_op jit(solution)/shard_map/ppermute | solution.py:18
  75.3 3.2 %fusion.77 = f32[512,512]{1,0:T(8,128)} fusion(bf16[512,3840]{0,1:T(8,128)(2,1)S(1)} %copy-done.2, bf16[3840,512]{1,0:T(8,128)(2,1)S(1)} %copy-done.1), kind=kOutput, calls=%fused_computation.115 | convolution fusion | flops 2013265920 | bytes 8912896 | tf_op jit(solution)/shard_map/dot_general | solution.py:85
  78.5 18.0 %collective-permute-done.1 = bf16[512,2,1,256]{0,3,2,1:T(8,128)(2,1)S(1)} collective-permute-done((bf16[512,2,1,256]{0,3,2,1:T(8,128)(2,1)S(1)}, bf16[512,2,1,256]{0,3,2,1:T(8,128)(2,1)S(1)}, u32[]{:S(2)}, u32[]{:S(2)}) %collective-permute-start.1) | collective-permute-done | bytes 524320 | tf_op jit(solution)/shard_map/ppermute | solution.py:18
  96.5 6.7 %collective-permute-done = bf16[512,2,1,256]{0,3,2,1:T(8,128)(2,1)S(1)} collective-permute-done((bf16[512,2,1,256]{0,3,2,1:T(8,128)(2,1)S(1)}, bf16[512,2,1,256]{0,3,2,1:T(8,128)(2,1)S(1)}, u32[]{:S(2)}, u32[]{:S(2)}) %collective-permute-start) | collective-permute-done | bytes 524320 | tf_op jit(solution)/shard_map/ppermute | solution.py:18
  104.6 2.3 %fusion.35 = f32[64,1,16,64]{3,2,0,1:T(8,128)S(1)} fusion(bf16[64,1,16,960]{3,2,0,1:T(8,128)(2,1)} %bitcast.4, bf16[1,64,960]{2,1,0:T(8,128)(2,1)S(1)} %copy-done.8), kind=kOutput, calls=%fused_computation.36 | convolution fusion | flops 125829120 | bytes 2351104 | tf_op jit(solution)/shard_map/sacd,ard->sacr/dot_general | solution.py:136
  106.9 20.2 %all-reduce.3 = bf16[64,1,16,64]{3,2,0,1:T(8,128)(2,1)S(1)} all-reduce(f32[64,1,16,64]{3,2,0,1:T(8,128)S(1)} %fusion.35), channel_id=1, replica_groups=mesh['seq'=64,'tensor'=4] {'tensor'}, use_global_device_ids=true, to_apply=%region_4.5 | all-reduce | flops 65536 | bytes 393216 | tf_op jit(solution)/shard_map/psum | solution.py:139
  127.9 10.7 %all-to-all-start.1 = ((bf16[64,2,512]{2,1,0:T(2,128)(2,1)}), bf16[64,2,512]{2,1,0:T(2,128)(2,1)S(1)}, u32[]{:S(2)}, u32[]{:S(2)}) async-start(bf16[64,2,512]{2,1,0:T(2,128)(2,1)} %reshape.369), calls=%async_computation.1 | async-start | bytes 262144 | tf_op jit(solution)/shard_map/all_to_all | solution.py:141
  140.4 8.6 %all-to-all-done.1 = bf16[64,2,512]{2,1,0:T(2,128)(2,1)S(1)} async-done(((bf16[64,2,512]{2,1,0:T(2,128)(2,1)}), bf16[64,2,512]{2,1,0:T(2,128)(2,1)S(1)}, u32[]{:S(2)}, u32[]{:S(2)}) %all-to-all-start.1) | async-done | bytes 131104 | tf_op jit(solution)/shard_map/all_to_all | solution.py:141
  149.3 2.9 %convolution_convert_fusion = bf16[64,16,512]{2,1,0:T(8,128)(2,1)S(1)} fusion(bf16[64,16,64]{2,1,0:T(8,128)(2,1)S(1)} %reshape.370, bf16[64,64,512]{2,1,0:T(8,128)(2,1)} %all-gather.5.cloned.1.call-done), kind=kOutput, calls=%fused_computation.30 | convolution fusion | flops 67633152 | bytes 5373952 | tf_op jit(solution)/shard_map/acr,are->ace/dot_general | solution.py:144
  154.6 2.6 %multiply_reduce_fusion = f32[512,2]{1,0:T(8,128)} fusion(f32[512,2,256]{2,1,0:T(2,128)} %reshape.356), kind=kLoop, calls=%fused_computation.46 | loop fusion | flops 523264 | bytes 1052672 | tf_op jit(solution)/shard_map/jvp()/reduce_sum | solution.py:22
  161.8 2.5 %fusion = (f32[2,512]{1,0:T(2,128)S(1)}, f32[1536,512,2]{1,0,2:T(8,128)S(1)}) fusion(f32[2,512]{1,0:T(2,128)S(1)} %get-tuple-element.36, f32[1536,512,2]{1,0,2:T(8,128)S(1)} %get-tuple-element.37, pred[512,1536]{0,1:T(8,128)(4,1)S(1)} %copy-done.5, bf16[64,2,8,256]{3,2,1,0:T(8,128)(2,1)S(1)} %bitcast.183, bf16[1536,1,256]{0,2,1:T(8,128)(2,1)S(1)} %copy-done.6), kind=kOutput, calls=%fused_computation.3 | convolution fusion | flops 813169664 | bytes 14688256 | tf_op jit(solution)/shard_map/tngd,knd->ngtk/dot_general | solution.py:56
  164.4 2.7 %fusion.26 = f32[512,2,256]{2,0,1:T(8,128)S(1)} fusion(f32[1536,512,2]{1,0,2:T(8,128)S(1)} %get-tuple-element.39, f32[2,512]{1,0:T(2,128)S(1)} %get-tuple-element.38, f32[2,512]{1,0:T(2,128)S(1)} %get-tuple-element.36, f32[1536,512,2]{1,0,2:T(8,128)S(1)} %get-tuple-element.37, pred[512,1536]{0,1:T(8,128)(4,1)S(1)} %copy-done.5, ...), kind=kOutput, calls=%fused_computation.31 | convolution fusion | flops 816316416 | bytes 15212544 | tf_op jit(solution)/shard_map/ngtk,knd->tngd/dot_general | solution.py:59
  171.8 4.9 %all-to-all-start.2 = ((bf16[64,16,512]{2,1,0:T(8,128)(2,1)}), bf16[64,16,512]{2,1,0:T(8,128)(2,1)S(1)}, u32[]{:S(2)}, u32[]{:S(2)}) async-start(bf16[64,16,512]{2,1,0:T(8,128)(2,1)} %bitcast.174), calls=%async_computation.2 | async-start | bytes 2097152 | tf_op jit(solution)/shard_map/all_to_all | solution.py:166
  176.7 6.1 %fusion.32 = bf16[256,2,512]{2,0,1:T(8,128)(2,1)} fusion(f32[2,512]{1,0:T(2,128)S(1)} %get-tuple-element.36, f32[1536,512,2]{1,0,2:T(8,128)} %copy-done.14, pred[512,1536]{0,1:T(8,128)(4,1)} %fusion.16, bf16[1536,1,256]{0,2,1:T(8,128)(2,1)} %get-tuple-element.7), kind=kOutput, calls=%fused_computation.35 | convolution fusion | flops 811859968 | bytes 8392704 | tf_op jit(solution)/shard_map/ngtk,knd->tngd/dot_general | solution.py:55
  184.8 20.4 %all-to-all-done.2 = bf16[64,16,512]{2,1,0:T(8,128)(2,1)S(1)} async-done(((bf16[64,16,512]{2,1,0:T(8,128)(2,1)}), bf16[64,16,512]{2,1,0:T(8,128)(2,1)S(1)}, u32[]{:S(2)}, u32[]{:S(2)}) %all-to-all-start.2) | async-done | bytes 1048608 | tf_op jit(solution)/shard_map/all_to_all | solution.py:166
  (78 shorter events, 26.6 us)
Async XLA Ops:
  7.2 54.8 %copy-start = (bf16[3840,256]{1,0:T(8,128)(2,1)S(1)}, bf16[3840,256]{1,0:T(8,128)(2,1)}, u32[]{:S(2)}) copy-start(bf16[3840,256]{1,0:T(8,128)(2,1)} %param.13) | copy-start | bytes 5898244
  7.2 54.8 %all-gather.3.cloned.1.call-start = ((), (), s32[]{:S(2)}) async-start(), calls=%async_computation.3 | async-start | bytes 4915200 | tf_op jit(solution)/shard_map/all_gather | solution.py:84
  7.9 141.3 %all-gather.5.cloned.1.call-start = ((), (), s32[]{:S(2)}) async-start(), calls=%async_computation.4 | async-start | bytes 4259840 | tf_op jit(solution)/shard_map/all_gather | solution.py:140
  8.7 30.4 %collective-permute-start.2 = (s32[512]{0:T(512)}, s32[512]{0:T(512)S(1)}, u32[]{:S(2)}, u32[]{:S(2)}) collective-permute-start(s32[512]{0:T(512)} %param.20), channel_id=1, source_target_pairs={{0,8},{4,12},{8,16},{12,20},{16,24},{20,28},{24,32},{28,36},{32,40... | collective-permute-start | bytes 6152 | tf_op jit(solution)/shard_map/ppermute | solution.py:18
  13.0 26.0 %collective-permute-start.3 = (s32[512]{0:T(512)}, s32[512]{0:T(512)S(1)}, u32[]{:S(2)}, u32[]{:S(2)}) collective-permute-start(s32[512]{0:T(512)} %param.20), channel_id=1, source_target_pairs={{0,4},{4,8},{8,12},{12,16},{16,20},{20,24},{24,28},{28,32},{32,36}... | collective-permute-start | bytes 6152 | tf_op jit(solution)/shard_map/ppermute | solution.py:18
  24.8 14.2 %copy-start.10 = (s32[512]{0:T(512)S(1)}, s32[512]{0:T(512)}, u32[]{:S(2)}) copy-start(s32[512]{0:T(512)} %param.20) | copy-start | bytes 6148
  28.8 75.8 %all-to-all-start = ((bf16[64,16,960]{2,1,0:T(8,128)(2,1)}), bf16[64,16,960]{2,1,0:T(8,128)(2,1)}, u32[]{:S(2)}, u32[]{:S(2)}) async-start(bf16[64,16,960]{2,1,0:T(8,128)(2,1)} %bitcast.170), calls=%async_computation | async-start | bytes 4194304 | tf_op jit(solution)/shard_map/all_to_all | solution.py:99
  41.6 23.9 %copy-start.11 = (f32[256]{0:T(256)S(1)}, f32[256]{0:T(256)}, u32[]{:S(2)}) copy-start(f32[256]{0:T(256)} %param.16) | copy-start | bytes 3076
  62.0 4.8 %copy-start.2 = (bf16[512,3840]{0,1:T(8,128)(2,1)S(1)}, bf16[512,3840]{0,1:T(8,128)(2,1)}, u32[]{:S(2)}) copy-start(bf16[512,3840]{0,1:T(8,128)(2,1)} %all-gather.3.cloned.1.call-done) | copy-start | bytes 11796484
  62.0 4.8 %copy-start.12 = (bf16[3840,256]{1,0:T(8,128)(2,1)S(1)}, bf16[3840,256]{1,0:T(8,128)(2,1)}, u32[]{:S(2)}) copy-start(bf16[3840,256]{1,0:T(8,128)(2,1)} %param.14) | copy-start | bytes 5898244
  66.8 8.4 %copy-start.1 = (bf16[3840,512]{1,0:T(8,128)(2,1)S(1)}, bf16[3840,512]{1,0:T(8,128)(2,1)}, u32[]{:S(2)}) copy-start(bf16[3840,512]{1,0:T(8,128)(2,1)} %param.12) | copy-start | bytes 11796484
  68.1 28.4 %collective-permute-start.1 = (bf16[512,2,1,256]{0,3,2,1:T(8,128)(2,1)S(1)}, bf16[512,2,1,256]{0,3,2,1:T(8,128)(2,1)S(1)}, u32[]{:S(2)}, u32[]{:S(2)}) collective-permute-start(bf16[512,2,1,256]{0,3,2,1:T(8,128)(2,1)S(1)} %pad_maximum_fusion.1), channel_id=1, source_target_pairs={{0,4},{4,8},{8,12},{12,16},{16,20},{20,24},{24,28},{28,32},{32,36}... | collective-permute-start | bytes 1572872 | tf_op jit(solution)/shard_map/ppermute | solution.py:18
  72.1 31.2 %collective-permute-start = (bf16[512,2,1,256]{0,3,2,1:T(8,128)(2,1)S(1)}, bf16[512,2,1,256]{0,3,2,1:T(8,128)(2,1)S(1)}, u32[]{:S(2)}, u32[]{:S(2)}) collective-permute-start(bf16[512,2,1,256]{0,3,2,1:T(8,128)(2,1)S(1)} %pad_maximum_fusion.1), channel_id=1, source_target_pairs={{0,8},{4,12},{8,16},{12,20},{16,24},{20,28},{24,32},{28,36},{32,40... | collective-permute-start | bytes 1572872 | tf_op jit(solution)/shard_map/ppermute | solution.py:18
  78.5 26.1 %copy-start.8 = (bf16[1,64,960]{2,1,0:T(8,128)(2,1)S(1)}, bf16[1,64,960]{2,1,0:T(8,128)(2,1)}, u32[]{:S(2)}) copy-start(bf16[1,64,960]{2,1,0:T(8,128)(2,1)} %param.17) | copy-start | bytes 368644
  127.9 21.1 %all-to-all-start.1 = ((bf16[64,2,512]{2,1,0:T(2,128)(2,1)}), bf16[64,2,512]{2,1,0:T(2,128)(2,1)S(1)}, u32[]{:S(2)}, u32[]{:S(2)}) async-start(bf16[64,2,512]{2,1,0:T(2,128)(2,1)} %reshape.369), calls=%async_computation.1 | async-start | bytes 262144 | tf_op jit(solution)/shard_map/all_to_all | solution.py:141
  149.2 3.0 %copy-start.4 = (f32[512,512]{1,0:T(8,128)S(1)}, f32[512,512]{1,0:T(8,128)}, u32[]{:S(2)}) copy-start(f32[512,512]{1,0:T(8,128)} %fusion.77) | copy-start | bytes 3145732
  152.2 6.1 %copy-start.9 = (f32[256]{0:T(256)S(1)}, f32[256]{0:T(256)}, u32[]{:S(2)}) copy-start(f32[256]{0:T(256)} %param.15) | copy-start | bytes 3076
  158.2 1.5 copy-start.5
  158.2 1.5 copy-start.7
  159.7 2.1 copy-start.6
  159.7 2.1 copy-start.13
  161.8 2.7 %copy-start.14 = (f32[1536,512,2]{1,0,2:T(8,128)}, f32[1536,512,2]{1,0,2:T(8,128)S(1)}, u32[]{:S(2)}) copy-start(f32[1536,512,2]{1,0,2:T(8,128)S(1)} %get-tuple-element.37) | copy-start | bytes 18874372
  164.4 2.7 %copy-start.3 = (f32[512,128]{1,0:T(8,128)S(1)}, f32[512,128]{1,0:T(8,128)}, u32[]{:S(2)}) copy-start(f32[512,128]{1,0:T(8,128)} %get-tuple-element.33) | copy-start | bytes 786436
  171.8 33.4 %all-to-all-start.2 = ((bf16[64,16,512]{2,1,0:T(8,128)(2,1)}), bf16[64,16,512]{2,1,0:T(8,128)(2,1)S(1)}, u32[]{:S(2)}, u32[]{:S(2)}) async-start(bf16[64,16,512]{2,1,0:T(8,128)(2,1)} %bitcast.174), calls=%async_computation.2 | async-start | bytes 2097152 | tf_op jit(solution)/shard_map/all_to_all | solution.py:166
Sparse Core Ops, SparseCore 0:
  9.8 52.1 all-gather.2
  64.8 81.3 all-gather.4

commit v7 on v5

--- a/solution.py
+++ b/solution.py
@@ -104,22 +104,13 @@
     )
     values = value_lin.astype(jnp.bfloat16).reshape(tok_count, kv_heads, HD)
     rim_count = WINDOW // tok_count
-    key_list = []
-    value_list = []
     doc_list = []
     place_list = []
     for distance in range(rim_count, 0, -1):
-        far_keys, far_values, far_docs = passed_along((key_rows, values, doc_ids), "seq", distance)
-        key_list.append(far_keys)
-        value_list.append(far_values)
-        doc_list.append(far_docs)
+        doc_list.append(passed_along(doc_ids, "seq", distance))
         place_list.append(positions - distance * tok_count)
-    key_list.append(key_rows)
-    value_list.append(values)
     doc_list.append(doc_ids)
     place_list.append(positions)
-    window_keys = jnp.concatenate(key_list, axis=0)
-    window_values = jnp.concatenate(value_list, axis=0)
     key_docs = jnp.concatenate(doc_list, axis=0)
     key_pos = jnp.concatenate(place_list, axis=0)
     key_gap = positions[:, None] - key_pos[None, :]
@@ -129,9 +120,20 @@
         & (key_gap < WINDOW)
         & (key_pos[None, :] >= 0)
     )
-    arrived, query_lin, window_keys, window_values, allowed = lax.optimization_barrier(
-        (arrived, query_lin, window_keys, window_values, allowed)
+    kv_rows = jnp.stack([key_rows, values], axis=1)
+    arrived, query_lin, kv_rows, allowed = lax.optimization_barrier(
+        (arrived, query_lin, kv_rows, allowed)
     )
+    key_list = []
+    value_list = []
+    for distance in range(rim_count, 0, -1):
+        far_kv = passed_along(kv_rows, "seq", distance)
+        key_list.append(far_kv[:, 0])
+        value_list.append(far_kv[:, 1])
+    key_list.append(kv_rows[:, 0])
+    value_list.append(kv_rows[:, 1])
+    window_keys = jnp.concatenate(key_list, axis=0)
+    window_values = jnp.concatenate(value_list, axis=0)
     partial_low = jnp.einsum(
         "sacd,ard->sacr", arrived, adapter_down, preferred_element_type=jnp.float32
     )

time: 215 us -> 215 us (level)
  local copies, waits for them, and re-layouts: 11.5 us -> 16.8 us
  waiting for transfers between devices: 68.3 us -> 64.6 us
    all_gather x1, waiting for transfers between devices: 20.4 us -> 0.01 us  [local(): shard_cols = lax.all_gather(tokens, 'tensor', axis=1, tiled=True)]
    ppermute x6 -> x4, waiting for transfers between devices: 17.5 us -> 35 us  [passed_along(): lax.ppermute(value, axis, [(source, source + steps) for source in range(f...]
    squeeze x0 -> x3, local copies, waits for them, and re-layouts: none -> 4.59 us  [the longest x2 3.73 us: local(): value_list.append(far_kv[:, 1])]
    ppermute x6 -> x4, starting transfers between devices: 21.6 us -> 18 us  [passed_along(): lax.ppermute(value, axis, [(source, source + steps) for source in range(f...]
    all_to_all x1, starting transfers between devices: 10.2 us -> 13.3 us  [local(): lax.all_to_all(outgoing, 'seq', 0, 0, tiled=True)]
    dot_general x1, matrix products: 4.1 us -> 1.23 us  [local(): value_lin = jnp.dot(shard_cols, w_value, preferred_element_type=jnp.float32)]
    dot_general x1, matrix products: 1.24 us -> 3.53 us  [local(): key_lin = jnp.dot(shard_cols, w_key, preferred_element_type=jnp.float32)]
  transfers between devices with their start and end apart: 11 -> 9, of which waited for: 7 -> 4; matrix products, arithmetic and copies ran while one was open for 18% -> 19% of each run, Pallas kernels for 0% -> 0%
where the time goes in v7:
time: 215 us; the launch traced here: 214 us
  waiting for transfers between devices  64.6 us (30%)
  starting transfers between devices  49.1 us (23%)
  matrix products  33.7 us (16%)
  blocking collectives  20.4 us (9%)
  local copies, waits for them, and re-layouts  16.8 us (8%)
  other arithmetic  14.6 us (7%)
  between operations  14.5 us (7%)
    ppermute x4, waiting for transfers between devices, passed_along(): lax.ppermute(value, axis, [(source, source + steps) for source in range(f...  35 us
    all_to_all x1, waiting for transfers between devices, local(): lax.all_to_all(out_grad, 'seq', 0, 0, tiled=True)  20.5 us
    psum x1, blocking collectives, local(): slot_low = lax.psum(partial_low, 'tensor').astype(jnp.bfloat16)  20.4 us
    ppermute x4, starting transfers between devices, passed_along(): lax.ppermute(value, axis, [(source, source + steps) for source in range(f...  18 us
    all_to_all x1, starting transfers between devices, local(): lax.all_to_all(outgoing, 'seq', 0, 0, tiled=True)  13.3 us
    all_to_all x1, starting transfers between devices, local(): lax.all_to_all(slot_low.reshape(seq_count * own_adapters * CAP, R), 'seq'...  11.9 us
    all_to_all x1, waiting for transfers between devices, local(): lax.all_to_all(slot_low.reshape(seq_count * own_adapters * CAP, R), 'seq'...  7.67 us
    dot_general x1, matrix products, attend(): jnp.einsum('ngtk,knd->tngd', probs_low, values, preferred_element_type=jn...  5.92 us
  transfers between devices with their start and end apart: 9, of which 4 were waited for; matrix products, arithmetic and copies ran while one was open for 19% of the time, Pallas kernels for 0%

profile of v7, /device:TPU:1, one launch (start us, length us, event | category | flops | bytes accessed | tf_op | source)
XLA Modules:
  0.0 213.7 jit_solution(7922960048282562399)
XLA Ops:
  12.3 3.8 %fusion.24 = bf16[1024,960]{0,1:T(8,128)(2,1)} fusion(bf16[512,960]{0,1:T(8,128)(2,1)} %param.11, s32[512]{0:T(512)S(1)} %multiply_add_fusion.3), kind=kOutput, calls=%fused_computation.27 | convolution fusion | flops 1008140288 | bytes 2951168 | tf_op jit(solution)/shard_map/dot_general | solution.py:96
  16.1 3.9 %copy.84 = bf16[1024,960]{1,0:T(8,128)(2,1)} copy(bf16[1024,960]{0,1:T(8,128)(2,1)} %fusion.24) | data formatting | bytes 3932160 | tf_op jit(solution)/shard_map/convert_element_type | solution.py:96
  20.0 13.3 %all-to-all-start = ((bf16[64,16,960]{2,1,0:T(8,128)(2,1)}), bf16[64,16,960]{2,1,0:T(8,128)(2,1)}, u32[]{:S(2)}, u32[]{:S(2)}) async-start(bf16[64,16,960]{2,1,0:T(8,128)(2,1)} %bitcast.174), calls=%async_computation | async-start | bytes 4194304 | tf_op jit(solution)/shard_map/all_to_all | solution.py:99
  33.4 3.3 %collective-permute-start = (s32[512]{0:T(512)S(1)}, s32[512]{0:T(512)S(1)}, u32[]{:S(2)}, u32[]{:S(2)}) collective-permute-start(s32[512]{0:T(512)S(1)} %copy-done.15), channel_id=1, source_target_pairs={{0,8},{4,12},{8,16},{12,20},{16,24},{20,28},{24,32},{28,36},{32,40... | collective-permute-start | bytes 6152 | tf_op jit(solution)/shard_map/ppermute | solution.py:18
  36.6 3.7 %collective-permute-start.1 = (s32[512]{0:T(512)S(1)}, s32[512]{0:T(512)S(1)}, u32[]{:S(2)}, u32[]{:S(2)}) collective-permute-start(s32[512]{0:T(512)S(1)} %copy-done.15), channel_id=1, source_target_pairs={{0,4},{4,8},{8,12},{12,16},{16,20},{20,24},{24,28},{28,32},{32,36}... | collective-permute-start | bytes 6152 | tf_op jit(solution)/shard_map/ppermute | solution.py:18
  40.4 34.9 %collective-permute-done = s32[512]{0:T(512)S(1)} collective-permute-done((s32[512]{0:T(512)S(1)}, s32[512]{0:T(512)S(1)}, u32[]{:S(2)}, u32[]{:S(2)}) %collective-permute-start) | collective-permute-done | bytes 2080 | tf_op jit(solution)/shard_map/ppermute | solution.py:18
  75.4 2.5 %fusion.16 = pred[512,1536]{0,1:T(8,128)(4,1)} fusion(s32[1536]{0:T(1024)S(1)} %pad_add_fusion.1, s32[512]{0:T(512)S(1)} %iota_add_fusion, s32[512]{0:T(512)S(1)} %copy-done.15, s32[1536]{0:T(1024)S(1)} %pad_add_fusion, pred[1536]{0:T(1024)(128)(4,1)S(1)} %broadcast_compare_fusion), kind=kLoop, calls=%fused_computation.20 | loop fusion | flops 5505024 | bytes 804352 | tf_op jit(solution)/shard_map/and | solution.py:118
  77.8 3.5 %multiply_reduce_fusion.1 = (f32[512]{0:T(512)S(1)}, f32[512,256]{0,1:T(8,128)S(1)}) fusion(bf16[512,3840]{0,1:T(8,128)(2,1)} %all-gather.3.cloned.1.call-done, bf16[3840,256]{1,0:T(8,128)(2,1)S(1)} %copy-done), kind=kOutput, calls=%fused_computation.66 | convolution fusion | flops 1006894592 | bytes 6424576 | tf_op jit(solution)/shard_map/dot_general | solution.py:86
  84.9 3.2 %fusion.79 = f32[512,512]{1,0:T(8,128)} fusion(bf16[512,3840]{0,1:T(8,128)(2,1)S(1)} %copy-done.2, bf16[3840,512]{1,0:T(8,128)(2,1)S(1)} %copy-done.1), kind=kOutput, calls=%fused_computation.119 | convolution fusion | flops 2013265920 | bytes 8912896 | tf_op jit(solution)/shard_map/dot_general | solution.py:85
  88.1 6.3 %collective-permute-start.3 = (bf16[512,2,1,256]{0,3,2,1:T(8,128)(2,1)S(1)}, bf16[512,2,1,256]{0,3,2,1:T(8,128)(2,1)}, u32[]{:S(2)}, u32[]{:S(2)}) collective-permute-start(bf16[512,2,1,256]{0,3,2,1:T(8,128)(2,1)S(1)} %pad_maximum_fusion), channel_id=1, source_target_pairs={{0,4},{4,8},{8,12},{12,16},{16,20},{20,24},{24,28},{28,32},{32,36}... | collective-permute-start | bytes 1572872 | tf_op jit(solution)/shard_map/ppermute | solution.py:18
  94.4 4.8 %collective-permute-start.2 = (bf16[512,2,1,256]{0,3,2,1:T(8,128)(2,1)S(1)}, bf16[512,2,1,256]{0,3,2,1:T(8,128)(2,1)}, u32[]{:S(2)}, u32[]{:S(2)}) collective-permute-start(bf16[512,2,1,256]{0,3,2,1:T(8,128)(2,1)S(1)} %pad_maximum_fusion), channel_id=1, source_target_pairs={{0,8},{4,12},{8,16},{12,20},{16,24},{20,28},{24,32},{28,36},{32,40... | collective-permute-start | bytes 1572872 | tf_op jit(solution)/shard_map/ppermute | solution.py:18
  99.2 2.3 %fusion.35 = f32[64,1,16,64]{3,2,0,1:T(8,128)S(1)} fusion(bf16[64,1,16,960]{3,2,0,1:T(8,128)(2,1)} %bitcast.4, bf16[1,64,960]{2,1,0:T(8,128)(2,1)S(1)} %copy-done.13), kind=kOutput, calls=%fused_computation.36 | convolution fusion | flops 125829120 | bytes 2351104 | tf_op jit(solution)/shard_map/sacd,ard->sacr/dot_general | solution.py:137
  101.5 20.4 %all-reduce.3 = bf16[64,1,16,64]{3,2,0,1:T(8,128)(2,1)S(1)} all-reduce(f32[64,1,16,64]{3,2,0,1:T(8,128)S(1)} %fusion.35), channel_id=1, replica_groups=mesh['seq'=64,'tensor'=4] {'tensor'}, use_global_device_ids=true, to_apply=%region_4.5 | all-reduce | flops 65536 | bytes 393216 | tf_op jit(solution)/shard_map/psum | solution.py:140
  122.8 11.9 %all-to-all-start.1 = ((bf16[64,2,512]{2,1,0:T(2,128)(2,1)}), bf16[64,2,512]{2,1,0:T(2,128)(2,1)S(1)}, u32[]{:S(2)}, u32[]{:S(2)}) async-start(bf16[64,2,512]{2,1,0:T(2,128)(2,1)} %reshape.344), calls=%async_computation.1 | async-start | bytes 262144 | tf_op jit(solution)/shard_map/all_to_all | solution.py:142
  137.3 7.7 %all-to-all-done.1 = bf16[64,2,512]{2,1,0:T(2,128)(2,1)S(1)} async-done(((bf16[64,2,512]{2,1,0:T(2,128)(2,1)}), bf16[64,2,512]{2,1,0:T(2,128)(2,1)S(1)}, u32[]{:S(2)}, u32[]{:S(2)}) %all-to-all-start.1) | async-done | bytes 131104 | tf_op jit(solution)/shard_map/all_to_all | solution.py:142
  148.9 2.9 %convolution_convert_fusion = bf16[64,16,512]{2,1,0:T(8,128)(2,1)S(1)} fusion(bf16[64,16,64]{2,1,0:T(8,128)(2,1)S(1)} %reshape.345, bf16[64,64,512]{2,1,0:T(8,128)(2,1)} %all-gather.5.cloned.1.call-done), kind=kOutput, calls=%fused_computation.30 | convolution fusion | flops 67633152 | bytes 5373952 | tf_op jit(solution)/shard_map/acr,are->ace/dot_general | solution.py:145
  154.3 2.6 %multiply_reduce_fusion = f32[512,2]{1,0:T(8,128)} fusion(f32[512,2,256]{2,1,0:T(2,128)} %reshape.331), kind=kLoop, calls=%fused_computation.47 | loop fusion | flops 523264 | bytes 1052672 | tf_op jit(solution)/shard_map/jvp()/reduce_sum | solution.py:22
  159.5 2.1 fusion.5
  161.6 2.5 %fusion = (f32[2,512]{1,0:T(2,128)S(1)}, f32[1536,512,2]{1,0,2:T(8,128)S(1)}) fusion(f32[2,512]{1,0:T(2,128)S(1)} %get-tuple-element.36, f32[1536,512,2]{1,0,2:T(8,128)S(1)} %get-tuple-element.37, pred[512,1536]{0,1:T(8,128)(4,1)S(1)} %copy-done.5, bf16[64,2,8,256]{3,2,1,0:T(8,128)(2,1)S(1)} %bitcast.183, bf16[512,1,256]{0,2,1:T(8,128)(2,1)S(1)} %copy-done.6, ...), kind=kOutput, calls=%fused_computation.3 | convolution fusion | flops 815528960 | bytes 14688256 | tf_op jit(solution)/shard_map/tngd,knd->ngtk/dot_general | solution.py:56
  164.2 2.7 %fusion.26 = f32[512,2,256]{2,0,1:T(8,128)S(1)} fusion(f32[1536,512,2]{1,0,2:T(8,128)S(1)} %get-tuple-element.39, f32[2,512]{1,0:T(2,128)S(1)} %get-tuple-element.38, f32[2,512]{1,0:T(2,128)S(1)} %get-tuple-element.36, f32[1536,512,2]{1,0,2:T(8,128)S(1)} %get-tuple-element.37, pred[512,1536]{0,1:T(8,128)(4,1)S(1)} %copy-done.5, ...), kind=kOutput, calls=%fused_computation.31 | convolution fusion | flops 818675712 | bytes 15212544 | tf_op jit(solution)/shard_map/ngtk,knd->tngd/dot_general | solution.py:59
  171.6 5.8 %all-to-all-start.2 = ((bf16[64,16,512]{2,1,0:T(8,128)(2,1)}), bf16[64,16,512]{2,1,0:T(8,128)(2,1)S(1)}, u32[]{:S(2)}, u32[]{:S(2)}) async-start(bf16[64,16,512]{2,1,0:T(8,128)(2,1)} %bitcast.176), calls=%async_computation.2 | async-start | bytes 2097152 | tf_op jit(solution)/shard_map/all_to_all | solution.py:167
  177.4 5.9 %fusion.32 = bf16[256,2,512]{2,0,1:T(8,128)(2,1)} fusion(f32[2,512]{1,0:T(2,128)S(1)} %get-tuple-element.36, f32[1536,512,2]{1,0,2:T(8,128)} %copy-done.19, pred[512,1536]{0,1:T(8,128)(4,1)} %fusion.16, bf16[512,1,256]{0,2,1:T(8,128)(2,1)S(1)} %copy-done.7, bf16[512,1,256]{0,2,1:T(8,128)(2,1)} %get-tuple-element.28, bf16[512,1,256]{0,2,1:T(8,128)(2,1)} %get-tuple-element.26), kind=kOutput, calls=%fused_computation.35 | convolution fusion | flops 814219264 | bytes 8392704 | tf_op jit(solution)/shard_map/ngtk,knd->tngd/dot_general | solution.py:55
  183.3 2.0 copy.98
  185.4 20.5 %all-to-all-done.2 = bf16[64,16,512]{2,1,0:T(8,128)(2,1)S(1)} async-done(((bf16[64,16,512]{2,1,0:T(8,128)(2,1)}), bf16[64,16,512]{2,1,0:T(8,128)(2,1)S(1)}, u32[]{:S(2)}, u32[]{:S(2)}) %all-to-all-start.2) | async-done | bytes 1048608 | tf_op jit(solution)/shard_map/all_to_all | solution.py:167
  (88 shorter events, 26.6 us)
Async XLA Ops:
  7.2 70.7 %copy-start = (bf16[3840,256]{1,0:T(8,128)(2,1)S(1)}, bf16[3840,256]{1,0:T(8,128)(2,1)}, u32[]{:S(2)}) copy-start(bf16[3840,256]{1,0:T(8,128)(2,1)} %param.13) | copy-start | bytes 5898244
  7.2 70.7 %all-gather.3.cloned.1.call-start = ((), (), s32[]{:S(2)}) async-start(), calls=%async_computation.3 | async-start | bytes 4915200 | tf_op jit(solution)/shard_map/all_gather | solution.py:84
  7.9 141.0 %all-gather.5.cloned.1.call-start = ((), (), s32[]{:S(2)}) async-start(), calls=%async_computation.4 | async-start | bytes 4259840 | tf_op jit(solution)/shard_map/all_gather | solution.py:141
  16.1 17.3 %copy-start.15 = (s32[512]{0:T(512)S(1)}, s32[512]{0:T(512)}, u32[]{:S(2)}) copy-start(s32[512]{0:T(512)} %param.20) | copy-start | bytes 6148
  20.0 68.0 %all-to-all-start = ((bf16[64,16,960]{2,1,0:T(8,128)(2,1)}), bf16[64,16,960]{2,1,0:T(8,128)(2,1)}, u32[]{:S(2)}, u32[]{:S(2)}) async-start(bf16[64,16,960]{2,1,0:T(8,128)(2,1)} %bitcast.174), calls=%async_computation | async-start | bytes 4194304 | tf_op jit(solution)/shard_map/all_to_all | solution.py:99
  33.4 41.9 %collective-permute-start = (s32[512]{0:T(512)S(1)}, s32[512]{0:T(512)S(1)}, u32[]{:S(2)}, u32[]{:S(2)}) collective-permute-start(s32[512]{0:T(512)S(1)} %copy-done.15), channel_id=1, source_target_pairs={{0,8},{4,12},{8,16},{12,20},{16,24},{20,28},{24,32},{28,36},{32,40... | collective-permute-start | bytes 6152 | tf_op jit(solution)/shard_map/ppermute | solution.py:18
  36.6 38.7 %collective-permute-start.1 = (s32[512]{0:T(512)S(1)}, s32[512]{0:T(512)S(1)}, u32[]{:S(2)}, u32[]{:S(2)}) collective-permute-start(s32[512]{0:T(512)S(1)} %copy-done.15), channel_id=1, source_target_pairs={{0,4},{4,8},{8,12},{12,16},{16,20},{20,24},{24,28},{28,32},{32,36}... | collective-permute-start | bytes 6152 | tf_op jit(solution)/shard_map/ppermute | solution.py:18
  77.8 3.6 %copy-start.16 = (f32[256]{0:T(256)S(1)}, f32[256]{0:T(256)}, u32[]{:S(2)}) copy-start(f32[256]{0:T(256)} %param.16) | copy-start | bytes 3076
  77.8 4.9 %copy-start.2 = (bf16[512,3840]{0,1:T(8,128)(2,1)S(1)}, bf16[512,3840]{0,1:T(8,128)(2,1)}, u32[]{:S(2)}) copy-start(bf16[512,3840]{0,1:T(8,128)(2,1)} %all-gather.3.cloned.1.call-done) | copy-start | bytes 11796484
  77.8 4.9 %copy-start.17 = (bf16[3840,256]{1,0:T(8,128)(2,1)S(1)}, bf16[3840,256]{1,0:T(8,128)(2,1)}, u32[]{:S(2)}) copy-start(bf16[3840,256]{1,0:T(8,128)(2,1)} %param.14) | copy-start | bytes 5898244
  84.9 14.3 %copy-start.13 = (bf16[1,64,960]{2,1,0:T(8,128)(2,1)S(1)}, bf16[1,64,960]{2,1,0:T(8,128)(2,1)}, u32[]{:S(2)}) copy-start(bf16[1,64,960]{2,1,0:T(8,128)(2,1)} %param.17) | copy-start | bytes 368644
  88.1 57.1 %collective-permute-start.3 = (bf16[512,2,1,256]{0,3,2,1:T(8,128)(2,1)S(1)}, bf16[512,2,1,256]{0,3,2,1:T(8,128)(2,1)}, u32[]{:S(2)}, u32[]{:S(2)}) collective-permute-start(bf16[512,2,1,256]{0,3,2,1:T(8,128)(2,1)S(1)} %pad_maximum_fusion), channel_id=1, source_target_pairs={{0,4},{4,8},{8,12},{12,16},{16,20},{20,24},{24,28},{28,32},{32,36}... | collective-permute-start | bytes 1572872 | tf_op jit(solution)/shard_map/ppermute | solution.py:18
  94.4 52.7 %collective-permute-start.2 = (bf16[512,2,1,256]{0,3,2,1:T(8,128)(2,1)S(1)}, bf16[512,2,1,256]{0,3,2,1:T(8,128)(2,1)}, u32[]{:S(2)}, u32[]{:S(2)}) collective-permute-start(bf16[512,2,1,256]{0,3,2,1:T(8,128)(2,1)S(1)} %pad_maximum_fusion), channel_id=1, source_target_pairs={{0,8},{4,12},{8,16},{12,20},{16,24},{20,28},{24,32},{28,36},{32,40... | collective-permute-start | bytes 1572872 | tf_op jit(solution)/shard_map/ppermute | solution.py:18
  122.8 22.2 %all-to-all-start.1 = ((bf16[64,2,512]{2,1,0:T(2,128)(2,1)}), bf16[64,2,512]{2,1,0:T(2,128)(2,1)S(1)}, u32[]{:S(2)}, u32[]{:S(2)}) async-start(bf16[64,2,512]{2,1,0:T(2,128)(2,1)} %reshape.344), calls=%async_computation.1 | async-start | bytes 262144 | tf_op jit(solution)/shard_map/all_to_all | solution.py:142
  148.9 3.0 %copy-start.4 = (f32[512,512]{1,0:T(8,128)S(1)}, f32[512,512]{1,0:T(8,128)}, u32[]{:S(2)}) copy-start(f32[512,512]{1,0:T(8,128)} %fusion.79) | copy-start | bytes 3145732
  151.9 6.1 %copy-start.14 = (f32[256]{0:T(256)S(1)}, f32[256]{0:T(256)}, u32[]{:S(2)}) copy-start(f32[256]{0:T(256)} %param.15) | copy-start | bytes 3076
  159.4 2.2 %copy-start.6 = (bf16[512,1,256]{0,2,1:T(8,128)(2,1)S(1)}, bf16[512,1,256]{0,2,1:T(8,128)(2,1)}, u32[]{:S(2)}) copy-start(bf16[512,1,256]{0,2,1:T(8,128)(2,1)} %get-tuple-element.30) | copy-start | bytes 786436
  159.4 2.2 %copy-start.8 = (bf16[512,1,256]{0,2,1:T(8,128)(2,1)S(1)}, bf16[512,1,256]{0,2,1:T(8,128)(2,1)}, u32[]{:S(2)}) copy-start(bf16[512,1,256]{0,2,1:T(8,128)(2,1)} %get-tuple-element.28) | copy-start | bytes 786436
  159.4 2.2 %copy-start.9 = (bf16[512,1,256]{0,2,1:T(8,128)(2,1)S(1)}, bf16[512,1,256]{0,2,1:T(8,128)(2,1)}, u32[]{:S(2)}) copy-start(bf16[512,1,256]{0,2,1:T(8,128)(2,1)} %get-tuple-element.26) | copy-start | bytes 786436
  159.5 2.2 %copy-start.18 = (bf16[512,512]{1,0:T(8,128)(2,1)S(1)}, bf16[512,512]{1,0:T(8,128)(2,1)}, u32[]{:S(2)}) copy-start(bf16[512,512]{1,0:T(8,128)(2,1)} %param.21) | copy-start | bytes 1572868
  161.6 2.7 %copy-start.19 = (f32[1536,512,2]{1,0,2:T(8,128)}, f32[1536,512,2]{1,0,2:T(8,128)S(1)}, u32[]{:S(2)}) copy-start(f32[1536,512,2]{1,0,2:T(8,128)S(1)} %get-tuple-element.37) | copy-start | bytes 18874372
  164.2 2.8 %copy-start.3 = (f32[512,128]{1,0:T(8,128)S(1)}, f32[512,128]{1,0:T(8,128)}, u32[]{:S(2)}) copy-start(f32[512,128]{1,0:T(8,128)} %get-tuple-element.33) | copy-start | bytes 786436
  167.4 10.0 %copy-start.7 = (bf16[512,1,256]{0,2,1:T(8,128)(2,1)S(1)}, bf16[512,1,256]{0,2,1:T(8,128)(2,1)}, u32[]{:S(2)}) copy-start(bf16[512,1,256]{0,2,1:T(8,128)(2,1)} %get-tuple-element.30) | copy-start | bytes 786436
  171.6 34.3 %all-to-all-start.2 = ((bf16[64,16,512]{2,1,0:T(8,128)(2,1)}), bf16[64,16,512]{2,1,0:T(8,128)(2,1)S(1)}, u32[]{:S(2)}, u32[]{:S(2)}) async-start(bf16[64,16,512]{2,1,0:T(8,128)(2,1)} %bitcast.176), calls=%async_computation.2 | async-start | bytes 2097152 | tf_op jit(solution)/shard_map/all_to_all | solution.py:167
  (5 other events, 8.1 us)
Sparse Core Ops, SparseCore 0:
  9.8 52.1 all-gather.2
  64.8 80.6 all-gather.4

commit v8 on v6

--- a/solution.py
+++ b/solution.py
@@ -93,7 +93,12 @@
     dispatch = (slot_index[None, :] == jnp.arange(ADAPTERS * CAP, dtype=jnp.int32)[:, None]).astype(
         jnp.bfloat16
     )
-    outgoing = jnp.dot(dispatch, tokens, preferred_element_type=jnp.float32).astype(jnp.bfloat16)
+    dispatch_t = (slot_index[:, None] == jnp.arange(ADAPTERS * CAP, dtype=jnp.int32)[None, :]).astype(
+        jnp.bfloat16
+    )
+    outgoing = jnp.einsum(
+        "ts,td->sd", dispatch_t, tokens, preferred_element_type=jnp.bfloat16
+    )
     seq_count = lax.axis_size("seq")
     own_adapters = adapter_down.shape[0]
     arrived = lax.all_to_all(outgoing, "seq", 0, 0, tiled=True).reshape(

time: 214 us -> 212 us (level)
  local copies, waits for them, and re-layouts: 11.5 us -> 7.56 us
    convert_element_type x1 -> x0, local copies, waits for them, and re-layouts: 3.99 us -> none  [local(): jnp.dot(dispatch, tokens, preferred_element_type=jnp.float32)]
    unnamed x0 -> x1, matrix products: none -> 3.96 us
    ppermute x4, waiting for transfers between devices: 24.7 us -> 21 us  [passed_along(): lax.ppermute(value, axis, [(source, source + steps) for source in range(f...]
    dot_general x1 -> x0, matrix products: 3.71 us -> none  [local(): jnp.dot(dispatch, tokens, preferred_element_type=jnp.float32)]
    all_gather x1, waiting for transfers between devices: 20.4 us -> 24 us  [local(): shard_cols = lax.all_gather(tokens, 'tensor', axis=1, tiled=True)]
  transfers between devices with their start and end apart: 9 -> 9, of which waited for: 5 -> 6; matrix products, arithmetic and copies ran while one was open for 18% -> 16% of each run, Pallas kernels for 0% -> 0%
where the time goes in v8:
time: 212 us; the launch traced here: 211 us
  waiting for transfers between devices  75.6 us (36%)
  starting transfers between devices  43.1 us (20%)
  matrix products  33.9 us (16%)
  blocking collectives  20.2 us (10%)
  other arithmetic  15.9 us (8%)
  between operations  14.5 us (7%)
  local copies, waits for them, and re-layouts  7.56 us (4%)
    all_gather x1, waiting for transfers between devices, local(): shard_cols = lax.all_gather(tokens, 'tensor', axis=1, tiled=True)  24 us
    ppermute x4, waiting for transfers between devices, passed_along(): lax.ppermute(value, axis, [(source, source + steps) for source in range(f...  21 us
    all_to_all x1, waiting for transfers between devices, local(): lax.all_to_all(out_grad, 'seq', 0, 0, tiled=True)  20.4 us
    psum x1, blocking collectives, local(): slot_low = lax.psum(partial_low, 'tensor').astype(jnp.bfloat16)  20.2 us
    ppermute x4, starting transfers between devices, passed_along(): lax.ppermute(value, axis, [(source, source + steps) for source in range(f...  15.9 us
    all_to_all x1, starting transfers between devices, local(): lax.all_to_all(slot_low.reshape(seq_count * own_adapters * CAP, R), 'seq'...  10.6 us
    all_to_all x1, starting transfers between devices, local(): lax.all_to_all(outgoing, 'seq', 0, 0, tiled=True)  10.3 us
    all_to_all x1, waiting for transfers between devices, local(): lax.all_to_all(slot_low.reshape(seq_count * own_adapters * CAP, R), 'seq'...  8.59 us
  transfers between devices with their start and end apart: 9, of which 6 were waited for; matrix products, arithmetic and copies ran while one was open for 16% of the time, Pallas kernels for 0%

profile of v8, /device:TPU:1, one launch (start us, length us, event | category | flops | bytes accessed | tf_op | source)
XLA Modules:
  0.0 210.8 jit_solution(8555510249436385123)
XLA Ops:
  8.7 4.4 %collective-permute-start.2 = (s32[512]{0:T(512)}, s32[512]{0:T(512)S(1)}, u32[]{:S(2)}, u32[]{:S(2)}) collective-permute-start(s32[512]{0:T(512)} %param.20), channel_id=1, source_target_pairs={{0,8},{4,12},{8,16},{12,20},{16,24},{20,28},{24,32},{28,36},{32,40... | collective-permute-start | bytes 6152 | tf_op jit(solution)/shard_map/ppermute | solution.py:18
  13.0 4.4 %collective-permute-start.3 = (s32[512]{0:T(512)}, s32[512]{0:T(512)S(1)}, u32[]{:S(2)}, u32[]{:S(2)}) collective-permute-start(s32[512]{0:T(512)} %param.20), channel_id=1, source_target_pairs={{0,4},{4,8},{8,12},{12,16},{16,20},{20,24},{24,28},{28,32},{32,36}... | collective-permute-start | bytes 6152 | tf_op jit(solution)/shard_map/ppermute | solution.py:18
  21.1 4.0 %convolution_convert_fusion = bf16[1024,960]{1,0:T(8,128)(2,1)} fusion(bf16[512,960]{0,1:T(8,128)(2,1)} %param.11, s32[512]{0:T(512)S(1)} %bitcast.186), kind=kOutput, calls=%fused_computation.28 | convolution fusion | flops 1008664576 | bytes 2951168
  25.1 10.3 %all-to-all-start = ((bf16[64,16,960]{2,1,0:T(8,128)(2,1)}), bf16[64,16,960]{2,1,0:T(8,128)(2,1)}, u32[]{:S(2)}, u32[]{:S(2)}) async-start(bf16[64,16,960]{2,1,0:T(8,128)(2,1)} %bitcast.173), calls=%async_computation | async-start | bytes 4194304 | tf_op jit(solution)/shard_map/all_to_all | solution.py:104
  35.5 2.5 %fusion.16 = pred[512,1536]{0,1:T(8,128)(4,1)} fusion(s32[1536]{0:T(1024)S(1)} %pad_add_fusion.1, s32[512]{0:T(512)S(1)} %iota_add_fusion, s32[512]{0:T(512)S(1)} %copy-done.11, s32[1536]{0:T(1024)S(1)} %pad_add_fusion, pred[1536]{0:T(1024)(128)(4,1)S(1)} %broadcast_compare_fusion), kind=kLoop, calls=%fused_computation.20 | loop fusion | flops 5505024 | bytes 804352 | tf_op jit(solution)/shard_map/and | solution.py:133
  38.0 24.0 %all-gather.3.cloned.1.call-done = bf16[512,3840]{0,1:T(8,128)(2,1)} async-done(((bf16[512,960]{0,1:T(8,128)(2,1)}), bf16[512,3840]{0,1:T(8,128)(2,1)}) %all-gather.3.cloned.1.call-update) | async-done | bytes 3932176 | tf_op jit(solution)/shard_map/all_gather | solution.py:84
  62.0 3.5 %multiply_reduce_fusion.1 = (f32[512]{0:T(512)S(1)}, f32[512,256]{0,1:T(8,128)S(1)}) fusion(bf16[512,3840]{0,1:T(8,128)(2,1)} %all-gather.3.cloned.1.call-done, bf16[3840,256]{1,0:T(8,128)(2,1)S(1)} %copy-done), kind=kOutput, calls=%fused_computation.70 | convolution fusion | flops 1006894592 | bytes 6424576 | tf_op jit(solution)/shard_map/dot_general | solution.py:86
  68.1 3.9 %collective-permute-start.1 = (bf16[512,2,1,256]{0,3,2,1:T(8,128)(2,1)S(1)}, bf16[512,2,1,256]{0,3,2,1:T(8,128)(2,1)S(1)}, u32[]{:S(2)}, u32[]{:S(2)}) collective-permute-start(bf16[512,2,1,256]{0,3,2,1:T(8,128)(2,1)S(1)} %pad_maximum_fusion.1), channel_id=1, source_target_pairs={{0,4},{4,8},{8,12},{12,16},{16,20},{20,24},{24,28},{28,32},{32,36}... | collective-permute-start | bytes 1572872 | tf_op jit(solution)/shard_map/ppermute | solution.py:18
  72.1 3.2 %collective-permute-start = (bf16[512,2,1,256]{0,3,2,1:T(8,128)(2,1)S(1)}, bf16[512,2,1,256]{0,3,2,1:T(8,128)(2,1)S(1)}, u32[]{:S(2)}, u32[]{:S(2)}) collective-permute-start(bf16[512,2,1,256]{0,3,2,1:T(8,128)(2,1)S(1)} %pad_maximum_fusion.1), channel_id=1, source_target_pairs={{0,8},{4,12},{8,16},{12,20},{16,24},{20,28},{24,32},{28,36},{32,40... | collective-permute-start | bytes 1572872 | tf_op jit(solution)/shard_map/ppermute | solution.py:18
  75.3 3.2 %fusion.77 = f32[512,512]{1,0:T(8,128)} fusion(bf16[512,3840]{0,1:T(8,128)(2,1)S(1)} %copy-done.2, bf16[3840,512]{1,0:T(8,128)(2,1)S(1)} %copy-done.1), kind=kOutput, calls=%fused_computation.117 | convolution fusion | flops 2013265920 | bytes 8912896 | tf_op jit(solution)/shard_map/dot_general | solution.py:85
  78.5 14.0 %collective-permute-done.1 = bf16[512,2,1,256]{0,3,2,1:T(8,128)(2,1)S(1)} collective-permute-done((bf16[512,2,1,256]{0,3,2,1:T(8,128)(2,1)S(1)}, bf16[512,2,1,256]{0,3,2,1:T(8,128)(2,1)S(1)}, u32[]{:S(2)}, u32[]{:S(2)}) %collective-permute-start.1) | collective-permute-done | bytes 524320 | tf_op jit(solution)/shard_map/ppermute | solution.py:18
  92.5 7.0 %collective-permute-done = bf16[512,2,1,256]{0,3,2,1:T(8,128)(2,1)S(1)} collective-permute-done((bf16[512,2,1,256]{0,3,2,1:T(8,128)(2,1)S(1)}, bf16[512,2,1,256]{0,3,2,1:T(8,128)(2,1)S(1)}, u32[]{:S(2)}, u32[]{:S(2)}) %collective-permute-start) | collective-permute-done | bytes 524320 | tf_op jit(solution)/shard_map/ppermute | solution.py:18
  100.8 2.3 %fusion.34 = f32[64,1,16,64]{3,2,0,1:T(8,128)S(1)} fusion(bf16[64,1,16,960]{3,2,0,1:T(8,128)(2,1)} %bitcast.6, bf16[1,64,960]{2,1,0:T(8,128)(2,1)S(1)} %copy-done.8), kind=kOutput, calls=%fused_computation.37 | convolution fusion | flops 125829120 | bytes 2351104 | tf_op jit(solution)/shard_map/sacd,ard->sacr/dot_general | solution.py:141
  103.1 20.2 %all-reduce.3 = bf16[64,1,16,64]{3,2,0,1:T(8,128)(2,1)S(1)} all-reduce(f32[64,1,16,64]{3,2,0,1:T(8,128)S(1)} %fusion.34), channel_id=1, replica_groups=mesh['seq'=64,'tensor'=4] {'tensor'}, use_global_device_ids=true, to_apply=%region_4.5 | all-reduce | flops 65536 | bytes 393216 | tf_op jit(solution)/shard_map/psum | solution.py:144
  124.2 10.6 %all-to-all-start.1 = ((bf16[64,2,512]{2,1,0:T(2,128)(2,1)}), bf16[64,2,512]{2,1,0:T(2,128)(2,1)S(1)}, u32[]{:S(2)}, u32[]{:S(2)}) async-start(bf16[64,2,512]{2,1,0:T(2,128)(2,1)} %reshape.370), calls=%async_computation.1 | async-start | bytes 262144 | tf_op jit(solution)/shard_map/all_to_all | solution.py:146
  136.6 8.6 %all-to-all-done.1 = bf16[64,2,512]{2,1,0:T(2,128)(2,1)S(1)} async-done(((bf16[64,2,512]{2,1,0:T(2,128)(2,1)}), bf16[64,2,512]{2,1,0:T(2,128)(2,1)S(1)}, u32[]{:S(2)}, u32[]{:S(2)}) %all-to-all-start.1) | async-done | bytes 131104 | tf_op jit(solution)/shard_map/all_to_all | solution.py:146
  145.7 2.9 %convolution_convert_fusion.1 = bf16[64,16,512]{2,1,0:T(8,128)(2,1)S(1)} fusion(bf16[64,16,64]{2,1,0:T(8,128)(2,1)S(1)} %reshape.371, bf16[64,64,512]{2,1,0:T(8,128)(2,1)} %all-gather.5.cloned.1.call-done), kind=kOutput, calls=%fused_computation.31 | convolution fusion | flops 67633152 | bytes 5373952 | tf_op jit(solution)/shard_map/acr,are->ace/dot_general | solution.py:149
  151.0 2.6 %multiply_reduce_fusion = f32[512,2]{1,0:T(8,128)} fusion(f32[512,2,256]{2,1,0:T(2,128)} %reshape.357), kind=kLoop, calls=%fused_computation.47 | loop fusion | flops 523264 | bytes 1052672 | tf_op jit(solution)/shard_map/jvp()/reduce_sum | solution.py:22
  158.2 2.5 %fusion = (f32[2,512]{1,0:T(2,128)S(1)}, f32[1536,512,2]{1,0,2:T(8,128)S(1)}) fusion(f32[2,512]{1,0:T(2,128)S(1)} %get-tuple-element.36, f32[1536,512,2]{1,0,2:T(8,128)S(1)} %get-tuple-element.37, pred[512,1536]{0,1:T(8,128)(4,1)S(1)} %copy-done.5, bf16[64,2,8,256]{3,2,1,0:T(8,128)(2,1)S(1)} %bitcast.187, bf16[1536,1,256]{0,2,1:T(8,128)(2,1)S(1)} %copy-done.6), kind=kOutput, calls=%fused_computation.3 | convolution fusion | flops 813169664 | bytes 14688256 | tf_op jit(solution)/shard_map/tngd,knd->ngtk/dot_general | solution.py:56
  160.8 2.7 %fusion.25 = f32[512,2,256]{2,0,1:T(8,128)S(1)} fusion(f32[1536,512,2]{1,0,2:T(8,128)S(1)} %get-tuple-element.39, f32[2,512]{1,0:T(2,128)S(1)} %get-tuple-element.38, f32[2,512]{1,0:T(2,128)S(1)} %get-tuple-element.36, f32[1536,512,2]{1,0,2:T(8,128)S(1)} %get-tuple-element.37, pred[512,1536]{0,1:T(8,128)(4,1)S(1)} %copy-done.5, ...), kind=kOutput, calls=%fused_computation.32 | convolution fusion | flops 816316416 | bytes 15212544 | tf_op jit(solution)/shard_map/ngtk,knd->tngd/dot_general | solution.py:59
  168.2 6.3 %all-to-all-start.2 = ((bf16[64,16,512]{2,1,0:T(8,128)(2,1)}), bf16[64,16,512]{2,1,0:T(8,128)(2,1)S(1)}, u32[]{:S(2)}, u32[]{:S(2)}) async-start(bf16[64,16,512]{2,1,0:T(8,128)(2,1)} %bitcast.176), calls=%async_computation.2 | async-start | bytes 2097152 | tf_op jit(solution)/shard_map/all_to_all | solution.py:171
  174.5 6.1 %fusion.31 = bf16[256,2,512]{2,0,1:T(8,128)(2,1)} fusion(f32[2,512]{1,0:T(2,128)S(1)} %get-tuple-element.36, f32[1536,512,2]{1,0,2:T(8,128)} %copy-done.15, pred[512,1536]{0,1:T(8,128)(4,1)} %fusion.16, bf16[1536,1,256]{0,2,1:T(8,128)(2,1)} %get-tuple-element.7), kind=kOutput, calls=%fused_computation.36 | convolution fusion | flops 811859968 | bytes 8392704 | tf_op jit(solution)/shard_map/ngtk,knd->tngd/dot_general | solution.py:55
  180.6 2.0 copy.98
  182.6 20.4 %all-to-all-done.2 = bf16[64,16,512]{2,1,0:T(8,128)(2,1)S(1)} async-done(((bf16[64,16,512]{2,1,0:T(8,128)(2,1)}), bf16[64,16,512]{2,1,0:T(8,128)(2,1)S(1)}, u32[]{:S(2)}, u32[]{:S(2)}) %all-to-all-start.2) | async-done | bytes 1048608 | tf_op jit(solution)/shard_map/all_to_all | solution.py:171
  (80 shorter events, 24.8 us)
Async XLA Ops:
  7.2 54.8 %copy-start = (bf16[3840,256]{1,0:T(8,128)(2,1)S(1)}, bf16[3840,256]{1,0:T(8,128)(2,1)}, u32[]{:S(2)}) copy-start(bf16[3840,256]{1,0:T(8,128)(2,1)} %param.13) | copy-start | bytes 5898244
  7.2 54.8 %all-gather.3.cloned.1.call-start = ((), (), s32[]{:S(2)}) async-start(), calls=%async_computation.3 | async-start | bytes 4915200 | tf_op jit(solution)/shard_map/all_gather | solution.py:84
  7.9 137.7 %all-gather.5.cloned.1.call-start = ((), (), s32[]{:S(2)}) async-start(), calls=%async_computation.4 | async-start | bytes 4259840 | tf_op jit(solution)/shard_map/all_gather | solution.py:145
  8.7 26.8 %collective-permute-start.2 = (s32[512]{0:T(512)}, s32[512]{0:T(512)S(1)}, u32[]{:S(2)}, u32[]{:S(2)}) collective-permute-start(s32[512]{0:T(512)} %param.20), channel_id=1, source_target_pairs={{0,8},{4,12},{8,16},{12,20},{16,24},{20,28},{24,32},{28,36},{32,40... | collective-permute-start | bytes 6152 | tf_op jit(solution)/shard_map/ppermute | solution.py:18
  13.0 22.4 %collective-permute-start.3 = (s32[512]{0:T(512)}, s32[512]{0:T(512)S(1)}, u32[]{:S(2)}, u32[]{:S(2)}) collective-permute-start(s32[512]{0:T(512)} %param.20), channel_id=1, source_target_pairs={{0,4},{4,8},{8,12},{12,16},{16,20},{20,24},{24,28},{28,32},{32,36}... | collective-permute-start | bytes 6152 | tf_op jit(solution)/shard_map/ppermute | solution.py:18
  25.1 10.4 %copy-start.11 = (s32[512]{0:T(512)S(1)}, s32[512]{0:T(512)}, u32[]{:S(2)}) copy-start(s32[512]{0:T(512)} %param.20) | copy-start | bytes 6148
  25.1 75.7 %all-to-all-start = ((bf16[64,16,960]{2,1,0:T(8,128)(2,1)}), bf16[64,16,960]{2,1,0:T(8,128)(2,1)}, u32[]{:S(2)}, u32[]{:S(2)}) async-start(bf16[64,16,960]{2,1,0:T(8,128)(2,1)} %bitcast.173), calls=%async_computation | async-start | bytes 4194304 | tf_op jit(solution)/shard_map/all_to_all | solution.py:104
  38.0 27.5 %copy-start.12 = (f32[256]{0:T(256)S(1)}, f32[256]{0:T(256)}, u32[]{:S(2)}) copy-start(f32[256]{0:T(256)} %param.16) | copy-start | bytes 3076
  62.0 4.8 %copy-start.2 = (bf16[512,3840]{0,1:T(8,128)(2,1)S(1)}, bf16[512,3840]{0,1:T(8,128)(2,1)}, u32[]{:S(2)}) copy-start(bf16[512,3840]{0,1:T(8,128)(2,1)} %all-gather.3.cloned.1.call-done) | copy-start | bytes 11796484
  62.0 4.8 %copy-start.13 = (bf16[3840,256]{1,0:T(8,128)(2,1)S(1)}, bf16[3840,256]{1,0:T(8,128)(2,1)}, u32[]{:S(2)}) copy-start(bf16[3840,256]{1,0:T(8,128)(2,1)} %param.14) | copy-start | bytes 5898244
  66.8 8.4 %copy-start.1 = (bf16[3840,512]{1,0:T(8,128)(2,1)S(1)}, bf16[3840,512]{1,0:T(8,128)(2,1)}, u32[]{:S(2)}) copy-start(bf16[3840,512]{1,0:T(8,128)(2,1)} %param.12) | copy-start | bytes 11796484
  68.1 24.3 %collective-permute-start.1 = (bf16[512,2,1,256]{0,3,2,1:T(8,128)(2,1)S(1)}, bf16[512,2,1,256]{0,3,2,1:T(8,128)(2,1)S(1)}, u32[]{:S(2)}, u32[]{:S(2)}) collective-permute-start(bf16[512,2,1,256]{0,3,2,1:T(8,128)(2,1)S(1)} %pad_maximum_fusion.1), channel_id=1, source_target_pairs={{0,4},{4,8},{8,12},{12,16},{16,20},{20,24},{24,28},{28,32},{32,36}... | collective-permute-start | bytes 1572872 | tf_op jit(solution)/shard_map/ppermute | solution.py:18
  72.1 27.4 %collective-permute-start = (bf16[512,2,1,256]{0,3,2,1:T(8,128)(2,1)S(1)}, bf16[512,2,1,256]{0,3,2,1:T(8,128)(2,1)S(1)}, u32[]{:S(2)}, u32[]{:S(2)}) collective-permute-start(bf16[512,2,1,256]{0,3,2,1:T(8,128)(2,1)S(1)} %pad_maximum_fusion.1), channel_id=1, source_target_pairs={{0,8},{4,12},{8,16},{12,20},{16,24},{20,28},{24,32},{28,36},{32,40... | collective-permute-start | bytes 1572872 | tf_op jit(solution)/shard_map/ppermute | solution.py:18
  78.5 22.4 %copy-start.8 = (bf16[1,64,960]{2,1,0:T(8,128)(2,1)S(1)}, bf16[1,64,960]{2,1,0:T(8,128)(2,1)}, u32[]{:S(2)}) copy-start(bf16[1,64,960]{2,1,0:T(8,128)(2,1)} %param.17) | copy-start | bytes 368644
  99.5 35.3 %copy-start.9 = (s32[512,1]{0,1:T(1,128)S(1)}, s32[512,1]{0,1:T(1,128)}, u32[]{:S(2)}) copy-start(s32[512,1]{0,1:T(1,128)} %param.19) | copy-start | bytes 6148
  124.2 21.0 %all-to-all-start.1 = ((bf16[64,2,512]{2,1,0:T(2,128)(2,1)}), bf16[64,2,512]{2,1,0:T(2,128)(2,1)S(1)}, u32[]{:S(2)}, u32[]{:S(2)}) async-start(bf16[64,2,512]{2,1,0:T(2,128)(2,1)} %reshape.370), calls=%async_computation.1 | async-start | bytes 262144 | tf_op jit(solution)/shard_map/all_to_all | solution.py:146
  145.7 3.0 %copy-start.4 = (f32[512,512]{1,0:T(8,128)S(1)}, f32[512,512]{1,0:T(8,128)}, u32[]{:S(2)}) copy-start(f32[512,512]{1,0:T(8,128)} %fusion.77) | copy-start | bytes 3145732
  148.6 6.1 %copy-start.10 = (f32[256]{0:T(256)S(1)}, f32[256]{0:T(256)}, u32[]{:S(2)}) copy-start(f32[256]{0:T(256)} %param.15) | copy-start | bytes 3076
  154.6 1.5 copy-start.7
  156.1 2.1 copy-start.6
  156.1 2.1 copy-start.14
  158.2 2.6 %copy-start.15 = (f32[1536,512,2]{1,0,2:T(8,128)}, f32[1536,512,2]{1,0,2:T(8,128)S(1)}, u32[]{:S(2)}) copy-start(f32[1536,512,2]{1,0,2:T(8,128)S(1)} %get-tuple-element.37) | copy-start | bytes 18874372
  160.8 2.7 %copy-start.3 = (f32[512,128]{1,0:T(8,128)S(1)}, f32[512,128]{1,0:T(8,128)}, u32[]{:S(2)}) copy-start(f32[512,128]{1,0:T(8,128)} %get-tuple-element.33) | copy-start | bytes 786436
  168.2 34.9 %all-to-all-start.2 = ((bf16[64,16,512]{2,1,0:T(8,128)(2,1)}), bf16[64,16,512]{2,1,0:T(8,128)(2,1)S(1)}, u32[]{:S(2)}, u32[]{:S(2)}) async-start(bf16[64,16,512]{2,1,0:T(8,128)(2,1)} %bitcast.176), calls=%async_computation.2 | async-start | bytes 2097152 | tf_op jit(solution)/shard_map/all_to_all | solution.py:171
  (1 other events, 1.5 us)
Sparse Core Ops, SparseCore 0:
  9.8 52.1 all-gather.2
  64.8 80.8 all-gather.4

commit v9 on v8

--- a/solution.py
+++ b/solution.py
@@ -141,18 +141,17 @@
     partial_low = jnp.einsum(
         "sacd,ard->sacr", arrived, adapter_down, preferred_element_type=jnp.float32
     )
-    slot_low = lax.psum(partial_low, "tensor").astype(jnp.bfloat16)
-    all_up = lax.all_gather(adapter_up, "seq", axis=0, tiled=True)
-    back_low = lax.all_to_all(
-        slot_low.reshape(seq_count * own_adapters * CAP, R), "seq", 0, 0, tiled=True
-    ).reshape(ADAPTERS, CAP, R)
+    slot_low = jnp.sum(lax.all_gather(partial_low, "tensor"), axis=0).astype(jnp.bfloat16)
     slot_lift = jnp.einsum(
-        "acr,are->ace", back_low, all_up, preferred_element_type=jnp.float32
+        "sacr,are->sace", slot_low, adapter_up, preferred_element_type=jnp.float32
     ).astype(jnp.bfloat16)
+    back_lift = lax.all_to_all(
+        slot_lift.reshape(seq_count * own_adapters * CAP, q_width), "seq", 0, 0, tiled=True
+    )
     lifted = jnp.einsum(
         "st,se->te",
         dispatch,
-        slot_lift.reshape(ADAPTERS * CAP, q_width),
+        back_lift,
         preferred_element_type=jnp.float32,
     ).astype(jnp.bfloat16)
     query_pre = (query_lin + lifted.astype(jnp.float32)).reshape(tok_count, local_heads, HD)

time: 212 us -> 244 us (1.15)
  waiting for transfers between devices: 75.6 us -> 125 us
  blocking collectives: 20.2 us -> 0 us
    all_gather x1, waiting for transfers between devices: 0.27 us -> 34.7 us  [local(): lax.all_gather(partial_low, 'tensor')]
    psum x1 -> x0, blocking collectives: 20.2 us -> none  [local(): slot_low = lax.psum(partial_low, 'tensor').astype(jnp.bfloat16)]
    all_to_all x1, waiting for transfers between devices: 8.59 us -> 26.7 us  [local(): lax.all_to_all(slot_lift.reshape(seq_count * own_adapters * CAP, q_width)...]
    ppermute x4, waiting for transfers between devices: 21 us -> 18.1 us  [passed_along(): lax.ppermute(value, axis, [(source, source + steps) for source in range(f...]
  transfers between devices with their start and end apart: 9 -> 9, of which waited for: 6 -> 6; matrix products, arithmetic and copies ran while one was open for 16% -> 13% of each run, Pallas kernels for 0% -> 0%
where the time goes in v9:
time: 244 us; the launch traced here: 243 us
  waiting for transfers between devices  125 us (51%)
  starting transfers between devices  43.3 us (18%)
  matrix products  34.8 us (14%)
  other arithmetic  17.7 us (7%)
  between operations  14.5 us (6%)
  local copies, waits for them, and re-layouts  7.48 us (3%)
    all_gather x1, waiting for transfers between devices, local(): lax.all_gather(partial_low, 'tensor')  34.7 us
    all_to_all x1, waiting for transfers between devices, local(): lax.all_to_all(slot_lift.reshape(seq_count * own_adapters * CAP, q_width)...  26.7 us
    all_gather x1, waiting for transfers between devices, local(): shard_cols = lax.all_gather(tokens, 'tensor', axis=1, tiled=True)  24.6 us
    all_to_all x1, waiting for transfers between devices, local(): lax.all_to_all(out_grad, 'seq', 0, 0, tiled=True)  20.4 us
    ppermute x4, waiting for transfers between devices, passed_along(): lax.ppermute(value, axis, [(source, source + steps) for source in range(f...  18.1 us
    ppermute x4, starting transfers between devices, passed_along(): lax.ppermute(value, axis, [(source, source + steps) for source in range(f...  15.9 us
    all_to_all x1, starting transfers between devices, local(): lax.all_to_all(slot_lift.reshape(seq_count * own_adapters * CAP, q_width)...  10.9 us
    all_to_all x1, starting transfers between devices, local(): lax.all_to_all(outgoing, 'seq', 0, 0, tiled=True)  10.3 us
  transfers between devices with their start and end apart: 9, of which 6 were waited for; matrix products, arithmetic and copies ran while one was open for 13% of the time, Pallas kernels for 0%

profile of v9, /device:TPU:1, one launch (start us, length us, event | category | flops | bytes accessed | tf_op | source)
XLA Modules:
  0.0 243.0 jit_solution(11597995902466958445)
XLA Ops:
  7.9 4.4 %collective-permute-start.2 = (s32[512]{0:T(512)}, s32[512]{0:T(512)S(1)}, u32[]{:S(2)}, u32[]{:S(2)}) collective-permute-start(s32[512]{0:T(512)} %param.20), channel_id=1, source_target_pairs={{0,8},{4,12},{8,16},{12,20},{16,24},{20,28},{24,32},{28,36},{32,40... | collective-permute-start | bytes 6152 | tf_op jit(solution)/shard_map/ppermute | solution.py:18
  12.3 4.4 %collective-permute-start.3 = (s32[512]{0:T(512)}, s32[512]{0:T(512)S(1)}, u32[]{:S(2)}, u32[]{:S(2)}) collective-permute-start(s32[512]{0:T(512)} %param.20), channel_id=1, source_target_pairs={{0,4},{4,8},{8,12},{12,16},{16,20},{20,24},{24,28},{28,32},{32,36}... | collective-permute-start | bytes 6152 | tf_op jit(solution)/shard_map/ppermute | solution.py:18
  20.4 4.0 %convolution_convert_fusion = bf16[1024,960]{1,0:T(8,128)(2,1)} fusion(bf16[512,960]{0,1:T(8,128)(2,1)} %param.11, s32[512]{0:T(512)S(1)} %bitcast.190), kind=kOutput, calls=%fused_computation.29 | convolution fusion | flops 1008664576 | bytes 2951168
  24.4 10.3 %all-to-all-start = ((bf16[64,16,960]{2,1,0:T(8,128)(2,1)}), bf16[64,16,960]{2,1,0:T(8,128)(2,1)}, u32[]{:S(2)}, u32[]{:S(2)}) async-start(bf16[64,16,960]{2,1,0:T(8,128)(2,1)} %bitcast.177), calls=%async_computation | async-start | bytes 4194304 | tf_op jit(solution)/shard_map/all_to_all | solution.py:104
  34.9 2.5 %fusion.16 = pred[512,1536]{0,1:T(8,128)(4,1)} fusion(s32[1536]{0:T(1024)S(1)} %pad_add_fusion.1, s32[512]{0:T(512)S(1)} %iota_add_fusion, s32[512]{0:T(512)S(1)} %copy-done.12, s32[1536]{0:T(1024)S(1)} %pad_add_fusion, pred[1536]{0:T(1024)(128)(4,1)S(1)} %broadcast_compare_fusion), kind=kLoop, calls=%fused_computation.20 | loop fusion | flops 5505024 | bytes 804352 | tf_op jit(solution)/shard_map/and | solution.py:133
  37.4 24.6 %all-gather.4.cloned.1.call-done = bf16[512,3840]{0,1:T(8,128)(2,1)} async-done(((bf16[512,960]{0,1:T(8,128)(2,1)}), bf16[512,3840]{0,1:T(8,128)(2,1)}) %all-gather.4.cloned.1.call-update) | async-done | bytes 3932176 | tf_op jit(solution)/shard_map/all_gather | solution.py:84
  62.0 3.5 %multiply_reduce_fusion.1 = (f32[512]{0:T(512)S(1)}, f32[512,256]{0,1:T(8,128)S(1)}) fusion(bf16[512,3840]{0,1:T(8,128)(2,1)} %all-gather.4.cloned.1.call-done, bf16[3840,256]{1,0:T(8,128)(2,1)S(1)} %copy-done), kind=kOutput, calls=%fused_computation.71 | convolution fusion | flops 1006894592 | bytes 6424576 | tf_op jit(solution)/shard_map/dot_general | solution.py:86
  68.1 3.9 %collective-permute-start.1 = (bf16[512,2,1,256]{0,3,2,1:T(8,128)(2,1)S(1)}, bf16[512,2,1,256]{0,3,2,1:T(8,128)(2,1)S(1)}, u32[]{:S(2)}, u32[]{:S(2)}) collective-permute-start(bf16[512,2,1,256]{0,3,2,1:T(8,128)(2,1)S(1)} %pad_maximum_fusion.1), channel_id=1, source_target_pairs={{0,4},{4,8},{8,12},{12,16},{16,20},{20,24},{24,28},{28,32},{32,36}... | collective-permute-start | bytes 1572872 | tf_op jit(solution)/shard_map/ppermute | solution.py:18
  72.1 3.2 %collective-permute-start = (bf16[512,2,1,256]{0,3,2,1:T(8,128)(2,1)S(1)}, bf16[512,2,1,256]{0,3,2,1:T(8,128)(2,1)S(1)}, u32[]{:S(2)}, u32[]{:S(2)}) collective-permute-start(bf16[512,2,1,256]{0,3,2,1:T(8,128)(2,1)S(1)} %pad_maximum_fusion.1), channel_id=1, source_target_pairs={{0,8},{4,12},{8,16},{12,20},{16,24},{20,28},{24,32},{28,36},{32,40... | collective-permute-start | bytes 1572872 | tf_op jit(solution)/shard_map/ppermute | solution.py:18
  75.3 3.2 %fusion.79 = f32[512,512]{1,0:T(8,128)} fusion(bf16[512,3840]{0,1:T(8,128)(2,1)S(1)} %copy-done.2, bf16[3840,512]{1,0:T(8,128)(2,1)S(1)} %copy-done.1), kind=kOutput, calls=%fused_computation.119 | convolution fusion | flops 2013265920 | bytes 8912896 | tf_op jit(solution)/shard_map/dot_general | solution.py:85
  78.5 12.0 %collective-permute-done.1 = bf16[512,2,1,256]{0,3,2,1:T(8,128)(2,1)S(1)} collective-permute-done((bf16[512,2,1,256]{0,3,2,1:T(8,128)(2,1)S(1)}, bf16[512,2,1,256]{0,3,2,1:T(8,128)(2,1)S(1)}, u32[]{:S(2)}, u32[]{:S(2)}) %collective-permute-start.1) | collective-permute-done | bytes 524320 | tf_op jit(solution)/shard_map/ppermute | solution.py:18
  90.5 6.1 %collective-permute-done = bf16[512,2,1,256]{0,3,2,1:T(8,128)(2,1)S(1)} collective-permute-done((bf16[512,2,1,256]{0,3,2,1:T(8,128)(2,1)S(1)}, bf16[512,2,1,256]{0,3,2,1:T(8,128)(2,1)S(1)}, u32[]{:S(2)}, u32[]{:S(2)}) %collective-permute-start) | collective-permute-done | bytes 524320 | tf_op jit(solution)/shard_map/ppermute | solution.py:18
  98.0 3.1 %fusion.34 = f32[64,1,16,64]{3,2,1,0:T(8,128)} fusion(bf16[64,1,16,960]{3,2,0,1:T(8,128)(2,1)} %bitcast.6, bf16[1,64,960]{2,1,0:T(8,128)(2,1)S(1)} %copy-done.8), kind=kOutput, calls=%fused_computation.38 | convolution fusion | flops 125829120 | bytes 2351104 | tf_op jit(solution)/shard_map/sacd,ard->sacr/dot_general | solution.py:141
  101.1 34.7 %all-gather.6.cloned.1.call-done = f32[256,1,16,64]{3,2,1,0:T(8,128)} async-done(((f32[64,1,16,64]{3,2,1,0:T(8,128)}), f32[256,1,16,64]{3,2,1,0:T(8,128)}) %all-gather.6.cloned.1.call-update) | async-done | bytes 1048592 | tf_op jit(solution)/shard_map/all_gather | solution.py:144
  139.0 10.9 %all-to-all-start.1 = ((bf16[64,16,512]{2,1,0:T(8,128)(2,1)}), bf16[64,16,512]{2,1,0:T(8,128)(2,1)S(1)}, u32[]{:S(2)}, u32[]{:S(2)}) async-start(bf16[64,16,512]{2,1,0:T(8,128)(2,1)} %convolution_convert_fusion.1), calls=%async_computation.1 | async-start | bytes 2097152 | tf_op jit(solution)/shard_map/all_to_all | solution.py:148
  151.7 26.7 %all-to-all-done.1 = bf16[64,16,512]{2,1,0:T(8,128)(2,1)S(1)} async-done(((bf16[64,16,512]{2,1,0:T(8,128)(2,1)}), bf16[64,16,512]{2,1,0:T(8,128)(2,1)S(1)}, u32[]{:S(2)}, u32[]{:S(2)}) %all-to-all-start.1) | async-done | bytes 1048608 | tf_op jit(solution)/shard_map/all_to_all | solution.py:148
  179.4 2.3 fusion.30
  183.3 2.6 %multiply_reduce_fusion = f32[512,2]{1,0:T(8,128)} fusion(f32[512,2,256]{2,1,0:T(2,128)} %reshape.367), kind=kLoop, calls=%fused_computation.48 | loop fusion | flops 523264 | bytes 1052672 | tf_op jit(solution)/shard_map/jvp()/reduce_sum | solution.py:22
  190.5 2.5 %fusion = (f32[2,512]{1,0:T(2,128)S(1)}, f32[1536,512,2]{1,0,2:T(8,128)S(1)}) fusion(f32[2,512]{1,0:T(2,128)S(1)} %get-tuple-element.36, f32[1536,512,2]{1,0,2:T(8,128)S(1)} %get-tuple-element.37, pred[512,1536]{0,1:T(8,128)(4,1)S(1)} %copy-done.5, bf16[64,2,8,256]{3,2,1,0:T(8,128)(2,1)S(1)} %bitcast.191, bf16[1536,1,256]{0,2,1:T(8,128)(2,1)S(1)} %copy-done.6), kind=kOutput, calls=%fused_computation.3 | convolution fusion | flops 813169664 | bytes 14688256 | tf_op jit(solution)/shard_map/tngd,knd->ngtk/dot_general | solution.py:56
  193.1 2.7 %fusion.25 = f32[512,2,256]{2,0,1:T(8,128)S(1)} fusion(f32[1536,512,2]{1,0,2:T(8,128)S(1)} %get-tuple-element.39, f32[2,512]{1,0:T(2,128)S(1)} %get-tuple-element.38, f32[2,512]{1,0:T(2,128)S(1)} %get-tuple-element.36, f32[1536,512,2]{1,0,2:T(8,128)S(1)} %get-tuple-element.37, pred[512,1536]{0,1:T(8,128)(4,1)S(1)} %copy-done.5, ...), kind=kOutput, calls=%fused_computation.33 | convolution fusion | flops 816316416 | bytes 15212544 | tf_op jit(solution)/shard_map/ngtk,knd->tngd/dot_general | solution.py:59
  200.5 6.2 %all-to-all-start.2 = ((bf16[64,16,512]{2,1,0:T(8,128)(2,1)}), bf16[64,16,512]{2,1,0:T(8,128)(2,1)S(1)}, u32[]{:S(2)}, u32[]{:S(2)}) async-start(bf16[64,16,512]{2,1,0:T(8,128)(2,1)} %bitcast.181), calls=%async_computation.2 | async-start | bytes 2097152 | tf_op jit(solution)/shard_map/all_to_all | solution.py:170
  206.7 6.1 %fusion.31 = bf16[256,2,512]{2,0,1:T(8,128)(2,1)} fusion(f32[2,512]{1,0:T(2,128)S(1)} %get-tuple-element.36, f32[1536,512,2]{1,0,2:T(8,128)} %copy-done.16, pred[512,1536]{0,1:T(8,128)(4,1)} %fusion.16, bf16[1536,1,256]{0,2,1:T(8,128)(2,1)} %get-tuple-element.7), kind=kOutput, calls=%fused_computation.37 | convolution fusion | flops 811859968 | bytes 8392704 | tf_op jit(solution)/shard_map/ngtk,knd->tngd/dot_general | solution.py:55
  212.8 2.0 copy.101
  214.8 20.4 %all-to-all-done.2 = bf16[64,16,512]{2,1,0:T(8,128)(2,1)S(1)} async-done(((bf16[64,16,512]{2,1,0:T(8,128)(2,1)}), bf16[64,16,512]{2,1,0:T(8,128)(2,1)S(1)}, u32[]{:S(2)}, u32[]{:S(2)}) %all-to-all-start.2) | async-done | bytes 1048608 | tf_op jit(solution)/shard_map/all_to_all | solution.py:170
  (80 shorter events, 26.3 us)
Async XLA Ops:
  7.2 54.8 %copy-start = (bf16[3840,256]{1,0:T(8,128)(2,1)S(1)}, bf16[3840,256]{1,0:T(8,128)(2,1)}, u32[]{:S(2)}) copy-start(bf16[3840,256]{1,0:T(8,128)(2,1)} %param.13) | copy-start | bytes 5898244
  7.2 54.8 %all-gather.4.cloned.1.call-start = ((), (), s32[]{:S(2)}) async-start(), calls=%async_computation.3 | async-start | bytes 4915200 | tf_op jit(solution)/shard_map/all_gather | solution.py:84
  7.9 26.9 %collective-permute-start.2 = (s32[512]{0:T(512)}, s32[512]{0:T(512)S(1)}, u32[]{:S(2)}, u32[]{:S(2)}) collective-permute-start(s32[512]{0:T(512)} %param.20), channel_id=1, source_target_pairs={{0,8},{4,12},{8,16},{12,20},{16,24},{20,28},{24,32},{28,36},{32,40... | collective-permute-start | bytes 6152 | tf_op jit(solution)/shard_map/ppermute | solution.py:18
  12.3 22.5 %collective-permute-start.3 = (s32[512]{0:T(512)}, s32[512]{0:T(512)S(1)}, u32[]{:S(2)}, u32[]{:S(2)}) collective-permute-start(s32[512]{0:T(512)} %param.20), channel_id=1, source_target_pairs={{0,4},{4,8},{8,12},{12,16},{16,20},{20,24},{24,28},{28,32},{32,36}... | collective-permute-start | bytes 6152 | tf_op jit(solution)/shard_map/ppermute | solution.py:18
  24.4 10.5 %copy-start.12 = (s32[512]{0:T(512)S(1)}, s32[512]{0:T(512)}, u32[]{:S(2)}) copy-start(s32[512]{0:T(512)} %param.20) | copy-start | bytes 6148
  24.4 73.6 %all-to-all-start = ((bf16[64,16,960]{2,1,0:T(8,128)(2,1)}), bf16[64,16,960]{2,1,0:T(8,128)(2,1)}, u32[]{:S(2)}, u32[]{:S(2)}) async-start(bf16[64,16,960]{2,1,0:T(8,128)(2,1)} %bitcast.177), calls=%async_computation | async-start | bytes 4194304 | tf_op jit(solution)/shard_map/all_to_all | solution.py:104
  34.7 101.2 %all-gather.6.cloned.1.call-start = ((), (), s32[]{:S(2)}) async-start(), calls=%async_computation.4 | async-start | bytes 2621440 | tf_op jit(solution)/shard_map/all_gather | solution.py:144
  37.4 28.1 %copy-start.13 = (f32[256]{0:T(256)S(1)}, f32[256]{0:T(256)}, u32[]{:S(2)}) copy-start(f32[256]{0:T(256)} %param.16) | copy-start | bytes 3076
  62.0 4.8 %copy-start.2 = (bf16[512,3840]{0,1:T(8,128)(2,1)S(1)}, bf16[512,3840]{0,1:T(8,128)(2,1)}, u32[]{:S(2)}) copy-start(bf16[512,3840]{0,1:T(8,128)(2,1)} %all-gather.4.cloned.1.call-done) | copy-start | bytes 11796484
  62.0 4.8 %copy-start.14 = (bf16[3840,256]{1,0:T(8,128)(2,1)S(1)}, bf16[3840,256]{1,0:T(8,128)(2,1)}, u32[]{:S(2)}) copy-start(bf16[3840,256]{1,0:T(8,128)(2,1)} %param.14) | copy-start | bytes 5898244
  66.8 8.4 %copy-start.1 = (bf16[3840,512]{1,0:T(8,128)(2,1)S(1)}, bf16[3840,512]{1,0:T(8,128)(2,1)}, u32[]{:S(2)}) copy-start(bf16[3840,512]{1,0:T(8,128)(2,1)} %param.12) | copy-start | bytes 11796484
  68.1 22.4 %collective-permute-start.1 = (bf16[512,2,1,256]{0,3,2,1:T(8,128)(2,1)S(1)}, bf16[512,2,1,256]{0,3,2,1:T(8,128)(2,1)S(1)}, u32[]{:S(2)}, u32[]{:S(2)}) collective-permute-start(bf16[512,2,1,256]{0,3,2,1:T(8,128)(2,1)S(1)} %pad_maximum_fusion.1), channel_id=1, source_target_pairs={{0,4},{4,8},{8,12},{12,16},{16,20},{20,24},{24,28},{28,32},{32,36}... | collective-permute-start | bytes 1572872 | tf_op jit(solution)/shard_map/ppermute | solution.py:18
  72.1 24.6 %collective-permute-start = (bf16[512,2,1,256]{0,3,2,1:T(8,128)(2,1)S(1)}, bf16[512,2,1,256]{0,3,2,1:T(8,128)(2,1)S(1)}, u32[]{:S(2)}, u32[]{:S(2)}) collective-permute-start(bf16[512,2,1,256]{0,3,2,1:T(8,128)(2,1)S(1)} %pad_maximum_fusion.1), channel_id=1, source_target_pairs={{0,8},{4,12},{8,16},{12,20},{16,24},{20,28},{24,32},{28,36},{32,40... | collective-permute-start | bytes 1572872 | tf_op jit(solution)/shard_map/ppermute | solution.py:18
  78.5 19.5 %copy-start.8 = (bf16[1,64,960]{2,1,0:T(8,128)(2,1)S(1)}, bf16[1,64,960]{2,1,0:T(8,128)(2,1)}, u32[]{:S(2)}) copy-start(bf16[1,64,960]{2,1,0:T(8,128)(2,1)} %param.17) | copy-start | bytes 368644
  96.7 40.9 %copy-start.9 = (bf16[1,64,512]{2,1,0:T(8,128)(2,1)S(1)}, bf16[1,64,512]{2,1,0:T(8,128)(2,1)}, u32[]{:S(2)}) copy-start(bf16[1,64,512]{2,1,0:T(8,128)(2,1)} %param.18) | copy-start | bytes 196612
  98.0 51.9 %copy-start.10 = (s32[512,1]{0,1:T(1,128)S(1)}, s32[512,1]{0,1:T(1,128)}, u32[]{:S(2)}) copy-start(s32[512,1]{0,1:T(1,128)} %param.19) | copy-start | bytes 6148
  139.0 39.4 %all-to-all-start.1 = ((bf16[64,16,512]{2,1,0:T(8,128)(2,1)}), bf16[64,16,512]{2,1,0:T(8,128)(2,1)S(1)}, u32[]{:S(2)}, u32[]{:S(2)}) async-start(bf16[64,16,512]{2,1,0:T(8,128)(2,1)} %convolution_convert_fusion.1), calls=%async_computation.1 | async-start | bytes 2097152 | tf_op jit(solution)/shard_map/all_to_all | solution.py:148
  151.7 35.3 %copy-start.11 = (f32[256]{0:T(256)S(1)}, f32[256]{0:T(256)}, u32[]{:S(2)}) copy-start(f32[256]{0:T(256)} %param.15) | copy-start | bytes 3076
  186.9 1.5 copy-start.7
  188.4 2.1 copy-start.6
  188.4 2.1 copy-start.15
  190.5 2.6 %copy-start.16 = (f32[1536,512,2]{1,0,2:T(8,128)}, f32[1536,512,2]{1,0,2:T(8,128)S(1)}, u32[]{:S(2)}) copy-start(f32[1536,512,2]{1,0,2:T(8,128)S(1)} %get-tuple-element.37) | copy-start | bytes 18874372
  193.1 2.7 %copy-start.3 = (f32[512,128]{1,0:T(8,128)S(1)}, f32[512,128]{1,0:T(8,128)}, u32[]{:S(2)}) copy-start(f32[512,128]{1,0:T(8,128)} %get-tuple-element.33) | copy-start | bytes 786436
  200.5 34.7 %all-to-all-start.2 = ((bf16[64,16,512]{2,1,0:T(8,128)(2,1)}), bf16[64,16,512]{2,1,0:T(8,128)(2,1)S(1)}, u32[]{:S(2)}, u32[]{:S(2)}) async-start(bf16[64,16,512]{2,1,0:T(8,128)(2,1)} %bitcast.181), calls=%async_computation.2 | async-start | bytes 2097152 | tf_op jit(solution)/shard_map/all_to_all | solution.py:170
  (2 other events, 2.5 us)
Sparse Core Ops, SparseCore 0:
  9.8 52.1 all-gather.3
  101.3 34.5 all-gather.5

commit v10 on v8

--- a/solution.py
+++ b/solution.py
@@ -113,12 +113,18 @@
     value_list = []
     doc_list = []
     place_list = []
-    kv_rows = jnp.stack([key_rows, values], axis=1)
+    kv_rows = jnp.concatenate(
+        [
+            jnp.stack([key_rows, values], axis=0).reshape(2 * tok_count, HD),
+            doc_ids.astype(jnp.bfloat16).reshape(-1, HD),
+        ],
+        axis=0,
+    )
     for distance in range(rim_count, 0, -1):
-        far_kv, far_docs = passed_along((kv_rows, doc_ids), "seq", distance)
-        key_list.append(far_kv[:, 0])
-        value_list.append(far_kv[:, 1])
-        doc_list.append(far_docs)
+        far_kv = passed_along(kv_rows, "seq", distance)
+        key_list.append(far_kv[:tok_count].reshape(tok_count, kv_heads, HD))
+        value_list.append(far_kv[tok_count : 2 * tok_count].reshape(tok_count, kv_heads, HD))
+        doc_list.append(far_kv[2 * tok_count :].reshape(tok_count).astype(jnp.int32))
         place_list.append(positions - distance * tok_count)
     key_list.append(key_rows)
     value_list.append(values)

time: 212 us -> 213 us (level)
  waiting for transfers between devices: 75.6 us -> 68.3 us
  local copies, waits for them, and re-layouts: 7.56 us -> 14.1 us
  starting transfers between devices: 43.1 us -> 36.8 us
  other arithmetic: 15.9 us -> 21.2 us
  matrix products: 33.9 us -> 37.3 us
    ppermute x4 -> x2, waiting for transfers between devices: 21 us -> 7.64 us  [passed_along(): lax.ppermute(value, axis, [(source, source + steps) for source in range(f...]
    ppermute x4 -> x2, starting transfers between devices: 15.9 us -> 7.87 us  [passed_along(): lax.ppermute(value, axis, [(source, source + steps) for source in range(f...]
    all_gather x1, waiting for transfers between devices: 24 us -> 30.4 us  [local(): shard_cols = lax.all_gather(tokens, 'tensor', axis=1, tiled=True)]
    unnamed x35 -> x51, local copies, waits for them, and re-layouts: 3.33 us -> 7.36 us
    dot_general x1, matrix products: 3.18 us -> 6.59 us  [local(): query_lin = jnp.dot(shard_cols, w_query, preferred_element_type=jnp.float32)]
    all_to_all x1, starting transfers between devices: 10.3 us -> 13.4 us  [local(): lax.all_to_all(outgoing, 'seq', 0, 0, tiled=True)]
  transfers between devices with their start and end apart: 9 -> 7, of which waited for: 6 -> 5; matrix products, arithmetic and copies ran while one was open for 16% -> 23% of each run, Pallas kernels for 0% -> 0%
where the time goes in v10:
time: 213 us; the launch traced here: 212 us
  waiting for transfers between devices  68.3 us (32%)
  matrix products  37.3 us (18%)
  starting transfers between devices  36.8 us (17%)
  other arithmetic  21.2 us (10%)
  blocking collectives  19.8 us (9%)
  between operations  14.5 us (7%)
  local copies, waits for them, and re-layouts  14.1 us (7%)
    all_gather x1, waiting for transfers between devices, local(): shard_cols = lax.all_gather(tokens, 'tensor', axis=1, tiled=True)  30.4 us
    all_to_all x1, waiting for transfers between devices, local(): lax.all_to_all(out_grad, 'seq', 0, 0, tiled=True)  20.4 us
    psum x1, blocking collectives, local(): slot_low = lax.psum(partial_low, 'tensor').astype(jnp.bfloat16)  19.8 us
    all_to_all x1, starting transfers between devices, local(): lax.all_to_all(outgoing, 'seq', 0, 0, tiled=True)  13.4 us
    all_to_all x1, starting transfers between devices, local(): lax.all_to_all(slot_low.reshape(seq_count * own_adapters * CAP, R), 'seq'...  10.4 us
    all_to_all x1, waiting for transfers between devices, local(): lax.all_to_all(slot_low.reshape(seq_count * own_adapters * CAP, R), 'seq'...  8.45 us
    ppermute x2, starting transfers between devices, passed_along(): lax.ppermute(value, axis, [(source, source + steps) for source in range(f...  7.87 us
    ppermute x2, waiting for transfers between devices, passed_along(): lax.ppermute(value, axis, [(source, source + steps) for source in range(f...  7.64 us
  transfers between devices with their start and end apart: 7, of which 5 were waited for; matrix products, arithmetic and copies ran while one was open for 23% of the time, Pallas kernels for 0%

profile of v10, /device:TPU:1, one launch (start us, length us, event | category | flops | bytes accessed | tf_op | source)
XLA Modules:
  0.0 211.9 jit_solution(1762120789361825328)
XLA Ops:
  12.9 4.0 %convolution_convert_fusion = bf16[1024,960]{1,0:T(8,128)(2,1)} fusion(bf16[512,960]{0,1:T(8,128)(2,1)} %param.11, s32[512]{0:T(512)S(1)} %bitcast.196), kind=kOutput, calls=%fused_computation.28 | convolution fusion | flops 1008664576 | bytes 2951168
  16.9 13.4 %all-to-all-start = ((bf16[64,16,960]{2,1,0:T(8,128)(2,1)}), bf16[64,16,960]{2,1,0:T(8,128)(2,1)}, u32[]{:S(2)}, u32[]{:S(2)}) async-start(bf16[64,16,960]{2,1,0:T(8,128)(2,1)} %bitcast.177), calls=%async_computation | async-start | bytes 4194304 | tf_op jit(solution)/shard_map/all_to_all | solution.py:104
  31.6 30.4 %all-gather.3.cloned.1.call-done = bf16[512,3840]{0,1:T(8,128)(2,1)} async-done(((bf16[512,960]{0,1:T(8,128)(2,1)}), bf16[512,3840]{0,1:T(8,128)(2,1)}) %all-gather.3.cloned.1.call-update) | async-done | bytes 3932176 | tf_op jit(solution)/shard_map/all_gather | solution.py:84
  62.0 3.5 %multiply_reduce_fusion.1 = (f32[512]{0:T(512)S(1)}, f32[512,256]{0,1:T(8,128)S(1)}) fusion(bf16[512,3840]{0,1:T(8,128)(2,1)} %all-gather.3.cloned.1.call-done, bf16[3840,256]{1,0:T(8,128)(2,1)S(1)} %copy-done), kind=kOutput, calls=%fused_computation.71 | convolution fusion | flops 1006894592 | bytes 6424576 | tf_op jit(solution)/shard_map/dot_general | solution.py:86
  69.9 3.9 %collective-permute-start.1 = (bf16[1026,256]{1,0:T(8,128)(2,1)}, bf16[1026,256]{1,0:T(8,128)(2,1)S(1)}, u32[]{:S(2)}, u32[]{:S(2)}) collective-permute-start(bf16[1026,256]{1,0:T(8,128)(2,1)} %pad_maximum_fusion.1), channel_id=1, source_target_pairs={{0,4},{4,8},{8,12},{12,16},{16,20},{20,24},{24,28},{28,32},{32,36}... | collective-permute-start | bytes 1575944 | tf_op jit(solution)/shard_map/ppermute | solution.py:18
  73.8 4.0 %collective-permute-start = (bf16[1026,256]{1,0:T(8,128)(2,1)}, bf16[1026,256]{1,0:T(8,128)(2,1)}, u32[]{:S(2)}, u32[]{:S(2)}) collective-permute-start(bf16[1026,256]{1,0:T(8,128)(2,1)} %pad_maximum_fusion.1), channel_id=1, source_target_pairs={{0,8},{4,12},{8,16},{12,20},{16,24},{20,28},{24,32},{28,36},{32,40... | collective-permute-start | bytes 1575944 | tf_op jit(solution)/shard_map/ppermute | solution.py:18
  77.7 6.6 %fusion.79 = f32[512,512]{1,0:T(8,128)} fusion(bf16[512,3840]{0,1:T(8,128)(2,1)} %all-gather.3.cloned.1.call-done, bf16[3840,512]{1,0:T(8,128)(2,1)} %param.12), kind=kOutput, calls=%fused_computation.118 | convolution fusion | flops 2013265920 | bytes 8912896 | tf_op jit(solution)/shard_map/dot_general | solution.py:85
  84.3 1.8 collective-permute-done.1
  88.5 5.8 %collective-permute-done = bf16[1026,256]{1,0:T(8,128)(2,1)} collective-permute-done((bf16[1026,256]{1,0:T(8,128)(2,1)}, bf16[1026,256]{1,0:T(8,128)(2,1)}, u32[]{:S(2)}, u32[]{:S(2)}) %collective-permute-start) | collective-permute-done | bytes 525344 | tf_op jit(solution)/shard_map/ppermute | solution.py:18
  100.5 3.6 %fusion.16 = pred[512,1536]{0,1:T(8,128)(4,1)} fusion(s32[1536]{0:T(1024)S(1)} %pad_add_fusion.1, s32[512]{0:T(512)S(1)} %iota_add_fusion, s32[512]{0:T(512)} %param.20, s32[1536]{0:T(1024)S(1)} %pad_add_fusion, pred[1536]{0:T(1024)(128)(4,1)} %broadcast_compare_fusion), kind=kLoop, calls=%fused_computation.20 | loop fusion | flops 5505024 | bytes 804352 | tf_op jit(solution)/shard_map/and | solution.py:139
  104.2 2.3 %fusion.34 = f32[64,1,16,64]{3,2,0,1:T(8,128)S(1)} fusion(bf16[64,1,16,960]{3,2,0,1:T(8,128)(2,1)} %bitcast.6, bf16[1,64,960]{2,1,0:T(8,128)(2,1)} %param.17), kind=kOutput, calls=%fused_computation.37 | convolution fusion | flops 125829120 | bytes 2351104 | tf_op jit(solution)/shard_map/sacd,ard->sacr/dot_general | solution.py:147
  106.5 19.8 %all-reduce.3 = bf16[64,1,16,64]{3,2,0,1:T(8,128)(2,1)S(1)} all-reduce(f32[64,1,16,64]{3,2,0,1:T(8,128)S(1)} %fusion.34), channel_id=1, replica_groups=mesh['seq'=64,'tensor'=4] {'tensor'}, use_global_device_ids=true, to_apply=%region_4.5 | all-reduce | flops 65536 | bytes 393216 | tf_op jit(solution)/shard_map/psum | solution.py:150
  127.1 10.4 %all-to-all-start.1 = ((bf16[64,2,512]{2,1,0:T(2,128)(2,1)}), bf16[64,2,512]{2,1,0:T(2,128)(2,1)S(1)}, u32[]{:S(2)}, u32[]{:S(2)}) async-start(bf16[64,2,512]{2,1,0:T(2,128)(2,1)} %reshape.402), calls=%async_computation.1 | async-start | bytes 262144 | tf_op jit(solution)/shard_map/all_to_all | solution.py:152
  137.5 1.8 multiply_cosine_fusion
  139.3 8.4 %all-to-all-done.1 = bf16[64,2,512]{2,1,0:T(2,128)(2,1)S(1)} async-done(((bf16[64,2,512]{2,1,0:T(2,128)(2,1)}), bf16[64,2,512]{2,1,0:T(2,128)(2,1)S(1)}, u32[]{:S(2)}, u32[]{:S(2)}) %all-to-all-start.1) | async-done | bytes 131104 | tf_op jit(solution)/shard_map/all_to_all | solution.py:152
  148.0 2.9 %convolution_convert_fusion.1 = bf16[64,16,512]{2,1,0:T(8,128)(2,1)S(1)} fusion(bf16[64,16,64]{2,1,0:T(8,128)(2,1)S(1)} %reshape.403, bf16[64,64,512]{2,1,0:T(8,128)(2,1)} %all-gather.5.cloned.1.call-done), kind=kOutput, calls=%fused_computation.31 | convolution fusion | flops 67633152 | bytes 5373952 | tf_op jit(solution)/shard_map/acr,are->ace/dot_general | solution.py:155
  153.4 2.6 %multiply_reduce_fusion = f32[512,2]{1,0:T(8,128)} fusion(f32[512,2,256]{2,1,0:T(2,128)} %reshape.387), kind=kLoop, calls=%fused_computation.47 | loop fusion | flops 523264 | bytes 1052672 | tf_op jit(solution)/shard_map/jvp()/reduce_sum | solution.py:22
  158.5 2.0 fusion.5
  160.6 2.5 %fusion = (f32[2,512]{1,0:T(2,128)S(1)}, f32[1536,512,2]{1,0,2:T(8,128)S(1)}) fusion(f32[2,512]{1,0:T(2,128)S(1)} %get-tuple-element.36, f32[1536,512,2]{1,0,2:T(8,128)S(1)} %get-tuple-element.37, pred[512,1536]{0,1:T(8,128)(4,1)S(1)} %copy-done.4, bf16[64,2,8,256]{3,2,1,0:T(8,128)(2,1)S(1)} %bitcast.197, bf16[1536,1,256]{0,2,1:T(8,128)(2,1)S(1)} %copy-done.5), kind=kOutput, calls=%fused_computation.3 | convolution fusion | flops 813169664 | bytes 14688256 | tf_op jit(solution)/shard_map/tngd,knd->ngtk/dot_general | solution.py:56
  163.2 2.7 %fusion.25 = f32[512,2,256]{2,0,1:T(8,128)S(1)} fusion(f32[1536,512,2]{1,0,2:T(8,128)S(1)} %get-tuple-element.39, f32[2,512]{1,0:T(2,128)S(1)} %get-tuple-element.38, f32[2,512]{1,0:T(2,128)S(1)} %get-tuple-element.36, f32[1536,512,2]{1,0,2:T(8,128)S(1)} %get-tuple-element.37, pred[512,1536]{0,1:T(8,128)(4,1)S(1)} %copy-done.4, ...), kind=kOutput, calls=%fused_computation.32 | convolution fusion | flops 816316416 | bytes 15212544 | tf_op jit(solution)/shard_map/ngtk,knd->tngd/dot_general | solution.py:59
  170.6 5.0 %all-to-all-start.2 = ((bf16[64,16,512]{2,1,0:T(8,128)(2,1)}), bf16[64,16,512]{2,1,0:T(8,128)(2,1)S(1)}, u32[]{:S(2)}, u32[]{:S(2)}) async-start(bf16[64,16,512]{2,1,0:T(8,128)(2,1)} %bitcast.184), calls=%async_computation.2 | async-start | bytes 2097152 | tf_op jit(solution)/shard_map/all_to_all | solution.py:177
  175.6 6.1 %fusion.31 = bf16[256,2,512]{2,0,1:T(8,128)(2,1)} fusion(f32[2,512]{1,0:T(2,128)S(1)} %get-tuple-element.36, f32[1536,512,2]{1,0,2:T(8,128)} %copy-done.20, pred[512,1536]{0,1:T(8,128)(4,1)} %fusion.16, bf16[1536,1,256]{0,2,1:T(8,128)(2,1)} %get-tuple-element.7), kind=kOutput, calls=%fused_computation.36 | convolution fusion | flops 811859968 | bytes 8392704 | tf_op jit(solution)/shard_map/ngtk,knd->tngd/dot_general | solution.py:55
  181.7 2.0 copy.118
  183.7 20.4 %all-to-all-done.2 = bf16[64,16,512]{2,1,0:T(8,128)(2,1)S(1)} async-done(((bf16[64,16,512]{2,1,0:T(8,128)(2,1)}), bf16[64,16,512]{2,1,0:T(8,128)(2,1)S(1)}, u32[]{:S(2)}, u32[]{:S(2)}) %all-to-all-start.2) | async-done | bytes 1048608 | tf_op jit(solution)/shard_map/all_to_all | solution.py:177
  (98 shorter events, 31.5 us)
Async XLA Ops:
  7.2 54.8 %copy-start = (bf16[3840,256]{1,0:T(8,128)(2,1)S(1)}, bf16[3840,256]{1,0:T(8,128)(2,1)}, u32[]{:S(2)}) copy-start(bf16[3840,256]{1,0:T(8,128)(2,1)} %param.13) | copy-start | bytes 5898244
  7.2 54.8 %all-gather.3.cloned.1.call-start = ((), (), s32[]{:S(2)}) async-start(), calls=%async_computation.3 | async-start | bytes 4915200 | tf_op jit(solution)/shard_map/all_gather | solution.py:84
  7.9 140.1 %all-gather.5.cloned.1.call-start = ((), (), s32[]{:S(2)}) async-start(), calls=%async_computation.4 | async-start | bytes 4259840 | tf_op jit(solution)/shard_map/all_gather | solution.py:151
  16.9 13.5 %copy-start.13 = (s32[512]{0:T(512)S(1)}, s32[512]{0:T(512)}, u32[]{:S(2)}) copy-start(s32[512]{0:T(512)} %param.20) | copy-start | bytes 6148
  16.9 87.3 %all-to-all-start = ((bf16[64,16,960]{2,1,0:T(8,128)(2,1)}), bf16[64,16,960]{2,1,0:T(8,128)(2,1)}, u32[]{:S(2)}, u32[]{:S(2)}) async-start(bf16[64,16,960]{2,1,0:T(8,128)(2,1)} %bitcast.177), calls=%async_computation | async-start | bytes 4194304 | tf_op jit(solution)/shard_map/all_to_all | solution.py:104
  31.0 34.7 %copy-start.15 = (f32[128]{0:T(128)}, f32[128]{0:T(128)S(1)}, u32[]{:S(2)}) copy-start(f32[128]{0:T(128)S(1)} %multiply_exponential_fusion) | copy-start | bytes 1540
  31.0 34.7 %copy-start.9 = (f32[512]{0:T(512)}, f32[512]{0:T(512)S(1)}, u32[]{:S(2)}) copy-start(f32[512]{0:T(512)S(1)} %fusion.70) | copy-start | bytes 6148
  31.6 33.9 %copy-start.17 = (f32[256]{0:T(256)S(1)}, f32[256]{0:T(256)}, u32[]{:S(2)}) copy-start(f32[256]{0:T(256)} %param.16) | copy-start | bytes 3076
  62.0 4.8 %copy-start.1 = (bf16[512,3840]{0,1:T(8,128)(2,1)S(1)}, bf16[512,3840]{0,1:T(8,128)(2,1)}, u32[]{:S(2)}) copy-start(bf16[512,3840]{0,1:T(8,128)(2,1)} %all-gather.3.cloned.1.call-done) | copy-start | bytes 11796484
  62.0 4.9 %copy-start.18 = (bf16[3840,256]{1,0:T(8,128)(2,1)S(1)}, bf16[3840,256]{1,0:T(8,128)(2,1)}, u32[]{:S(2)}) copy-start(bf16[3840,256]{1,0:T(8,128)(2,1)} %param.14) | copy-start | bytes 5898244
  69.9 16.3 %collective-permute-start.1 = (bf16[1026,256]{1,0:T(8,128)(2,1)}, bf16[1026,256]{1,0:T(8,128)(2,1)S(1)}, u32[]{:S(2)}, u32[]{:S(2)}) collective-permute-start(bf16[1026,256]{1,0:T(8,128)(2,1)} %pad_maximum_fusion.1), channel_id=1, source_target_pairs={{0,4},{4,8},{8,12},{12,16},{16,20},{20,24},{24,28},{28,32},{32,36}... | collective-permute-start | bytes 1575944 | tf_op jit(solution)/shard_map/ppermute | solution.py:18
  73.8 20.6 %collective-permute-start = (bf16[1026,256]{1,0:T(8,128)(2,1)}, bf16[1026,256]{1,0:T(8,128)(2,1)}, u32[]{:S(2)}, u32[]{:S(2)}) collective-permute-start(bf16[1026,256]{1,0:T(8,128)(2,1)} %pad_maximum_fusion.1), channel_id=1, source_target_pairs={{0,8},{4,12},{8,16},{12,20},{16,24},{20,28},{24,32},{28,36},{32,40... | collective-permute-start | bytes 1575944 | tf_op jit(solution)/shard_map/ppermute | solution.py:18
  99.3 38.2 %copy-start.8 = (s32[512,1]{0,1:T(1,128)S(1)}, s32[512,1]{0,1:T(1,128)}, u32[]{:S(2)}) copy-start(s32[512,1]{0,1:T(1,128)} %param.19) | copy-start | bytes 6148
  100.5 37.0 %copy-start.12 = (s32[512]{0:T(512)S(1)}, s32[512]{0:T(512)}, u32[]{:S(2)}) copy-start(s32[512]{0:T(512)} %copy-done.11) | copy-start | bytes 6148
  100.5 37.0 %copy-start.10 = (f32[512]{0:T(512)S(1)}, f32[512]{0:T(512)}, u32[]{:S(2)}) copy-start(f32[512]{0:T(512)} %copy-done.9) | copy-start | bytes 6148
  100.5 37.0 %copy-start.16 = (f32[128]{0:T(128)S(1)}, f32[128]{0:T(128)}, u32[]{:S(2)}) copy-start(f32[128]{0:T(128)} %copy-done.15) | copy-start | bytes 1540
  127.1 20.7 %all-to-all-start.1 = ((bf16[64,2,512]{2,1,0:T(2,128)(2,1)}), bf16[64,2,512]{2,1,0:T(2,128)(2,1)S(1)}, u32[]{:S(2)}, u32[]{:S(2)}) async-start(bf16[64,2,512]{2,1,0:T(2,128)(2,1)} %reshape.402), calls=%async_computation.1 | async-start | bytes 262144 | tf_op jit(solution)/shard_map/all_to_all | solution.py:152
  148.0 3.0 %copy-start.3 = (f32[512,512]{1,0:T(8,128)S(1)}, f32[512,512]{1,0:T(8,128)}, u32[]{:S(2)}) copy-start(f32[512,512]{1,0:T(8,128)} %fusion.79) | copy-start | bytes 3145732
  151.0 6.1 %copy-start.14 = (f32[256]{0:T(256)S(1)}, f32[256]{0:T(256)}, u32[]{:S(2)}) copy-start(f32[256]{0:T(256)} %param.15) | copy-start | bytes 3076
  158.5 2.1 copy-start.5
  158.5 2.1 copy-start.19
  160.6 2.7 %copy-start.20 = (f32[1536,512,2]{1,0,2:T(8,128)}, f32[1536,512,2]{1,0,2:T(8,128)S(1)}, u32[]{:S(2)}) copy-start(f32[1536,512,2]{1,0,2:T(8,128)S(1)} %get-tuple-element.37) | copy-start | bytes 18874372
  163.2 2.7 %copy-start.2 = (f32[512,128]{1,0:T(8,128)S(1)}, f32[512,128]{1,0:T(8,128)}, u32[]{:S(2)}) copy-start(f32[512,128]{1,0:T(8,128)} %get-tuple-element.33) | copy-start | bytes 786436
  170.6 33.5 %all-to-all-start.2 = ((bf16[64,16,512]{2,1,0:T(8,128)(2,1)}), bf16[64,16,512]{2,1,0:T(8,128)(2,1)S(1)}, u32[]{:S(2)}, u32[]{:S(2)}) async-start(bf16[64,16,512]{2,1,0:T(8,128)(2,1)} %bitcast.184), calls=%async_computation.2 | async-start | bytes 2097152 | tf_op jit(solution)/shard_map/all_to_all | solution.py:177
  (4 other events, 4.3 us)
Sparse Core Ops, SparseCore 0:
  9.8 52.1 all-gather.2
  64.8 80.3 all-gather.4

commit v11 on v8

--- a/solution.py
+++ b/solution.py
@@ -87,7 +87,12 @@
     value_lin = jnp.dot(shard_cols, w_value, preferred_element_type=jnp.float32)
     token_adapter = adapter_ids[:, 0]
     chosen = token_adapter[:, None] == jnp.arange(ADAPTERS, dtype=jnp.int32)[None, :]
-    before = jnp.cumsum(chosen.astype(jnp.int32), axis=0) - 1
+    earlier = (
+        jnp.arange(tok_count, dtype=jnp.int32)[:, None] > jnp.arange(tok_count, dtype=jnp.int32)[None, :]
+    ).astype(jnp.bfloat16)
+    before = jnp.dot(
+        earlier, chosen.astype(jnp.bfloat16), preferred_element_type=jnp.float32
+    ).astype(jnp.int32)
     slot_rank = jnp.sum(jnp.where(chosen, before, 0), axis=1)
     slot_index = token_adapter * CAP + slot_rank
     dispatch = (slot_index[None, :] == jnp.arange(ADAPTERS * CAP, dtype=jnp.int32)[:, None]).astype(

time: 212 us -> 211 us (level)
  other arithmetic: 15.9 us -> 13.3 us
  transfers between devices with their start and end apart: 9 -> 9, of which waited for: 6 -> 6; matrix products, arithmetic and copies ran while one was open for 16% -> 15% of each run, Pallas kernels for 0% -> 0%
where the time goes in v11:
time: 211 us
  waiting for transfers between devices  76.7 us (36%)
  starting transfers between devices  44.7 us (21%)
  matrix products  35 us (17%)
  blocking collectives  19.3 us (9%)
  between operations  14.5 us (7%)
  other arithmetic  13.3 us (6%)
  local copies, waits for them, and re-layouts  7.36 us (3%)
    all_gather x1, waiting for transfers between devices, local(): shard_cols = lax.all_gather(tokens, 'tensor', axis=1, tiled=True)  25.9 us
    all_to_all x1, waiting for transfers between devices, local(): lax.all_to_all(out_grad, 'seq', 0, 0, tiled=True)  20.4 us
    psum x1, blocking collectives, local(): slot_low = lax.psum(partial_low, 'tensor').astype(jnp.bfloat16)  19.3 us
    ppermute x4, waiting for transfers between devices, passed_along(): lax.ppermute(value, axis, [(source, source + steps) for source in range(f...  18.9 us
    ppermute x4, starting transfers between devices, passed_along(): lax.ppermute(value, axis, [(source, source + steps) for source in range(f...  15.9 us
    all_to_all x1, starting transfers between devices, local(): lax.all_to_all(slot_low.reshape(seq_count * own_adapters * CAP, R), 'seq'...  12.1 us
    all_to_all x1, starting transfers between devices, local(): lax.all_to_all(outgoing, 'seq', 0, 0, tiled=True)  10.3 us
    all_to_all x1, waiting for transfers between devices, local(): lax.all_to_all(slot_low.reshape(seq_count * own_adapters * CAP, R), 'seq'...  8.86 us
  transfers between devices with their start and end apart: 9, of which 6 were waited for; matrix products, arithmetic and copies ran while one was open for 15% of the time, Pallas kernels for 0%

profile of v11, /device:TPU:1, one launch (start us, length us, event | category | flops | bytes accessed | tf_op | source)
XLA Modules:
  0.0 210.7 jit_solution(6613343694976694909)
XLA Ops:
  8.7 4.4 %collective-permute-start.2 = (s32[512]{0:T(512)}, s32[512]{0:T(512)S(1)}, u32[]{:S(2)}, u32[]{:S(2)}) collective-permute-start(s32[512]{0:T(512)} %param.20), channel_id=1, source_target_pairs={{0,8},{4,12},{8,16},{12,20},{16,24},{20,28},{24,32},{28,36},{32,40... | collective-permute-start | bytes 6152 | tf_op jit(solution)/shard_map/ppermute | solution.py:18
  13.0 4.4 %collective-permute-start.3 = (s32[512]{0:T(512)}, s32[512]{0:T(512)S(1)}, u32[]{:S(2)}, u32[]{:S(2)}) collective-permute-start(s32[512]{0:T(512)} %param.20), channel_id=1, source_target_pairs={{0,4},{4,8},{8,12},{12,16},{16,20},{20,24},{24,28},{28,32},{32,36}... | collective-permute-start | bytes 6152 | tf_op jit(solution)/shard_map/ppermute | solution.py:18
  19.2 4.0 %convolution_convert_fusion = bf16[1024,960]{1,0:T(8,128)(2,1)} fusion(bf16[512,960]{0,1:T(8,128)(2,1)} %param.11, s32[512]{0:T(512)S(1)} %bitcast.169), kind=kOutput, calls=%fused_computation.28 | convolution fusion | flops 1008664576 | bytes 2951168
  23.2 10.3 %all-to-all-start = ((bf16[64,16,960]{2,1,0:T(8,128)(2,1)}), bf16[64,16,960]{2,1,0:T(8,128)(2,1)}, u32[]{:S(2)}, u32[]{:S(2)}) async-start(bf16[64,16,960]{2,1,0:T(8,128)(2,1)} %bitcast.157), calls=%async_computation | async-start | bytes 4194304 | tf_op jit(solution)/shard_map/all_to_all | solution.py:109
  33.6 2.5 %fusion.16 = pred[512,1536]{0,1:T(8,128)(4,1)} fusion(s32[1536]{0:T(1024)S(1)} %pad_add_fusion.1, s32[512]{0:T(512)S(1)} %iota_add_fusion, s32[512]{0:T(512)S(1)} %copy-done.10, s32[1536]{0:T(1024)S(1)} %pad_add_fusion, pred[1536]{0:T(1024)(128)(4,1)S(1)} %broadcast_compare_fusion), kind=kLoop, calls=%fused_computation.20 | loop fusion | flops 5505024 | bytes 804352 | tf_op jit(solution)/shard_map/and | solution.py:138
  36.1 25.9 %all-gather.3.cloned.1.call-done = bf16[512,3840]{0,1:T(8,128)(2,1)} async-done(((bf16[512,960]{0,1:T(8,128)(2,1)}), bf16[512,3840]{0,1:T(8,128)(2,1)}) %all-gather.3.cloned.1.call-update) | async-done | bytes 3932176 | tf_op jit(solution)/shard_map/all_gather | solution.py:84
  62.0 3.5 %multiply_reduce_fusion.1 = (f32[512]{0:T(512)S(1)}, f32[512,256]{0,1:T(8,128)S(1)}) fusion(bf16[512,3840]{0,1:T(8,128)(2,1)} %all-gather.3.cloned.1.call-done, bf16[3840,256]{1,0:T(8,128)(2,1)S(1)} %copy-done), kind=kOutput, calls=%fused_computation.74 | convolution fusion | flops 1006894592 | bytes 6424576 | tf_op jit(solution)/shard_map/dot_general | solution.py:86
  68.1 3.9 %collective-permute-start.1 = (bf16[512,2,1,256]{0,3,2,1:T(8,128)(2,1)S(1)}, bf16[512,2,1,256]{0,3,2,1:T(8,128)(2,1)S(1)}, u32[]{:S(2)}, u32[]{:S(2)}) collective-permute-start(bf16[512,2,1,256]{0,3,2,1:T(8,128)(2,1)S(1)} %pad_maximum_fusion.1), channel_id=1, source_target_pairs={{0,4},{4,8},{8,12},{12,16},{16,20},{20,24},{24,28},{28,32},{32,36}... | collective-permute-start | bytes 1572872 | tf_op jit(solution)/shard_map/ppermute | solution.py:18
  72.1 3.2 %collective-permute-start = (bf16[512,2,1,256]{0,3,2,1:T(8,128)(2,1)S(1)}, bf16[512,2,1,256]{0,3,2,1:T(8,128)(2,1)S(1)}, u32[]{:S(2)}, u32[]{:S(2)}) collective-permute-start(bf16[512,2,1,256]{0,3,2,1:T(8,128)(2,1)S(1)} %pad_maximum_fusion.1), channel_id=1, source_target_pairs={{0,8},{4,12},{8,16},{12,20},{16,24},{20,28},{24,32},{28,36},{32,40... | collective-permute-start | bytes 1572872 | tf_op jit(solution)/shard_map/ppermute | solution.py:18
  75.3 3.2 %fusion.77 = f32[512,512]{1,0:T(8,128)} fusion(bf16[512,3840]{0,1:T(8,128)(2,1)S(1)} %copy-done.2, bf16[3840,512]{1,0:T(8,128)(2,1)S(1)} %copy-done.1), kind=kOutput, calls=%fused_computation.115 | convolution fusion | flops 2013265920 | bytes 8912896 | tf_op jit(solution)/shard_map/dot_general | solution.py:85
  78.5 11.9 %collective-permute-done.1 = bf16[512,2,1,256]{0,3,2,1:T(8,128)(2,1)S(1)} collective-permute-done((bf16[512,2,1,256]{0,3,2,1:T(8,128)(2,1)S(1)}, bf16[512,2,1,256]{0,3,2,1:T(8,128)(2,1)S(1)}, u32[]{:S(2)}, u32[]{:S(2)}) %collective-permute-start.1) | collective-permute-done | bytes 524320 | tf_op jit(solution)/shard_map/ppermute | solution.py:18
  90.4 6.9 %collective-permute-done = bf16[512,2,1,256]{0,3,2,1:T(8,128)(2,1)S(1)} collective-permute-done((bf16[512,2,1,256]{0,3,2,1:T(8,128)(2,1)S(1)}, bf16[512,2,1,256]{0,3,2,1:T(8,128)(2,1)S(1)}, u32[]{:S(2)}, u32[]{:S(2)}) %collective-permute-start) | collective-permute-done | bytes 524320 | tf_op jit(solution)/shard_map/ppermute | solution.py:18
  98.8 2.3 %fusion.34 = f32[64,1,16,64]{3,2,0,1:T(8,128)S(1)} fusion(bf16[64,1,16,960]{3,2,0,1:T(8,128)(2,1)} %bitcast.4, bf16[1,64,960]{2,1,0:T(8,128)(2,1)S(1)} %copy-done.8), kind=kOutput, calls=%fused_computation.37 | convolution fusion | flops 125829120 | bytes 2351104 | tf_op jit(solution)/shard_map/sacd,ard->sacr/dot_general | solution.py:146
  101.1 19.3 %all-reduce.3 = bf16[64,1,16,64]{3,2,0,1:T(8,128)(2,1)S(1)} all-reduce(f32[64,1,16,64]{3,2,0,1:T(8,128)S(1)} %fusion.34), channel_id=1, replica_groups=mesh['seq'=64,'tensor'=4] {'tensor'}, use_global_device_ids=true, to_apply=%region_2.3 | all-reduce | flops 65536 | bytes 393216 | tf_op jit(solution)/shard_map/psum | solution.py:149
  121.2 12.1 %all-to-all-start.1 = ((bf16[64,2,512]{2,1,0:T(2,128)(2,1)}), bf16[64,2,512]{2,1,0:T(2,128)(2,1)S(1)}, u32[]{:S(2)}, u32[]{:S(2)}) async-start(bf16[64,2,512]{2,1,0:T(2,128)(2,1)} %reshape.350), calls=%async_computation.1 | async-start | bytes 262144 | tf_op jit(solution)/shard_map/all_to_all | solution.py:151
  135.1 8.9 %all-to-all-done.1 = bf16[64,2,512]{2,1,0:T(2,128)(2,1)S(1)} async-done(((bf16[64,2,512]{2,1,0:T(2,128)(2,1)}), bf16[64,2,512]{2,1,0:T(2,128)(2,1)S(1)}, u32[]{:S(2)}, u32[]{:S(2)}) %all-to-all-start.1) | async-done | bytes 131104 | tf_op jit(solution)/shard_map/all_to_all | solution.py:151
  145.5 2.9 %convolution_convert_fusion.1 = bf16[64,16,512]{2,1,0:T(8,128)(2,1)S(1)} fusion(bf16[64,16,64]{2,1,0:T(8,128)(2,1)S(1)} %reshape.351, bf16[64,64,512]{2,1,0:T(8,128)(2,1)} %all-gather.5.cloned.1.call-done), kind=kOutput, calls=%fused_computation.31 | convolution fusion | flops 67633152 | bytes 5373952 | tf_op jit(solution)/shard_map/acr,are->ace/dot_general | solution.py:154
  150.9 2.6 %multiply_reduce_fusion = f32[512,2]{1,0:T(8,128)} fusion(f32[512,2,256]{2,1,0:T(2,128)} %reshape.338), kind=kLoop, calls=%fused_computation.50 | loop fusion | flops 523264 | bytes 1052672 | tf_op jit(solution)/shard_map/jvp()/reduce_sum | solution.py:22
  158.1 2.5 %fusion = (f32[2,512]{1,0:T(2,128)S(1)}, f32[1536,512,2]{1,0,2:T(8,128)S(1)}) fusion(f32[2,512]{1,0:T(2,128)S(1)} %get-tuple-element.36, f32[1536,512,2]{1,0,2:T(8,128)S(1)} %get-tuple-element.37, pred[512,1536]{0,1:T(8,128)(4,1)S(1)} %copy-done.5, bf16[64,2,8,256]{3,2,1,0:T(8,128)(2,1)S(1)} %bitcast.170, bf16[1536,1,256]{0,2,1:T(8,128)(2,1)S(1)} %copy-done.6), kind=kOutput, calls=%fused_computation.3 | convolution fusion | flops 813169664 | bytes 14688256 | tf_op jit(solution)/shard_map/tngd,knd->ngtk/dot_general | solution.py:56
  160.7 2.7 %fusion.25 = f32[512,2,256]{2,0,1:T(8,128)S(1)} fusion(f32[1536,512,2]{1,0,2:T(8,128)S(1)} %get-tuple-element.39, f32[2,512]{1,0:T(2,128)S(1)} %get-tuple-element.38, f32[2,512]{1,0:T(2,128)S(1)} %get-tuple-element.36, f32[1536,512,2]{1,0,2:T(8,128)S(1)} %get-tuple-element.37, pred[512,1536]{0,1:T(8,128)(4,1)S(1)} %copy-done.5, ...), kind=kOutput, calls=%fused_computation.32 | convolution fusion | flops 816316416 | bytes 15212544 | tf_op jit(solution)/shard_map/ngtk,knd->tngd/dot_general | solution.py:59
  168.0 6.4 %all-to-all-start.2 = ((bf16[64,16,512]{2,1,0:T(8,128)(2,1)}), bf16[64,16,512]{2,1,0:T(8,128)(2,1)S(1)}, u32[]{:S(2)}, u32[]{:S(2)}) async-start(bf16[64,16,512]{2,1,0:T(8,128)(2,1)} %bitcast.160), calls=%async_computation.2 | async-start | bytes 2097152 | tf_op jit(solution)/shard_map/all_to_all | solution.py:176
  174.4 6.1 %fusion.31 = bf16[256,2,512]{2,0,1:T(8,128)(2,1)} fusion(f32[2,512]{1,0:T(2,128)S(1)} %get-tuple-element.36, f32[1536,512,2]{1,0,2:T(8,128)} %copy-done.15, pred[512,1536]{0,1:T(8,128)(4,1)} %fusion.16, bf16[1536,1,256]{0,2,1:T(8,128)(2,1)} %get-tuple-element.7), kind=kOutput, calls=%fused_computation.36 | convolution fusion | flops 811859968 | bytes 8392704 | tf_op jit(solution)/shard_map/ngtk,knd->tngd/dot_general | solution.py:55
  180.5 2.0 copy.94
  182.5 20.4 %all-to-all-done.2 = bf16[64,16,512]{2,1,0:T(8,128)(2,1)S(1)} async-done(((bf16[64,16,512]{2,1,0:T(8,128)(2,1)}), bf16[64,16,512]{2,1,0:T(8,128)(2,1)S(1)}, u32[]{:S(2)}, u32[]{:S(2)}) %all-to-all-start.2) | async-done | bytes 1048608 | tf_op jit(solution)/shard_map/all_to_all | solution.py:176
  (75 shorter events, 24.0 us)
Async XLA Ops:
  7.2 54.8 %copy-start = (bf16[3840,256]{1,0:T(8,128)(2,1)S(1)}, bf16[3840,256]{1,0:T(8,128)(2,1)}, u32[]{:S(2)}) copy-start(bf16[3840,256]{1,0:T(8,128)(2,1)} %param.13) | copy-start | bytes 5898244
  7.2 54.8 %all-gather.3.cloned.1.call-start = ((), (), s32[]{:S(2)}) async-start(), calls=%async_computation.3 | async-start | bytes 4915200 | tf_op jit(solution)/shard_map/all_gather | solution.py:84
  7.9 137.6 %all-gather.5.cloned.1.call-start = ((), (), s32[]{:S(2)}) async-start(), calls=%async_computation.4 | async-start | bytes 4259840 | tf_op jit(solution)/shard_map/all_gather | solution.py:150
  8.7 24.9 %collective-permute-start.2 = (s32[512]{0:T(512)}, s32[512]{0:T(512)S(1)}, u32[]{:S(2)}, u32[]{:S(2)}) collective-permute-start(s32[512]{0:T(512)} %param.20), channel_id=1, source_target_pairs={{0,8},{4,12},{8,16},{12,20},{16,24},{20,28},{24,32},{28,36},{32,40... | collective-permute-start | bytes 6152 | tf_op jit(solution)/shard_map/ppermute | solution.py:18
  13.0 20.5 %collective-permute-start.3 = (s32[512]{0:T(512)}, s32[512]{0:T(512)S(1)}, u32[]{:S(2)}, u32[]{:S(2)}) collective-permute-start(s32[512]{0:T(512)} %param.20), channel_id=1, source_target_pairs={{0,4},{4,8},{8,12},{12,16},{16,20},{20,24},{24,28},{28,32},{32,36}... | collective-permute-start | bytes 6152 | tf_op jit(solution)/shard_map/ppermute | solution.py:18
  23.2 10.4 %copy-start.10 = (s32[512]{0:T(512)S(1)}, s32[512]{0:T(512)}, u32[]{:S(2)}) copy-start(s32[512]{0:T(512)} %param.20) | copy-start | bytes 6148
  23.2 75.6 %all-to-all-start = ((bf16[64,16,960]{2,1,0:T(8,128)(2,1)}), bf16[64,16,960]{2,1,0:T(8,128)(2,1)}, u32[]{:S(2)}, u32[]{:S(2)}) async-start(bf16[64,16,960]{2,1,0:T(8,128)(2,1)} %bitcast.157), calls=%async_computation | async-start | bytes 4194304 | tf_op jit(solution)/shard_map/all_to_all | solution.py:109
  36.1 29.4 %copy-start.12 = (f32[256]{0:T(256)S(1)}, f32[256]{0:T(256)}, u32[]{:S(2)}) copy-start(f32[256]{0:T(256)} %param.16) | copy-start | bytes 3076
  62.0 4.8 %copy-start.2 = (bf16[512,3840]{0,1:T(8,128)(2,1)S(1)}, bf16[512,3840]{0,1:T(8,128)(2,1)}, u32[]{:S(2)}) copy-start(bf16[512,3840]{0,1:T(8,128)(2,1)} %all-gather.3.cloned.1.call-done) | copy-start | bytes 11796484
  62.0 4.8 %copy-start.13 = (bf16[3840,256]{1,0:T(8,128)(2,1)S(1)}, bf16[3840,256]{1,0:T(8,128)(2,1)}, u32[]{:S(2)}) copy-start(bf16[3840,256]{1,0:T(8,128)(2,1)} %param.14) | copy-start | bytes 5898244
  66.8 8.4 %copy-start.1 = (bf16[3840,512]{1,0:T(8,128)(2,1)S(1)}, bf16[3840,512]{1,0:T(8,128)(2,1)}, u32[]{:S(2)}) copy-start(bf16[3840,512]{1,0:T(8,128)(2,1)} %param.12) | copy-start | bytes 11796484
  68.1 22.3 %collective-permute-start.1 = (bf16[512,2,1,256]{0,3,2,1:T(8,128)(2,1)S(1)}, bf16[512,2,1,256]{0,3,2,1:T(8,128)(2,1)S(1)}, u32[]{:S(2)}, u32[]{:S(2)}) collective-permute-start(bf16[512,2,1,256]{0,3,2,1:T(8,128)(2,1)S(1)} %pad_maximum_fusion.1), channel_id=1, source_target_pairs={{0,4},{4,8},{8,12},{12,16},{16,20},{20,24},{24,28},{28,32},{32,36}... | collective-permute-start | bytes 1572872 | tf_op jit(solution)/shard_map/ppermute | solution.py:18
  72.1 25.3 %collective-permute-start = (bf16[512,2,1,256]{0,3,2,1:T(8,128)(2,1)S(1)}, bf16[512,2,1,256]{0,3,2,1:T(8,128)(2,1)S(1)}, u32[]{:S(2)}, u32[]{:S(2)}) collective-permute-start(bf16[512,2,1,256]{0,3,2,1:T(8,128)(2,1)S(1)} %pad_maximum_fusion.1), channel_id=1, source_target_pairs={{0,8},{4,12},{8,16},{12,20},{16,24},{20,28},{24,32},{28,36},{32,40... | collective-permute-start | bytes 1572872 | tf_op jit(solution)/shard_map/ppermute | solution.py:18
  78.5 20.3 %copy-start.8 = (bf16[1,64,960]{2,1,0:T(8,128)(2,1)S(1)}, bf16[1,64,960]{2,1,0:T(8,128)(2,1)}, u32[]{:S(2)}) copy-start(bf16[1,64,960]{2,1,0:T(8,128)(2,1)} %param.17) | copy-start | bytes 368644
  97.4 35.9 %copy-start.11 = (s32[512,1]{0,1:T(1,128)S(1)}, s32[512,1]{0,1:T(1,128)}, u32[]{:S(2)}) copy-start(s32[512,1]{0,1:T(1,128)} %param.19) | copy-start | bytes 6148
  121.2 22.7 %all-to-all-start.1 = ((bf16[64,2,512]{2,1,0:T(2,128)(2,1)}), bf16[64,2,512]{2,1,0:T(2,128)(2,1)S(1)}, u32[]{:S(2)}, u32[]{:S(2)}) async-start(bf16[64,2,512]{2,1,0:T(2,128)(2,1)} %reshape.350), calls=%async_computation.1 | async-start | bytes 262144 | tf_op jit(solution)/shard_map/all_to_all | solution.py:151
  145.5 3.0 %copy-start.4 = (f32[512,512]{1,0:T(8,128)S(1)}, f32[512,512]{1,0:T(8,128)}, u32[]{:S(2)}) copy-start(f32[512,512]{1,0:T(8,128)} %fusion.77) | copy-start | bytes 3145732
  148.4 6.1 %copy-start.9 = (f32[256]{0:T(256)S(1)}, f32[256]{0:T(256)}, u32[]{:S(2)}) copy-start(f32[256]{0:T(256)} %param.15) | copy-start | bytes 3076
  154.5 1.5 copy-start.7
  156.0 2.1 copy-start.6
  156.0 2.1 copy-start.14
  158.0 2.7 %copy-start.15 = (f32[1536,512,2]{1,0,2:T(8,128)}, f32[1536,512,2]{1,0,2:T(8,128)S(1)}, u32[]{:S(2)}) copy-start(f32[1536,512,2]{1,0,2:T(8,128)S(1)} %get-tuple-element.37) | copy-start | bytes 18874372
  160.7 2.7 %copy-start.3 = (f32[512,128]{1,0:T(8,128)S(1)}, f32[512,128]{1,0:T(8,128)}, u32[]{:S(2)}) copy-start(f32[512,128]{1,0:T(8,128)} %get-tuple-element.33) | copy-start | bytes 786436
  168.0 34.9 %all-to-all-start.2 = ((bf16[64,16,512]{2,1,0:T(8,128)(2,1)}), bf16[64,16,512]{2,1,0:T(8,128)(2,1)S(1)}, u32[]{:S(2)}, u32[]{:S(2)}) async-start(bf16[64,16,512]{2,1,0:T(8,128)(2,1)} %bitcast.160), calls=%async_computation.2 | async-start | bytes 2097152 | tf_op jit(solution)/shard_map/all_to_all | solution.py:176
  (1 other events, 1.5 us)
Sparse Core Ops, SparseCore 0:
  9.8 52.1 all-gather.2
  64.8 80.6 all-gather.4
